TPU v7x, 32 devices: a whole 2x2x4 slice. The times are simulated.
32 devices in a mesh: cell: 16 (over z, x, core), gene: 2 (over y).
Axes of the slice: x: 2, y: 2, z: 4, core: 2. Of those that a mesh axis runs over, the one named last changes fastest.
Arguments:
- counts: bfloat16 [15360, 16384], P('cell', 'gene'), as said below
- w_factor: float32 [15360, 128], P('cell'), may hold values from 0.004 to 2, as said below
- h_factor: float32 [128, 16384], P('cell', 'gene'), may hold values from 0.03 to 0.3, as said below
Outputs:
- w_updated: float32 [15360, 128], P('cell')
- h_updated: float32 [128, 16384], P('cell', 'gene')
Inputs may be any that keep to these rules, and one draw needn't show every extreme that they name: `counts`: nonnegative whole numbers. `w_factor`: positive. `h_factor`: positive.
All inputs are finite; a program needn't handle non-finite values.
Results may differ from a plain program's by a relative error of at most 0.00092.
Values may be sent and summed in bfloat16 or wider, within the bound.
No kernel may reach another device: no remote copies, remote signals or barrier semaphores. Data moves between devices by JAX's collectives and lax.ppermute only.
A program may use at most 64 MiB of HBM per device.

v0:
```python
import functools

import jax
import jax.numpy as jnp
from jax import lax
from jax.experimental import pallas as pl
from jax.experimental.pallas import tpu as pltpu
from jax.sharding import PartitionSpec as P


F32 = jnp.float32
BF16 = jnp.bfloat16
CHUNKS = 2
H_KNEE = 2.0**20
W_KNEE = 2.0**17


def encode(value, knee):
    part = jnp.minimum(value * (1.0 / knee), 1.0)
    return (value * part * part * part).astype(BF16)


def decode(code, knee):
    code = code.astype(F32)
    root = knee * jnp.sqrt(jnp.sqrt(code * (1.0 / knee)))
    return jnp.where(code < knee, root, code)


def prepare_kernel(w_ref, pick_ref, w_rel_ref, wt_rel_ref, sum_ref):
    w_value = w_ref[...]
    w_copy = w_value.astype(BF16)
    pick = pick_ref[...]
    second = (((1,), (1,)), ((), ()))
    w_rel_ref[...] = lax.dot_general(w_copy, pick, second, preferred_element_type=F32).astype(BF16)
    wt_rel_ref[...] = lax.dot_general(pick, w_copy, second, preferred_element_type=F32).astype(BF16)
    sum_ref[...] = jnp.broadcast_to(jnp.sum(w_value, axis=0, keepdims=True), sum_ref.shape)


def prepare(w_factor, pick):
    cells, rank = w_factor.shape
    return pl.pallas_call(
        prepare_kernel,
        out_shape=[
            jax.ShapeDtypeStruct((cells, rank), BF16),
            jax.ShapeDtypeStruct((rank, cells), BF16),
            jax.ShapeDtypeStruct((8, rank), F32),
        ],
        name="prepare",
    )(w_factor, pick)


def h_kernel(wt_ref, w_ref, *refs):
    pieces, counts_ref, keep_ref, send_ref = refs[:-3], refs[-3], refs[-2], refs[-1]
    h_tile = jnp.concatenate([piece[...] for piece in pieces], axis=0)
    modeled = jnp.dot(w_ref[...], h_tile, preferred_element_type=F32)
    quotient = (counts_ref[...].astype(F32) / modeled).astype(BF16)
    term = jnp.dot(wt_ref[...], quotient, preferred_element_type=F32)
    keep = keep_ref.shape[0]
    keep_ref[...] = term[:keep]
    send_ref[...] = term[keep:]


def w_kernel(w_ref, *refs, count, first, last):
    pieces, counts_ref = refs[:count], refs[count]
    running = refs[count + 1 : -3]
    out_ref, sum_ref, total_ref = refs[-3:]
    h_tile = jnp.concatenate([piece[...] for piece in pieces], axis=0)
    across = (((1,), (1,)), ((), ()))
    ones = jnp.ones((sum_ref.shape[0], h_tile.shape[1]), BF16)

    @pl.when(pl.program_id(0) == 0)
    def _():
        if first:
            total_ref[...] = jnp.zeros_like(total_ref)
            sum_ref[...] = jnp.zeros_like(sum_ref)
        else:
            total_ref[...] = running[0][...]
            sum_ref[...] = running[1][...]

    modeled = jnp.dot(w_ref[...], h_tile, preferred_element_type=F32)
    quotient = (counts_ref[...].astype(F32) / modeled).astype(BF16)
    total_ref[...] += lax.dot_general(quotient, h_tile, across, preferred_element_type=F32)
    sum_ref[...] += lax.dot_general(ones, h_tile, across, preferred_element_type=F32)

    @pl.when(pl.program_id(0) == pl.num_programs(0) - 1)
    def _():
        total = total_ref[...]
        out_ref[...] = encode(total, W_KNEE) if last else total


def tile_of(width):
    return next(t for t in (1024, 512, 256, 128, width) if width % t == 0)


def cost(cells, rank, width):
    return pl.CostEstimate(
        flops=4 * cells * rank * width, transcendentals=0, bytes_accessed=2 * cells * width
    )


def h_partial(start, wt_rel, w_rel, pieces, counts, width):
    cells, rank = w_rel.shape
    tile = tile_of(width)
    part = pl.BlockSpec((rank // 2, tile), lambda i: (0, i))
    return pl.pallas_call(
        h_kernel,
        grid=(width // tile,),
        in_specs=[
            pl.BlockSpec((rank, cells), lambda i: (0, 0)),
            pl.BlockSpec((cells, rank), lambda i: (0, 0)),
        ]
        + [pl.BlockSpec((piece.shape[0], tile), lambda i: (0, i)) for piece in pieces]
        + [pl.BlockSpec((cells, tile), lambda i: (0, start // tile + i))],
        out_specs=[part, part],
        out_shape=[jax.ShapeDtypeStruct((rank // 2, width), F32)] * 2,
        cost_estimate=cost(cells, rank, width),
        name="h_partial",
    )(wt_rel, w_rel, *pieces, counts)


def w_partial(start, w_rel, pieces, counts, width, running, last):
    cells, rank = w_rel.shape
    tile = tile_of(width)
    rows = pl.BlockSpec((cells, rank), lambda i: (0, 0))
    sums = pl.BlockSpec((8, rank), lambda i: (0, 0))
    return pl.pallas_call(
        functools.partial(w_kernel, count=len(pieces), first=not running, last=last),
        grid=(width // tile,),
        in_specs=[rows]
        + [pl.BlockSpec((piece.shape[0], tile), lambda i: (0, i)) for piece in pieces]
        + [pl.BlockSpec((cells, tile), lambda i: (0, start // tile + i))]
        + ([rows, sums] if running else []),
        out_specs=[rows, sums],
        scratch_shapes=[pltpu.VMEM((cells, rank), F32)],
        out_shape=[
            jax.ShapeDtypeStruct((cells, rank), BF16 if last else F32),
            jax.ShapeDtypeStruct((8, rank), F32),
        ],
        cost_estimate=cost(cells, rank, width),
        name="w_partial",
    )(w_rel, *pieces, counts, *running)


def per_device(counts, w_factor, h_factor, *, devices, gene_devices):
    rows, genes = h_factor.shape
    _, rank = w_factor.shape
    chips = devices // 2
    across = 2 ** ((chips.bit_length() - 1) // 2)
    along = chips // across
    block = along * rows
    width = genes // CHUNKS

    index = lax.axis_index("cell")
    core = index % 2
    x_at = (index // 2) % across
    z_at = index // (2 * across)

    def send(value, route):
        return lax.ppermute(value, "cell", [(i, route(i)) for i in range(devices)])

    def swap(value):
        return send(value, lambda i: i ^ 1)

    def shift_x(value, s):
        return send(
            value, lambda i: i % 2 + 2 * ((i // 2 + s) % across) + i // (2 * across) * 2 * across
        )

    def shift_z(value, s):
        return send(value, lambda i: (i + 2 * across * s) % devices)

    place = jnp.arange(rank)
    source = (
        (z_at + place // rows % along) % along * (2 * across * rows)
        + (x_at + place // block % across) % across * (2 * rows)
        + (core + place // (block * across)) % 2 * rows
        + place % rows
    )
    pick = source[:, None] == jnp.arange(rank)[None, :]

    w_rel, wt_rel, w_sum = prepare(w_factor, pick.astype(BF16))
    w_sum = w_sum[0]
    high = lax.reduce_precision(w_sum, 8, 7)
    middle = lax.reduce_precision(w_sum - high, 8, 7)
    low = w_sum - high - middle
    lanes = -(-3 // rows)
    sums = jnp.pad(jnp.stack([high, middle, low]), ((0, lanes * rows - 3), (0, 0)))
    sums = jnp.concatenate(jnp.split(sums, lanes, 0), 1).astype(BF16)

    def gather(own):
        column = [own] + [shift_z(own, along - s) for s in range(1, along)]
        column = jnp.concatenate(column, 0)
        mine = [column] + [shift_x(column, across - s) for s in range(1, across)]
        return mine + [swap(piece) for piece in mine]

    def reduce(keep, other):
        total = keep + swap(other)
        sent = encode(total[block:], H_KNEE)
        column = total[:block]
        got = [shift_x(sent[(s - 1) * block : s * block], s) for s in range(1, across)]
        for piece in got:
            column = column + decode(piece, H_KNEE)
        sent = encode(column[rows:], H_KNEE)
        mine = column[:rows]
        got = [shift_z(sent[(s - 1) * rows : s * rows], s) for s in range(1, along)]
        for piece in got:
            mine = mine + decode(piece, H_KNEE)
        return mine

    gathered = []
    for i in range(CHUNKS):
        own = h_factor[:, i * width : (i + 1) * width].astype(BF16)
        if i == CHUNKS - 1:
            own = jnp.concatenate([own, sums], 1)
        gathered.append(gather(own))
    w_totals = jnp.concatenate([piece[:, width:] for piece in gathered[-1]], 0).astype(F32)
    w_totals = jnp.sum(jnp.sum(w_totals, axis=0).reshape(lanes, rank), axis=0)
    own_totals = lax.dynamic_slice_in_dim(w_totals, index * rows, rows, 0)[:, None]

    updated = []
    again = []
    for i in range(CHUNKS):
        keep, other = h_partial(i * width, wt_rel, w_rel, gathered[i], counts, width)
        numerator = reduce(keep, other)
        if updated:
            numerator, _ = lax.optimization_barrier((numerator, updated[-1]))
        new = h_factor[:, i * width : (i + 1) * width] * numerator / own_totals
        updated.append(new)
        again.append(gather(new.astype(BF16)))
    h_updated = jnp.concatenate(updated, 1)

    running = ()
    for i in range(CHUNKS):
        last = i == CHUNKS - 1 and gene_devices == 2
        running = w_partial(i * width, w_rel, again[i], counts, width, running, last)
    numerator, h_totals = running

    if gene_devices == 2:
        swap_gene = [(0, 1), (1, 0)]
        h_totals = h_totals + lax.ppermute(h_totals, "gene", swap_gene)
        got = lax.ppermute(numerator, "gene", swap_gene)
        numerator = decode(numerator, W_KNEE) + decode(got, W_KNEE)
    else:
        numerator, h_totals = lax.psum((numerator, h_totals), "gene")
    ratio = jnp.dot(
        numerator / h_totals[:1], pick.astype(F32), precision=lax.Precision.HIGHEST
    )
    w_updated = w_factor * ratio
    return (w_updated, h_updated)


def solution(mesh):
    in_specs = (P("cell", "gene"), P("cell", None), P("cell", "gene"))
    out_specs = (P("cell", None), P("cell", "gene"))

    def body(counts, w_factor, h_factor):
        return per_device(
            counts,
            w_factor,
            h_factor,
            devices=mesh.shape["cell"],
            gene_devices=mesh.shape["gene"],
        )

    return jax.shard_map(
        body, mesh=mesh, in_specs=in_specs, out_specs=out_specs, check_vma=False
    )
```

profile of v0, /device:TPU:0, one launch (start us, length us, event | category | flops | bytes accessed | tf_op | source)
XLA Modules:
  0.0 128.5 jit_solution(1395789691462718852)
XLA Ops:
  1.6 3.1 %collective-permute-start.13 = (bf16[8,4096]{1,0:T(8,128)(2,1)S(1)}, bf16[8,4096]{1,0:T(8,128)(2,1)S(1)}, u32[]{:S(2)}, u32[]{:S(2)}) collective-permute-start(bf16[8,4096]{1,0:T(8,128)(2,1)S(1)} %get-tuple-element.30), channel_id=1, source_target_pairs={{0,8},{2,10},{4,12},{6,14},{8,16},{10,18},{12,20},{14,22},{16,24},... | collective-permute-start | bytes 196616 | tf_op jit(solution)/shard_map/ppermute | solution.py:159
  4.7 2.6 %collective-permute-start.12 = (bf16[8,4096]{1,0:T(8,128)(2,1)S(1)}, bf16[8,4096]{1,0:T(8,128)(2,1)S(1)}, u32[]{:S(2)}, u32[]{:S(2)}) collective-permute-start(bf16[8,4096]{1,0:T(8,128)(2,1)S(1)} %get-tuple-element.30), channel_id=1, source_target_pairs={{0,16},{2,18},{4,20},{6,22},{8,24},{10,26},{12,28},{14,30},{16,0},... | collective-permute-start | bytes 196616 | tf_op jit(solution)/shard_map/ppermute | solution.py:159
  7.3 1.3 %collective-permute-start.11 = (bf16[8,4096]{1,0:T(8,128)(2,1)S(1)}, bf16[8,4096]{1,0:T(8,128)(2,1)S(1)}, u32[]{:S(2)}, u32[]{:S(2)}) collective-permute-start(bf16[8,4096]{1,0:T(8,128)(2,1)S(1)} %get-tuple-element.30), channel_id=1, source_target_pairs={{0,24},{2,26},{4,28},{6,30},{8,0},{10,2},{12,4},{14,6},{16,8},{18,... | collective-permute-start | bytes 196616 | tf_op jit(solution)/shard_map/ppermute | solution.py:159
  9.4 2.1 %prepare.1 = (bf16[960,128]{1,0:T(8,128)(2,1)}, bf16[128,960]{1,0:T(8,128)(2,1)}, f32[8,128]{1,0:T(8,128)}) custom-call(f32[960,128]{1,0:T(8,128)} %w_ref.1, bf16[128,128]{1,0:T(8,128)(2,1)} %fusion.50.pick_ref), custom_call_target="tpu_custom_call" | custom-call | tf_op jit(solution)/shard_map/prepare/pallas_call | solution.py:41
  12.1 1.5 %collective-permute-start.14 = (bf16[32,4096]{1,0:T(8,128)(2,1)S(1)}, bf16[32,4096]{1,0:T(8,128)(2,1)S(1)}, u32[]{:S(2)}, u32[]{:S(2)}) collective-permute-start(bf16[32,4096]{1,0:T(8,128)(2,1)S(1)} %pad_maximum_fusion.1.refs_0_), channel_id=1, source_target_pairs={{0,4},{2,6},{4,0},{6,2},{8,12},{10,14},{12,8},{14,10},{16,20},{18,... | collective-permute-start | bytes 786440 | tf_op jit(solution)/shard_map/ppermute | solution.py:159
  14.4 5.5 %collective-permute-done.14.refs_1_ = bf16[32,4096]{1,0:T(8,128)(2,1)S(1)} collective-permute-done((bf16[32,4096]{1,0:T(8,128)(2,1)S(1)}, bf16[32,4096]{1,0:T(8,128)(2,1)S(1)}, u32[]{:S(2)}, u32[]{:S(2)}) %collective-permute-start.14) | collective-permute-done | bytes 262176 | tf_op jit(solution)/shard_map/ppermute | solution.py:159
  19.9 2.0 %collective-permute-start.2 = (bf16[8,4224]{1,0:T(8,128)(2,1)S(1)}, bf16[8,4224]{1,0:T(8,128)(2,1)S(1)}, u32[]{:S(2)}, u32[]{:S(2)}) collective-permute-start(bf16[8,4224]{1,0:T(8,128)(2,1)S(1)} %pad_maximum_fusion.5), channel_id=1, source_target_pairs={{0,8},{2,10},{4,12},{6,14},{8,16},{10,18},{12,20},{14,22},{16,24},... | collective-permute-start | bytes 202760 | tf_op jit(solution)/shard_map/ppermute | solution.py:159
  22.2 2.2 %collective-permute-start = (bf16[8,4224]{1,0:T(8,128)(2,1)S(1)}, bf16[8,4224]{1,0:T(8,128)(2,1)S(1)}, u32[]{:S(2)}, u32[]{:S(2)}) collective-permute-start(bf16[8,4224]{1,0:T(8,128)(2,1)S(1)} %pad_maximum_fusion.5), channel_id=1, source_target_pairs={{0,24},{2,26},{4,28},{6,30},{8,0},{10,2},{12,4},{14,6},{16,8},{18,... | collective-permute-start | bytes 202760 | tf_op jit(solution)/shard_map/ppermute | solution.py:159
  25.2 7.5 %h_partial.3 = (f32[64,4096]{1,0:T(8,128)}, f32[64,4096]{1,0:T(8,128)}) custom-call(bf16[128,960]{1,0:T(8,128)(2,1)} %get-tuple-element.15.wt_ref, bf16[960,128]{1,0:T(8,128)(2,1)} %get-tuple-element.14.w_ref, bf16[32,4096]{1,0:T(8,128)(2,1)} %copy-done.3, bf16[32,4096]{1,0:T(8,128)(2,1)} %copy-done.12, bf16[32,4096]{1,0:T(8,128)(2,1)} %copy-done.13, ...), custom_call_target="tpu_custom_call" | custom-call | flops 2013265920 | bytes 7864320 | tf_op jit(solution)/shard_map/h_partial/pallas_call | solution.py:105
  32.9 1.3 %collective-permute-start.3 = (bf16[32,4224]{1,0:T(8,128)(2,1)S(1)}, bf16[32,4224]{1,0:T(8,128)(2,1)S(1)}, u32[]{:S(2)}, u32[]{:S(2)}) collective-permute-start(bf16[32,4224]{1,0:T(8,128)(2,1)S(1)} %pad_maximum_fusion.refs_0_), channel_id=1, source_target_pairs={{0,4},{2,6},{4,0},{6,2},{8,12},{10,14},{12,8},{14,10},{16,20},{18,... | collective-permute-start | bytes 811016 | tf_op jit(solution)/shard_map/ppermute | solution.py:159
  34.4 7.4 %collective-permute-done.3.refs_1_ = bf16[32,4224]{1,0:T(8,128)(2,1)S(1)} collective-permute-done((bf16[32,4224]{1,0:T(8,128)(2,1)S(1)}, bf16[32,4224]{1,0:T(8,128)(2,1)S(1)}, u32[]{:S(2)}, u32[]{:S(2)}) %collective-permute-start.3) | collective-permute-done | bytes 270368 | tf_op jit(solution)/shard_map/ppermute | solution.py:159
  41.9 1.5 %collective-permute-done.5.refs_3_ = bf16[32,4224]{1,0:T(8,128)(2,1)S(1)} collective-permute-done((bf16[32,4224]{1,0:T(8,128)(2,1)S(1)}, bf16[32,4224]{1,0:T(8,128)(2,1)S(1)}, u32[]{:S(2)}, u32[]{:S(2)}) %collective-permute-start.5) | collective-permute-done | bytes 270368 | tf_op jit(solution)/shard_map/ppermute | solution.py:159
  44.1 7.5 %h_partial.2 = (f32[64,4096]{1,0:T(8,128)}, f32[64,4096]{1,0:T(8,128)}) custom-call(bf16[128,960]{1,0:T(8,128)(2,1)} %get-tuple-element.15.wt_ref, bf16[960,128]{1,0:T(8,128)(2,1)} %get-tuple-element.14.w_ref, bf16[32,4224]{1,0:T(8,128)(2,1)} %copy-done, bf16[32,4224]{1,0:T(8,128)(2,1)} %copy-done.7, bf16[32,4224]{1,0:T(8,128)(2,1)} %copy-done.8, ...), custom_call_target="tpu_custom_call" | custom-call | flops 2013265920 | bytes 7864320 | tf_op jit(solution)/shard_map/h_partial/pallas_call | solution.py:105
  54.9 1.3 %collective-permute-start.18 = (bf16[32,4096]{1,0:T(8,128)(2,1)S(1)}, bf16[32,4096]{1,0:T(8,128)(2,1)S(1)}, u32[]{:S(2)}, u32[]{:S(2)}) collective-permute-start(bf16[32,4096]{1,0:T(8,128)(2,1)S(1)} %fusion.7), channel_id=1, source_target_pairs={{0,4},{2,6},{4,0},{6,2},{8,12},{10,14},{12,8},{14,10},{16,20},{18,... | collective-permute-start | bytes 786440 | tf_op jit(solution)/shard_map/ppermute | solution.py:159
  56.2 1.3 %add.183 = f32[64,4096]{1,0:T(8,128)S(1)} add(f32[64,4096]{1,0:T(8,128)} %get-tuple-element.17, f32[64,4096]{1,0:T(8,128)S(1)} %collective-permute-done.6) | non-fusion elementwise | flops 262144 | bytes 3145728 | tf_op jit(solution)/shard_map/add | solution.py:197
  58.5 5.6 %collective-permute-done.18 = bf16[32,4096]{1,0:T(8,128)(2,1)S(1)} collective-permute-done((bf16[32,4096]{1,0:T(8,128)(2,1)S(1)}, bf16[32,4096]{1,0:T(8,128)(2,1)S(1)}, u32[]{:S(2)}, u32[]{:S(2)}) %collective-permute-start.18) | collective-permute-done | bytes 262176 | tf_op jit(solution)/shard_map/ppermute | solution.py:159
  64.6 2.0 %collective-permute-start.21 = (bf16[8,4096]{1,0:T(8,128)(2,1)S(1)}, bf16[8,4096]{1,0:T(8,128)(2,1)S(1)}, u32[]{:S(2)}, u32[]{:S(2)}) collective-permute-start(bf16[8,4096]{1,0:T(8,128)(2,1)S(1)} %get-tuple-element.33), channel_id=1, source_target_pairs={{0,24},{2,26},{4,28},{6,30},{8,0},{10,2},{12,4},{14,6},{16,8},{18,... | collective-permute-start | bytes 196616 | tf_op jit(solution)/shard_map/ppermute | solution.py:159
  66.6 1.5 %collective-permute-start.19 = (bf16[8,4096]{1,0:T(8,128)(2,1)S(1)}, bf16[8,4096]{1,0:T(8,128)(2,1)S(1)}, u32[]{:S(2)}, u32[]{:S(2)}) collective-permute-start(bf16[8,4096]{1,0:T(8,128)(2,1)S(1)} %get-tuple-element.32), channel_id=1, source_target_pairs={{0,8},{2,10},{4,12},{6,14},{8,16},{10,18},{12,20},{14,22},{16,24},... | collective-permute-start | bytes 196616 | tf_op jit(solution)/shard_map/ppermute | solution.py:159
  70.6 1.6 %collective-permute-start.9 = (bf16[8,4096]{1,0:T(8,128)(2,1)S(1)}, bf16[8,4096]{1,0:T(8,128)(2,1)S(1)}, u32[]{:S(2)}, u32[]{:S(2)}) collective-permute-start(bf16[8,4096]{1,0:T(8,128)(2,1)S(1)} %get-tuple-element.36), channel_id=1, source_target_pairs={{0,16},{2,18},{4,20},{6,22},{8,24},{10,26},{12,28},{14,30},{16,0},... | collective-permute-start | bytes 196616 | tf_op jit(solution)/shard_map/ppermute | solution.py:159
  72.2 1.9 %collective-permute-start.10 = (bf16[8,4096]{1,0:T(8,128)(2,1)S(1)}, bf16[8,4096]{1,0:T(8,128)(2,1)S(1)}, u32[]{:S(2)}, u32[]{:S(2)}) collective-permute-start(bf16[8,4096]{1,0:T(8,128)(2,1)S(1)} %get-tuple-element.35), channel_id=1, source_target_pairs={{0,24},{2,26},{4,28},{6,30},{8,0},{10,2},{12,4},{14,6},{16,8},{18,... | collective-permute-start | bytes 196616 | tf_op jit(solution)/shard_map/ppermute | solution.py:159
  74.5 1.4 %collective-permute-start.29 = (bf16[8,4096]{1,0:T(8,128)(2,1)S(1)}, bf16[8,4096]{1,0:T(8,128)(2,1)S(1)}, u32[]{:S(2)}, u32[]{:S(2)}) collective-permute-start(bf16[8,4096]{1,0:T(8,128)(2,1)S(1)} %get-tuple-element.26), channel_id=1, source_target_pairs={{0,16},{2,18},{4,20},{6,22},{8,24},{10,26},{12,28},{14,30},{16,0},... | collective-permute-start | bytes 196616 | tf_op jit(solution)/shard_map/ppermute | solution.py:159
  76.5 2.3 %collective-permute-start.28 = (bf16[8,4096]{1,0:T(8,128)(2,1)S(1)}, bf16[8,4096]{1,0:T(8,128)(2,1)S(1)}, u32[]{:S(2)}, u32[]{:S(2)}) collective-permute-start(bf16[8,4096]{1,0:T(8,128)(2,1)S(1)} %get-tuple-element.26), channel_id=1, source_target_pairs={{0,24},{2,26},{4,28},{6,30},{8,0},{10,2},{12,4},{14,6},{16,8},{18,... | collective-permute-start | bytes 196616 | tf_op jit(solution)/shard_map/ppermute | solution.py:159
  79.6 4.1 %collective-permute-start.24 = (bf16[8,4096]{1,0:T(8,128)(2,1)S(1)}, bf16[8,4096]{1,0:T(8,128)(2,1)S(1)}, u32[]{:S(2)}, u32[]{:S(2)}) collective-permute-start(bf16[8,4096]{1,0:T(8,128)(2,1)S(1)} %get-tuple-element.28), channel_id=1, source_target_pairs={{0,8},{2,10},{4,12},{6,14},{8,16},{10,18},{12,20},{14,22},{16,24},... | collective-permute-start | bytes 196616 | tf_op jit(solution)/shard_map/ppermute | solution.py:159
  84.8 1.4 %collective-permute-start.22 = (bf16[8,4096]{1,0:T(8,128)(2,1)S(1)}, bf16[8,4096]{1,0:T(8,128)(2,1)S(1)}, u32[]{:S(2)}, u32[]{:S(2)}) collective-permute-start(bf16[8,4096]{1,0:T(8,128)(2,1)S(1)} %get-tuple-element.28), channel_id=1, source_target_pairs={{0,24},{2,26},{4,28},{6,30},{8,0},{10,2},{12,4},{14,6},{16,8},{18,... | collective-permute-start | bytes 196616 | tf_op jit(solution)/shard_map/ppermute | solution.py:159
  86.8 2.4 %collective-permute-done.23 = bf16[8,4096]{1,0:T(8,128)(2,1)S(1)} collective-permute-done((bf16[8,4096]{1,0:T(8,128)(2,1)S(1)}, bf16[8,4096]{1,0:T(8,128)(2,1)S(1)}, u32[]{:S(2)}, u32[]{:S(2)}) %collective-permute-start.23) | collective-permute-done | bytes 65568 | tf_op jit(solution)/shard_map/ppermute | solution.py:159
  90.5 4.7 %collective-permute-done.31.refs_1_ = bf16[32,4096]{1,0:T(8,128)(2,1)S(1)} collective-permute-done((bf16[32,4096]{1,0:T(8,128)(2,1)S(1)}, bf16[32,4096]{1,0:T(8,128)(2,1)S(1)}, u32[]{:S(2)}, u32[]{:S(2)}) %collective-permute-start.31) | collective-permute-done | bytes 262176 | tf_op jit(solution)/shard_map/ppermute | solution.py:159
  95.6 2.3 %collective-permute-done.25.refs_1_ = bf16[32,4096]{1,0:T(8,128)(2,1)S(1)} collective-permute-done((bf16[32,4096]{1,0:T(8,128)(2,1)S(1)}, bf16[32,4096]{1,0:T(8,128)(2,1)S(1)}, u32[]{:S(2)}, u32[]{:S(2)}) %collective-permute-start.25) | collective-permute-done | bytes 262176 | tf_op jit(solution)/shard_map/ppermute | solution.py:159
  99.4 8.0 %w_partial.2 = (f32[960,128]{1,0:T(8,128)}, f32[8,128]{1,0:T(8,128)}) custom-call(bf16[960,128]{1,0:T(8,128)(2,1)} %get-tuple-element.14.w_ref, bf16[32,4096]{1,0:T(8,128)(2,1)} %copy-done.1, bf16[32,4096]{1,0:T(8,128)(2,1)} %copy-done.10, bf16[32,4096]{1,0:T(8,128)(2,1)} %copy-done.15, bf16[32,4096]{1,0:T(8,128)(2,1)} %copy-done.18, bf16[960,8192]{1,0:T(8,128)(2,1)} %refs_4_.7), custom_call_target="tpu_custom_call" | custom-call | flops 2013265920 | bytes 7864320 | tf_op jit(solution)/shard_map/w_partial/pallas_call | solution.py:126
  108.2 8.2 %w_partial.3 = (bf16[960,128]{1,0:T(8,128)(2,1)}, f32[8,128]{1,0:T(8,128)}) custom-call(bf16[960,128]{1,0:T(8,128)(2,1)} %get-tuple-element.14.w_ref, bf16[32,4096]{1,0:T(8,128)(2,1)} %copy-done.2, bf16[32,4096]{1,0:T(8,128)(2,1)} %copy-done.11, bf16[32,4096]{1,0:T(8,128)(2,1)} %copy-done.14, bf16[32,4096]{1,0:T(8,128)(2,1)} %copy-done.17, ...), custom_call_target="tpu_custom_call" | custom-call | flops 2013265920 | bytes 7864320 | tf_op jit(solution)/shard_map/w_partial/pallas_call | solution.py:126
  117.3 1.1 collective-permute-start.35
  119.1 5.9 %collective-permute-done.35 = f32[8,128]{1,0:T(8,128)S(1)} collective-permute-done((f32[8,128]{1,0:T(8,128)}, f32[8,128]{1,0:T(8,128)S(1)}, u32[]{:S(2)}, u32[]{:S(2)}) %collective-permute-start.35) | collective-permute-done | bytes 4128 | tf_op jit(solution)/shard_map/ppermute | solution.py:240
  125.7 2.8 %convolution_multiply_fusion = f32[960,128]{1,0:T(8,128)} fusion(f32[960,128]{1,0:T(8,128)S(1)} %copy-done.6, bf16[960,128]{1,0:T(8,128)(2,1)} %get-tuple-element.24, bf16[960,128]{1,0:T(8,128)(2,1)S(1)} %collective-permute-done.34, f32[128]{0:T(128)S(1)} %slice_bitcast_fusion, s32[128]{0:T(128)S(1)} %fusion.57), kind=kOutput, calls=%fused_computation.4 | convolution fusion | flops 190357504 | bytes 1475584 | tf_op jit(solution)/shard_map/dot_general | solution.py:245
  (116 shorter events, 22.0 us)
Async XLA Ops:
  1.6 9.9 %collective-permute-start.13 = (bf16[8,4096]{1,0:T(8,128)(2,1)S(1)}, bf16[8,4096]{1,0:T(8,128)(2,1)S(1)}, u32[]{:S(2)}, u32[]{:S(2)}) collective-permute-start(bf16[8,4096]{1,0:T(8,128)(2,1)S(1)} %get-tuple-element.30), channel_id=1, source_target_pairs={{0,8},{2,10},{4,12},{6,14},{8,16},{10,18},{12,20},{14,22},{16,24},... | collective-permute-start | bytes 196616 | tf_op jit(solution)/shard_map/ppermute | solution.py:159
  4.7 7.1 %collective-permute-start.12 = (bf16[8,4096]{1,0:T(8,128)(2,1)S(1)}, bf16[8,4096]{1,0:T(8,128)(2,1)S(1)}, u32[]{:S(2)}, u32[]{:S(2)}) collective-permute-start(bf16[8,4096]{1,0:T(8,128)(2,1)S(1)} %get-tuple-element.30), channel_id=1, source_target_pairs={{0,16},{2,18},{4,20},{6,22},{8,24},{10,26},{12,28},{14,30},{16,0},... | collective-permute-start | bytes 196616 | tf_op jit(solution)/shard_map/ppermute | solution.py:159
  7.3 4.7 %collective-permute-start.11 = (bf16[8,4096]{1,0:T(8,128)(2,1)S(1)}, bf16[8,4096]{1,0:T(8,128)(2,1)S(1)}, u32[]{:S(2)}, u32[]{:S(2)}) collective-permute-start(bf16[8,4096]{1,0:T(8,128)(2,1)S(1)} %get-tuple-element.30), channel_id=1, source_target_pairs={{0,24},{2,26},{4,28},{6,30},{8,0},{10,2},{12,4},{14,6},{16,8},{18,... | collective-permute-start | bytes 196616 | tf_op jit(solution)/shard_map/ppermute | solution.py:159
  12.1 7.9 %collective-permute-start.14 = (bf16[32,4096]{1,0:T(8,128)(2,1)S(1)}, bf16[32,4096]{1,0:T(8,128)(2,1)S(1)}, u32[]{:S(2)}, u32[]{:S(2)}) collective-permute-start(bf16[32,4096]{1,0:T(8,128)(2,1)S(1)} %pad_maximum_fusion.1.refs_0_), channel_id=1, source_target_pairs={{0,4},{2,6},{4,0},{6,2},{8,12},{10,14},{12,8},{14,10},{16,20},{18,... | collective-permute-start | bytes 786440 | tf_op jit(solution)/shard_map/ppermute | solution.py:159
  14.3 10.1 %collective-permute-start.15 = (bf16[32,4096]{1,0:T(8,128)(2,1)S(1)}, bf16[32,4096]{1,0:T(8,128)(2,1)S(1)}, u32[]{:S(2)}, u32[]{:S(2)}) collective-permute-start(bf16[32,4096]{1,0:T(8,128)(2,1)S(1)} %pad_maximum_fusion.1.refs_0_), channel_id=1, source_target_pairs={{0,2},{2,0},{4,6},{6,4},{8,10},{10,8},{12,14},{14,12},{16,18},{18,... | collective-permute-start | bytes 786440 | tf_op jit(solution)/shard_map/ppermute | solution.py:159
  19.9 12.9 %collective-permute-start.2 = (bf16[8,4224]{1,0:T(8,128)(2,1)S(1)}, bf16[8,4224]{1,0:T(8,128)(2,1)S(1)}, u32[]{:S(2)}, u32[]{:S(2)}) collective-permute-start(bf16[8,4224]{1,0:T(8,128)(2,1)S(1)} %pad_maximum_fusion.5), channel_id=1, source_target_pairs={{0,8},{2,10},{4,12},{6,14},{8,16},{10,18},{12,20},{14,22},{16,24},... | collective-permute-start | bytes 202760 | tf_op jit(solution)/shard_map/ppermute | solution.py:159
  22.0 10.9 %collective-permute-start.1 = (bf16[8,4224]{1,0:T(8,128)(2,1)S(1)}, bf16[8,4224]{1,0:T(8,128)(2,1)S(1)}, u32[]{:S(2)}, u32[]{:S(2)}) collective-permute-start(bf16[8,4224]{1,0:T(8,128)(2,1)S(1)} %pad_maximum_fusion.5), channel_id=1, source_target_pairs={{0,16},{2,18},{4,20},{6,22},{8,24},{10,26},{12,28},{14,30},{16,0},... | collective-permute-start | bytes 202760 | tf_op jit(solution)/shard_map/ppermute | solution.py:159
  22.2 10.7 %collective-permute-start = (bf16[8,4224]{1,0:T(8,128)(2,1)S(1)}, bf16[8,4224]{1,0:T(8,128)(2,1)S(1)}, u32[]{:S(2)}, u32[]{:S(2)}) collective-permute-start(bf16[8,4224]{1,0:T(8,128)(2,1)S(1)} %pad_maximum_fusion.5), channel_id=1, source_target_pairs={{0,24},{2,26},{4,28},{6,30},{8,0},{10,2},{12,4},{14,6},{16,8},{18,... | collective-permute-start | bytes 202760 | tf_op jit(solution)/shard_map/ppermute | solution.py:159
  32.8 21.9 %collective-permute-start.17 = (f32[64,4096]{1,0:T(8,128)}, f32[64,4096]{1,0:T(8,128)S(1)}, u32[]{:S(2)}, u32[]{:S(2)}) collective-permute-start(f32[64,4096]{1,0:T(8,128)} %get-tuple-element.20), channel_id=1, source_target_pairs={{0,2},{2,0},{4,6},{6,4},{8,10},{10,8},{12,14},{14,12},{16,18},{18,... | collective-permute-start | bytes 3145736 | tf_op jit(solution)/shard_map/ppermute | solution.py:159
  32.9 8.9 %collective-permute-start.3 = (bf16[32,4224]{1,0:T(8,128)(2,1)S(1)}, bf16[32,4224]{1,0:T(8,128)(2,1)S(1)}, u32[]{:S(2)}, u32[]{:S(2)}) collective-permute-start(bf16[32,4224]{1,0:T(8,128)(2,1)S(1)} %pad_maximum_fusion.refs_0_), channel_id=1, source_target_pairs={{0,4},{2,6},{4,0},{6,2},{8,12},{10,14},{12,8},{14,10},{16,20},{18,... | collective-permute-start | bytes 811016 | tf_op jit(solution)/shard_map/ppermute | solution.py:159
  34.2 7.6 %collective-permute-start.4 = (bf16[32,4224]{1,0:T(8,128)(2,1)S(1)}, bf16[32,4224]{1,0:T(8,128)(2,1)S(1)}, u32[]{:S(2)}, u32[]{:S(2)}) collective-permute-start(bf16[32,4224]{1,0:T(8,128)(2,1)S(1)} %pad_maximum_fusion.refs_0_), channel_id=1, source_target_pairs={{0,2},{2,0},{4,6},{6,4},{8,10},{10,8},{12,14},{14,12},{16,18},{18,... | collective-permute-start | bytes 811016 | tf_op jit(solution)/shard_map/ppermute | solution.py:159
  54.9 9.2 %collective-permute-start.18 = (bf16[32,4096]{1,0:T(8,128)(2,1)S(1)}, bf16[32,4096]{1,0:T(8,128)(2,1)S(1)}, u32[]{:S(2)}, u32[]{:S(2)}) collective-permute-start(bf16[32,4096]{1,0:T(8,128)(2,1)S(1)} %fusion.7), channel_id=1, source_target_pairs={{0,4},{2,6},{4,0},{6,2},{8,12},{10,14},{12,8},{14,10},{16,20},{18,... | collective-permute-start | bytes 786440 | tf_op jit(solution)/shard_map/ppermute | solution.py:159
  57.6 11.5 %collective-permute-start.7 = (bf16[32,4096]{1,0:T(8,128)(2,1)S(1)}, bf16[32,4096]{1,0:T(8,128)(2,1)S(1)}, u32[]{:S(2)}, u32[]{:S(2)}) collective-permute-start(bf16[32,4096]{1,0:T(8,128)(2,1)S(1)} %fusion.6), channel_id=1, source_target_pairs={{0,4},{2,6},{4,0},{6,2},{8,12},{10,14},{12,8},{14,10},{16,20},{18,... | collective-permute-start | bytes 786440 | tf_op jit(solution)/shard_map/ppermute | solution.py:159
  64.6 7.6 %collective-permute-start.21 = (bf16[8,4096]{1,0:T(8,128)(2,1)S(1)}, bf16[8,4096]{1,0:T(8,128)(2,1)S(1)}, u32[]{:S(2)}, u32[]{:S(2)}) collective-permute-start(bf16[8,4096]{1,0:T(8,128)(2,1)S(1)} %get-tuple-element.33), channel_id=1, source_target_pairs={{0,24},{2,26},{4,28},{6,30},{8,0},{10,2},{12,4},{14,6},{16,8},{18,... | collective-permute-start | bytes 196616 | tf_op jit(solution)/shard_map/ppermute | solution.py:159
  66.6 7.5 %collective-permute-start.20 = (bf16[8,4096]{1,0:T(8,128)(2,1)S(1)}, bf16[8,4096]{1,0:T(8,128)(2,1)S(1)}, u32[]{:S(2)}, u32[]{:S(2)}) collective-permute-start(bf16[8,4096]{1,0:T(8,128)(2,1)S(1)} %get-tuple-element.34), channel_id=1, source_target_pairs={{0,16},{2,18},{4,20},{6,22},{8,24},{10,26},{12,28},{14,30},{16,0},... | collective-permute-start | bytes 196616 | tf_op jit(solution)/shard_map/ppermute | solution.py:159
  66.6 7.5 %collective-permute-start.19 = (bf16[8,4096]{1,0:T(8,128)(2,1)S(1)}, bf16[8,4096]{1,0:T(8,128)(2,1)S(1)}, u32[]{:S(2)}, u32[]{:S(2)}) collective-permute-start(bf16[8,4096]{1,0:T(8,128)(2,1)S(1)} %get-tuple-element.32), channel_id=1, source_target_pairs={{0,8},{2,10},{4,12},{6,14},{8,16},{10,18},{12,20},{14,22},{16,24},... | collective-permute-start | bytes 196616 | tf_op jit(solution)/shard_map/ppermute | solution.py:159
  69.6 6.9 %collective-permute-start.8 = (bf16[8,4096]{1,0:T(8,128)(2,1)S(1)}, bf16[8,4096]{1,0:T(8,128)(2,1)S(1)}, u32[]{:S(2)}, u32[]{:S(2)}) collective-permute-start(bf16[8,4096]{1,0:T(8,128)(2,1)S(1)} %get-tuple-element.37), channel_id=1, source_target_pairs={{0,8},{2,10},{4,12},{6,14},{8,16},{10,18},{12,20},{14,22},{16,24},... | collective-permute-start | bytes 196616 | tf_op jit(solution)/shard_map/ppermute | solution.py:159
  70.6 8.7 %collective-permute-start.9 = (bf16[8,4096]{1,0:T(8,128)(2,1)S(1)}, bf16[8,4096]{1,0:T(8,128)(2,1)S(1)}, u32[]{:S(2)}, u32[]{:S(2)}) collective-permute-start(bf16[8,4096]{1,0:T(8,128)(2,1)S(1)} %get-tuple-element.36), channel_id=1, source_target_pairs={{0,16},{2,18},{4,20},{6,22},{8,24},{10,26},{12,28},{14,30},{16,0},... | collective-permute-start | bytes 196616 | tf_op jit(solution)/shard_map/ppermute | solution.py:159
  72.2 7.1 %collective-permute-start.10 = (bf16[8,4096]{1,0:T(8,128)(2,1)S(1)}, bf16[8,4096]{1,0:T(8,128)(2,1)S(1)}, u32[]{:S(2)}, u32[]{:S(2)}) collective-permute-start(bf16[8,4096]{1,0:T(8,128)(2,1)S(1)} %get-tuple-element.35), channel_id=1, source_target_pairs={{0,24},{2,26},{4,28},{6,30},{8,0},{10,2},{12,4},{14,6},{16,8},{18,... | collective-permute-start | bytes 196616 | tf_op jit(solution)/shard_map/ppermute | solution.py:159
  74.3 10.4 %collective-permute-start.30 = (bf16[8,4096]{1,0:T(8,128)(2,1)S(1)}, bf16[8,4096]{1,0:T(8,128)(2,1)S(1)}, u32[]{:S(2)}, u32[]{:S(2)}) collective-permute-start(bf16[8,4096]{1,0:T(8,128)(2,1)S(1)} %get-tuple-element.26), channel_id=1, source_target_pairs={{0,8},{2,10},{4,12},{6,14},{8,16},{10,18},{12,20},{14,22},{16,24},... | collective-permute-start | bytes 196616 | tf_op jit(solution)/shard_map/ppermute | solution.py:159
  74.5 11.6 %collective-permute-start.29 = (bf16[8,4096]{1,0:T(8,128)(2,1)S(1)}, bf16[8,4096]{1,0:T(8,128)(2,1)S(1)}, u32[]{:S(2)}, u32[]{:S(2)}) collective-permute-start(bf16[8,4096]{1,0:T(8,128)(2,1)S(1)} %get-tuple-element.26), channel_id=1, source_target_pairs={{0,16},{2,18},{4,20},{6,22},{8,24},{10,26},{12,28},{14,30},{16,0},... | collective-permute-start | bytes 196616 | tf_op jit(solution)/shard_map/ppermute | solution.py:159
  76.5 9.7 %collective-permute-start.28 = (bf16[8,4096]{1,0:T(8,128)(2,1)S(1)}, bf16[8,4096]{1,0:T(8,128)(2,1)S(1)}, u32[]{:S(2)}, u32[]{:S(2)}) collective-permute-start(bf16[8,4096]{1,0:T(8,128)(2,1)S(1)} %get-tuple-element.26), channel_id=1, source_target_pairs={{0,24},{2,26},{4,28},{6,30},{8,0},{10,2},{12,4},{14,6},{16,8},{18,... | collective-permute-start | bytes 196616 | tf_op jit(solution)/shard_map/ppermute | solution.py:159
  79.6 7.2 %collective-permute-start.24 = (bf16[8,4096]{1,0:T(8,128)(2,1)S(1)}, bf16[8,4096]{1,0:T(8,128)(2,1)S(1)}, u32[]{:S(2)}, u32[]{:S(2)}) collective-permute-start(bf16[8,4096]{1,0:T(8,128)(2,1)S(1)} %get-tuple-element.28), channel_id=1, source_target_pairs={{0,8},{2,10},{4,12},{6,14},{8,16},{10,18},{12,20},{14,22},{16,24},... | collective-permute-start | bytes 196616 | tf_op jit(solution)/shard_map/ppermute | solution.py:159
  83.7 5.5 %collective-permute-start.23 = (bf16[8,4096]{1,0:T(8,128)(2,1)S(1)}, bf16[8,4096]{1,0:T(8,128)(2,1)S(1)}, u32[]{:S(2)}, u32[]{:S(2)}) collective-permute-start(bf16[8,4096]{1,0:T(8,128)(2,1)S(1)} %get-tuple-element.28), channel_id=1, source_target_pairs={{0,16},{2,18},{4,20},{6,22},{8,24},{10,26},{12,28},{14,30},{16,0},... | collective-permute-start | bytes 196616 | tf_op jit(solution)/shard_map/ppermute | solution.py:159
  84.8 5.0 %collective-permute-start.22 = (bf16[8,4096]{1,0:T(8,128)(2,1)S(1)}, bf16[8,4096]{1,0:T(8,128)(2,1)S(1)}, u32[]{:S(2)}, u32[]{:S(2)}) collective-permute-start(bf16[8,4096]{1,0:T(8,128)(2,1)S(1)} %get-tuple-element.28), channel_id=1, source_target_pairs={{0,24},{2,26},{4,28},{6,30},{8,0},{10,2},{12,4},{14,6},{16,8},{18,... | collective-permute-start | bytes 196616 | tf_op jit(solution)/shard_map/ppermute | solution.py:159
  86.2 8.9 %collective-permute-start.31 = (bf16[32,4096]{1,0:T(8,128)(2,1)S(1)}, bf16[32,4096]{1,0:T(8,128)(2,1)S(1)}, u32[]{:S(2)}, u32[]{:S(2)}) collective-permute-start(bf16[32,4096]{1,0:T(8,128)(2,1)S(1)} %pad_maximum_fusion.3.refs_0_), channel_id=1, source_target_pairs={{0,4},{2,6},{4,0},{6,2},{8,12},{10,14},{12,8},{14,10},{16,20},{18,... | collective-permute-start | bytes 786440 | tf_op jit(solution)/shard_map/ppermute | solution.py:159
  89.8 8.1 %collective-permute-start.25 = (bf16[32,4096]{1,0:T(8,128)(2,1)S(1)}, bf16[32,4096]{1,0:T(8,128)(2,1)S(1)}, u32[]{:S(2)}, u32[]{:S(2)}) collective-permute-start(bf16[32,4096]{1,0:T(8,128)(2,1)S(1)} %pad_maximum_fusion.2.refs_0_), channel_id=1, source_target_pairs={{0,4},{2,6},{4,0},{6,2},{8,12},{10,14},{12,8},{14,10},{16,20},{18,... | collective-permute-start | bytes 786440 | tf_op jit(solution)/shard_map/ppermute | solution.py:159
  90.5 7.5 %collective-permute-start.32 = (bf16[32,4096]{1,0:T(8,128)(2,1)S(1)}, bf16[32,4096]{1,0:T(8,128)(2,1)S(1)}, u32[]{:S(2)}, u32[]{:S(2)}) collective-permute-start(bf16[32,4096]{1,0:T(8,128)(2,1)S(1)} %pad_maximum_fusion.3.refs_0_), channel_id=1, source_target_pairs={{0,2},{2,0},{4,6},{6,4},{8,10},{10,8},{12,14},{14,12},{16,18},{18,... | collective-permute-start | bytes 786440 | tf_op jit(solution)/shard_map/ppermute | solution.py:159
  95.1 12.3 %collective-permute-start.26 = (bf16[32,4096]{1,0:T(8,128)(2,1)S(1)}, bf16[32,4096]{1,0:T(8,128)(2,1)S(1)}, u32[]{:S(2)}, u32[]{:S(2)}) collective-permute-start(bf16[32,4096]{1,0:T(8,128)(2,1)S(1)} %pad_maximum_fusion.2.refs_0_), channel_id=1, source_target_pairs={{0,2},{2,0},{4,6},{6,4},{8,10},{10,8},{12,14},{14,12},{16,18},{18,... | collective-permute-start | bytes 786440 | tf_op jit(solution)/shard_map/ppermute | solution.py:159
  97.9 9.5 %collective-permute-start.27 = (bf16[32,4096]{1,0:T(8,128)(2,1)S(1)}, bf16[32,4096]{1,0:T(8,128)(2,1)S(1)}, u32[]{:S(2)}, u32[]{:S(2)}) collective-permute-start(bf16[32,4096]{1,0:T(8,128)(2,1)S(1)} %collective-permute-done.25.refs_1_), channel_id=1, source_target_pairs={{0,2},{2,0},{4,6},{6,4},{8,10},{10,8},{12,14},{14,12},{16,18},{18,... | collective-permute-start | bytes 786440 | tf_op jit(solution)/shard_map/ppermute | solution.py:159
  116.4 9.3 %collective-permute-start.34 = (bf16[960,128]{1,0:T(8,128)(2,1)}, bf16[960,128]{1,0:T(8,128)(2,1)S(1)}, u32[]{:S(2)}, u32[]{:S(2)}) collective-permute-start(bf16[960,128]{1,0:T(8,128)(2,1)} %get-tuple-element.24), channel_id=1, source_target_pairs={{0,1},{1,0},{2,3},{3,2},{4,5},{5,4},{6,7},{7,6},{8,9},{9,8},{10,11... | collective-permute-start | bytes 737288 | tf_op jit(solution)/shard_map/ppermute | solution.py:241
  117.3 7.7 %collective-permute-start.35 = (f32[8,128]{1,0:T(8,128)}, f32[8,128]{1,0:T(8,128)S(1)}, u32[]{:S(2)}, u32[]{:S(2)}) collective-permute-start(f32[8,128]{1,0:T(8,128)} %get-tuple-element.25), channel_id=1, source_target_pairs={{0,1},{1,0},{2,3},{3,2},{4,5},{5,4},{6,7},{7,6},{8,9},{9,8},{10,11... | collective-permute-start | bytes 12296 | tf_op jit(solution)/shard_map/ppermute | solution.py:240
  (23 other events, 190.0 us)
where the time goes:
time: 129 us; the launch traced here: 128 us
  starting transfers between devices  39.3 us (30%)
  waiting for transfers between devices  38.4 us (30%)
  Pallas kernels  33.3 us (26%)
  local copies, waits for them, and re-layouts  7.61 us (6%)
  other arithmetic  6.06 us (5%)
  matrix products  2.79 us (2%)
    ppermute x34, starting transfers between devices, send(): return lax.ppermute(value, 'cell', [(i, route(i)) for i in range(devices)])  37.3 us
    ppermute x34, waiting for transfers between devices, send(): return lax.ppermute(value, 'cell', [(i, route(i)) for i in range(devices)])  32.5 us
    pallas_call x2, Pallas kernels, w_partial(): pl.pallas_call(functools.partial(w_kernel, count=len(pieces), first=not r...  16.1 us
    pallas_call x2, Pallas kernels, h_partial(): pl.pallas_call(h_kernel, grid=(width // tile,), in_specs=[pl.BlockSpec((r...  15 us
    ppermute x1, waiting for transfers between devices, per_device(): h_totals = h_totals + lax.ppermute(h_totals, 'gene', swap_gene)  5.89 us
    unnamed x38, local copies, waits for them, and re-layouts  3.72 us
    slice x4, local copies, waits for them, and re-layouts, per_device(): piece[:, width:]  2.79 us
    dot_general x1, matrix products, per_device(): jnp.dot(numerator / h_totals[:1], pick.astype(F32), precision=lax.Precisi...  2.79 us
  transfers between devices with their start and end apart: 36, of which 14 were waited for; matrix products, arithmetic and copies ran while one was open for 7% of the time, Pallas kernels for 20%

commit v1 on v0

--- a/solution.py
+++ b/solution.py
@@ -1,4 +1,5 @@
 import functools
+import math
 
 import jax
 import jax.numpy as jnp
@@ -10,7 +11,8 @@
 
 F32 = jnp.float32
 BF16 = jnp.bfloat16
-CHUNKS = 2
+SPACE = pltpu.VMEM
+SPLIT = (4, 4)
 H_KNEE = 2.0**20
 W_KNEE = 2.0**17
 
@@ -22,8 +24,18 @@
 
 def decode(code, knee):
     code = code.astype(F32)
-    root = knee * jnp.sqrt(jnp.sqrt(code * (1.0 / knee)))
+    root = knee * lax.rsqrt(lax.rsqrt(code * (1.0 / knee)))
     return jnp.where(code < knee, root, code)
+
+
+def encode_square(value, knee):
+    return (value * jnp.minimum(value * (1.0 / knee), 1.0)).astype(BF16)
+
+
+def decode_square(code, knee):
+    code = code.astype(F32)
+    square = code * knee
+    return jnp.where(code < knee, square * lax.rsqrt(jnp.maximum(square, 1e-30)), code)
 
 
 def prepare_kernel(w_ref, pick_ref, w_rel_ref, wt_rel_ref, sum_ref):
@@ -57,13 +69,17 @@
     term = jnp.dot(wt_ref[...], quotient, preferred_element_type=F32)
     keep = keep_ref.shape[0]
     keep_ref[...] = term[:keep]
-    send_ref[...] = term[keep:]
+    send_ref[...] = encode_square(term[keep:], H_KNEE)
 
 
 def w_kernel(w_ref, *refs, count, first, last):
     pieces, counts_ref = refs[:count], refs[count]
-    running = refs[count + 1 : -3]
-    out_ref, sum_ref, total_ref = refs[-3:]
+    if last:
+        running, pick_ref = refs[count + 1 : -4], refs[-4]
+        out_ref, total_ref, sum_ref = refs[-3:]
+    else:
+        running = refs[count + 1 : -2]
+        total_ref, sum_ref = refs[-2:]
     h_tile = jnp.concatenate([piece[...] for piece in pieces], axis=0)
     across = (((1,), (1,)), ((), ()))
     ones = jnp.ones((sum_ref.shape[0], h_tile.shape[1]), BF16)
@@ -82,14 +98,28 @@
     total_ref[...] += lax.dot_general(quotient, h_tile, across, preferred_element_type=F32)
     sum_ref[...] += lax.dot_general(ones, h_tile, across, preferred_element_type=F32)
 
-    @pl.when(pl.program_id(0) == pl.num_programs(0) - 1)
-    def _():
-        total = total_ref[...]
-        out_ref[...] = encode(total, W_KNEE) if last else total
+    if last:
+
+        @pl.when(pl.program_id(0) == pl.num_programs(0) - 1)
+        def _():
+            cells = total_ref.shape[0]
+            exact = lax.Precision.HIGHEST
+            pick = pick_ref[...]
+            total = jnp.dot(total_ref[...], pick, precision=exact, preferred_element_type=F32)
+            sums = jnp.dot(sum_ref[...], pick, precision=exact, preferred_element_type=F32)
+            high = sums.astype(BF16)
+            rest = sums - high.astype(F32)
+            middle = rest.astype(BF16)
+            low = (rest - middle.astype(F32)).astype(BF16)
+            out_ref[:cells, :] = encode(total, W_KNEE)
+            row = lax.broadcasted_iota(jnp.int32, (16, sums.shape[1]), 0)
+            part = [jnp.broadcast_to(x.astype(F32)[:1], row.shape) for x in (high, middle, low)]
+            tail = jnp.where(row == 0, part[0], jnp.where(row == 1, part[1], part[2]))
+            out_ref[cells:, :] = jnp.where(row < 3, tail, 0.0).astype(BF16)
 
 
 def tile_of(width):
-    return next(t for t in (1024, 512, 256, 128, width) if width % t == 0)
+    return next(t for t in (2048, 1024, 512, 256, 128, width) if width % t == 0)
 
 
 def cost(cells, rank, width):
@@ -98,9 +128,13 @@
     )
 
 
+def held(pieces):
+    return [pltpu.with_memory_space_constraint(piece, SPACE) for piece in pieces]
+
+
 def h_partial(start, wt_rel, w_rel, pieces, counts, width):
     cells, rank = w_rel.shape
-    tile = tile_of(width)
+    tile = tile_of(math.gcd(width, start))
     part = pl.BlockSpec((rank // 2, tile), lambda i: (0, i))
     return pl.pallas_call(
         h_kernel,
@@ -112,43 +146,57 @@
         + [pl.BlockSpec((piece.shape[0], tile), lambda i: (0, i)) for piece in pieces]
         + [pl.BlockSpec((cells, tile), lambda i: (0, start // tile + i))],
         out_specs=[part, part],
-        out_shape=[jax.ShapeDtypeStruct((rank // 2, width), F32)] * 2,
+        out_shape=[jax.ShapeDtypeStruct((rank // 2, width), kind) for kind in (F32, BF16)],
         cost_estimate=cost(cells, rank, width),
         name="h_partial",
-    )(wt_rel, w_rel, *pieces, counts)
-
-
-def w_partial(start, w_rel, pieces, counts, width, running, last):
+    )(wt_rel, w_rel, *held(pieces), counts)
+
+
+def w_partial(start, w_rel, pieces, counts, width, running, pick):
     cells, rank = w_rel.shape
-    tile = tile_of(width)
+    tile = tile_of(math.gcd(width, start))
+    last = pick is not None
     rows = pl.BlockSpec((cells, rank), lambda i: (0, 0))
     sums = pl.BlockSpec((8, rank), lambda i: (0, 0))
+    square = pl.BlockSpec((rank, rank), lambda i: (0, 0))
+    if last:
+        how = dict(
+            out_specs=pl.BlockSpec((cells + 16, rank), lambda i: (0, 0)),
+            out_shape=jax.ShapeDtypeStruct((cells + 16, rank), BF16),
+            scratch_shapes=[pltpu.VMEM((cells, rank), F32), pltpu.VMEM((8, rank), F32)],
+        )
+    else:
+        how = dict(
+            out_specs=[rows, sums],
+            out_shape=[
+                jax.ShapeDtypeStruct((cells, rank), F32),
+                jax.ShapeDtypeStruct((8, rank), F32),
+            ],
+        )
     return pl.pallas_call(
         functools.partial(w_kernel, count=len(pieces), first=not running, last=last),
         grid=(width // tile,),
         in_specs=[rows]
         + [pl.BlockSpec((piece.shape[0], tile), lambda i: (0, i)) for piece in pieces]
         + [pl.BlockSpec((cells, tile), lambda i: (0, start // tile + i))]
-        + ([rows, sums] if running else []),
-        out_specs=[rows, sums],
-        scratch_shapes=[pltpu.VMEM((cells, rank), F32)],
-        out_shape=[
-            jax.ShapeDtypeStruct((cells, rank), BF16 if last else F32),
-            jax.ShapeDtypeStruct((8, rank), F32),
-        ],
+        + ([rows, sums] if running else [])
+        + ([square] if last else []),
         cost_estimate=cost(cells, rank, width),
         name="w_partial",
-    )(w_rel, *pieces, counts, *running)
+        **how,
+    )(w_rel, *held(pieces), counts, *running, *([pick] if last else []))
 
 
 def per_device(counts, w_factor, h_factor, *, devices, gene_devices):
     rows, genes = h_factor.shape
-    _, rank = w_factor.shape
+    cells, rank = w_factor.shape
     chips = devices // 2
     across = 2 ** ((chips.bit_length() - 1) // 2)
     along = chips // across
     block = along * rows
-    width = genes // CHUNKS
+    widths = [genes * share // sum(SPLIT) for share in SPLIT]
+    starts = [sum(widths[:i]) for i in range(len(widths))]
+    chunks = len(widths)
 
     index = lax.axis_index("cell")
     core = index % 2
@@ -188,13 +236,15 @@
     sums = jnp.concatenate(jnp.split(sums, lanes, 0), 1).astype(BF16)
 
     def gather(own):
-        column = [own] + [shift_z(own, along - s) for s in range(1, along)]
+        column = [own]
+        for s in range(1, along):
+            column.append(shift_z(own, along - s))
         column = jnp.concatenate(column, 0)
         mine = [column] + [shift_x(column, across - s) for s in range(1, across)]
         return mine + [swap(piece) for piece in mine]
 
     def reduce(keep, other):
-        total = keep + swap(other)
+        total = keep + decode_square(swap(other), H_KNEE)
         sent = encode(total[block:], H_KNEE)
         column = total[:block]
         got = [shift_x(sent[(s - 1) * block : s * block], s) for s in range(1, across)]
@@ -202,50 +252,55 @@
             column = column + decode(piece, H_KNEE)
         sent = encode(column[rows:], H_KNEE)
         mine = column[:rows]
-        got = [shift_z(sent[(s - 1) * rows : s * rows], s) for s in range(1, along)]
+        got = []
+        for s in range(1, along):
+            got.append(shift_z(sent[(s - 1) * rows : s * rows], s))
         for piece in got:
             mine = mine + decode(piece, H_KNEE)
         return mine
 
     gathered = []
-    for i in range(CHUNKS):
-        own = h_factor[:, i * width : (i + 1) * width].astype(BF16)
-        if i == CHUNKS - 1:
+    for i in range(chunks):
+        own = h_factor[:, starts[i] : starts[i] + widths[i]].astype(BF16)
+        if i == chunks - 1:
             own = jnp.concatenate([own, sums], 1)
         gathered.append(gather(own))
-    w_totals = jnp.concatenate([piece[:, width:] for piece in gathered[-1]], 0).astype(F32)
+    w_totals = jnp.concatenate([piece[:, widths[-1] :] for piece in gathered[-1]], 0).astype(F32)
     w_totals = jnp.sum(jnp.sum(w_totals, axis=0).reshape(lanes, rank), axis=0)
     own_totals = lax.dynamic_slice_in_dim(w_totals, index * rows, rows, 0)[:, None]
 
     updated = []
     again = []
-    for i in range(CHUNKS):
-        keep, other = h_partial(i * width, wt_rel, w_rel, gathered[i], counts, width)
+    for i in range(chunks):
+        keep, other = h_partial(starts[i], wt_rel, w_rel, gathered[i], counts, widths[i])
         numerator = reduce(keep, other)
         if updated:
             numerator, _ = lax.optimization_barrier((numerator, updated[-1]))
-        new = h_factor[:, i * width : (i + 1) * width] * numerator / own_totals
+        new = h_factor[:, starts[i] : starts[i] + widths[i]] * numerator / own_totals
         updated.append(new)
         again.append(gather(new.astype(BF16)))
     h_updated = jnp.concatenate(updated, 1)
 
+    pick = pick.astype(F32)
     running = ()
-    for i in range(CHUNKS):
-        last = i == CHUNKS - 1 and gene_devices == 2
-        running = w_partial(i * width, w_rel, again[i], counts, width, running, last)
-    numerator, h_totals = running
-
+    for i in range(chunks):
+        last = i == chunks - 1 and gene_devices == 2
+        running = w_partial(
+            starts[i], w_rel, again[i], counts, widths[i], running, pick if last else None
+        )
     if gene_devices == 2:
-        swap_gene = [(0, 1), (1, 0)]
-        h_totals = h_totals + lax.ppermute(h_totals, "gene", swap_gene)
-        got = lax.ppermute(numerator, "gene", swap_gene)
-        numerator = decode(numerator, W_KNEE) + decode(got, W_KNEE)
+        got = lax.ppermute(running, "gene", [(0, 1), (1, 0)])
+        totals = sum(
+            side[cells + row : cells + row + 1].astype(F32)
+            for row in range(3)
+            for side in (running, got)
+        )
+        numerator = decode(running[:cells], W_KNEE) + decode(got[:cells], W_KNEE)
+        w_updated = w_factor * numerator / totals
     else:
-        numerator, h_totals = lax.psum((numerator, h_totals), "gene")
-    ratio = jnp.dot(
-        numerator / h_totals[:1], pick.astype(F32), precision=lax.Precision.HIGHEST
-    )
-    w_updated = w_factor * ratio
+        numerator, h_totals = lax.psum(running, "gene")
+        ratio = jnp.dot(numerator / h_totals[:1], pick, precision=lax.Precision.HIGHEST)
+        w_updated = w_factor * ratio
     return (w_updated, h_updated)
 
 

time: 129 us -> 111 us (0.86)
  waiting for transfers between devices: 38.4 us -> 31.5 us
  local copies, waits for them, and re-layouts: 7.61 us -> 1.11 us
  matrix products: 2.79 us -> 0 us
  other arithmetic: 6.06 us -> 7.83 us
  Pallas kernels: 33.3 us -> 31.6 us
  starting transfers between devices: 39.3 us -> 38 us
    ppermute x34, waiting for transfers between devices: 32.5 us -> 24.9 us  [send(): return lax.ppermute(value, 'cell', [(i, route(i)) for i in range(devices)])]
    unnamed x38 -> x6, local copies, waits for them, and re-layouts: 3.72 us -> 0.01 us
    div x0 -> x2, other arithmetic: none -> 2.81 us  [per_device(): w_updated = w_factor * numerator / totals]
    dot_general x1 -> x0, matrix products: 2.79 us -> none  [per_device(): jnp.dot(numerator / h_totals[:1], pick.astype(F32), precision=lax.Precisi...]
    slice x7, local copies, waits for them, and re-layouts: 3.81 us -> 1.02 us  [the longest x1 0.99 us: per_device(): new = h_factor[:, starts[i]:starts[i] + widths[i]] * numerator / own_totals]
    pallas_call x2, Pallas kernels: 15 us -> 13.6 us  [h_partial(): pl.pallas_call(h_kernel, grid=(width // tile,), in_specs=[pl.BlockSpec((r...]
    ppermute x2 -> x1, waiting for transfers between devices: 5.89 us -> 6.62 us  [per_device(): got = lax.ppermute(running, 'gene', [(0, 1), (1, 0)])]
  transfers between devices with their start and end apart: 36 -> 35, of which waited for: 14 -> 14; matrix products, arithmetic and copies ran while one was open for 7% -> 5% of each run, Pallas kernels for 20% -> 21%
where the time goes in v1:
time: 111 us
  starting transfers between devices  38 us (34%)
  Pallas kernels  31.6 us (28%)
  waiting for transfers between devices  31.5 us (28%)
  other arithmetic  7.83 us (7%)
  local copies, waits for them, and re-layouts  1.11 us (1%)
    ppermute x34, starting transfers between devices, send(): return lax.ppermute(value, 'cell', [(i, route(i)) for i in range(devices)])  36.7 us
    ppermute x34, waiting for transfers between devices, send(): return lax.ppermute(value, 'cell', [(i, route(i)) for i in range(devices)])  24.9 us
    pallas_call x2, Pallas kernels, w_partial(): pl.pallas_call(functools.partial(w_kernel, count=len(pieces), first=not r...  15.9 us
    pallas_call x2, Pallas kernels, h_partial(): pl.pallas_call(h_kernel, grid=(width // tile,), in_specs=[pl.BlockSpec((r...  13.6 us
    ppermute x1, waiting for transfers between devices, per_device(): got = lax.ppermute(running, 'gene', [(0, 1), (1, 0)])  6.62 us
    div x2, other arithmetic, per_device(): w_updated = w_factor * numerator / totals  2.81 us
  transfers between devices with their start and end apart: 35, of which 14 were waited for; matrix products, arithmetic and copies ran while one was open for 5% of the time, Pallas kernels for 21%

profile of v1, /device:TPU:0, one launch (start us, length us, event | category | flops | bytes accessed | tf_op | source)
XLA Modules:
  0.0 110.9 jit_solution(3489082974041481861)
XLA Ops:
  1.6 3.1 %collective-permute-start.13 = (bf16[8,4096]{1,0:T(8,128)(2,1)S(1)}, bf16[8,4096]{1,0:T(8,128)(2,1)S(1)}, u32[]{:S(2)}, u32[]{:S(2)}) collective-permute-start(bf16[8,4096]{1,0:T(8,128)(2,1)S(1)} %get-tuple-element.26), channel_id=1, source_target_pairs={{0,8},{2,10},{4,12},{6,14},{8,16},{10,18},{12,20},{14,22},{16,24},... | collective-permute-start | bytes 196616 | tf_op jit(solution)/shard_map/ppermute | solution.py:207
  4.7 2.6 %collective-permute-start.12 = (bf16[8,4096]{1,0:T(8,128)(2,1)S(1)}, bf16[8,4096]{1,0:T(8,128)(2,1)S(1)}, u32[]{:S(2)}, u32[]{:S(2)}) collective-permute-start(bf16[8,4096]{1,0:T(8,128)(2,1)S(1)} %get-tuple-element.26), channel_id=1, source_target_pairs={{0,16},{2,18},{4,20},{6,22},{8,24},{10,26},{12,28},{14,30},{16,0},... | collective-permute-start | bytes 196616 | tf_op jit(solution)/shard_map/ppermute | solution.py:207
  7.3 1.3 %collective-permute-start.11 = (bf16[8,4096]{1,0:T(8,128)(2,1)S(1)}, bf16[8,4096]{1,0:T(8,128)(2,1)S(1)}, u32[]{:S(2)}, u32[]{:S(2)}) collective-permute-start(bf16[8,4096]{1,0:T(8,128)(2,1)S(1)} %get-tuple-element.26), channel_id=1, source_target_pairs={{0,24},{2,26},{4,28},{6,30},{8,0},{10,2},{12,4},{14,6},{16,8},{18,... | collective-permute-start | bytes 196616 | tf_op jit(solution)/shard_map/ppermute | solution.py:207
  9.4 2.1 %prepare.1 = (bf16[960,128]{1,0:T(8,128)(2,1)}, bf16[128,960]{1,0:T(8,128)(2,1)}, f32[8,128]{1,0:T(8,128)}) custom-call(f32[960,128]{1,0:T(8,128)} %w_ref.1, bf16[128,128]{1,0:T(8,128)(2,1)} %get-tuple-element.38.pick_ref), custom_call_target="tpu_custom_call" | custom-call | tf_op jit(solution)/shard_map/prepare/pallas_call | solution.py:53
  12.3 1.6 %collective-permute-start.14 = (bf16[32,4096]{1,0:T(8,128)(2,1)S(1)}, bf16[32,4096]{1,0:T(8,128)(2,1)S(1)}, u32[]{:S(2)}, u32[]{:S(2)}) collective-permute-start(bf16[32,4096]{1,0:T(8,128)(2,1)S(1)} %pad_maximum_fusion.1.refs_0_), channel_id=1, source_target_pairs={{0,4},{2,6},{4,0},{6,2},{8,12},{10,14},{12,8},{14,10},{16,20},{18,... | collective-permute-start | bytes 786440 | tf_op jit(solution)/shard_map/ppermute | solution.py:207
  13.8 1.4 %collective-permute-start.2 = (bf16[8,4224]{1,0:T(8,128)(2,1)S(1)}, bf16[8,4224]{1,0:T(8,128)(2,1)S(1)}, u32[]{:S(2)}, u32[]{:S(2)}) collective-permute-start(bf16[8,4224]{1,0:T(8,128)(2,1)S(1)} %pad_maximum_fusion.5), channel_id=1, source_target_pairs={{0,8},{2,10},{4,12},{6,14},{8,16},{10,18},{12,20},{14,22},{16,24},... | collective-permute-start | bytes 202760 | tf_op jit(solution)/shard_map/ppermute | solution.py:207
  15.2 2.0 %collective-permute-start.1 = (bf16[8,4224]{1,0:T(8,128)(2,1)S(1)}, bf16[8,4224]{1,0:T(8,128)(2,1)S(1)}, u32[]{:S(2)}, u32[]{:S(2)}) collective-permute-start(bf16[8,4224]{1,0:T(8,128)(2,1)S(1)} %pad_maximum_fusion.5), channel_id=1, source_target_pairs={{0,16},{2,18},{4,20},{6,22},{8,24},{10,26},{12,28},{14,30},{16,0},... | collective-permute-start | bytes 202760 | tf_op jit(solution)/shard_map/ppermute | solution.py:207
  17.7 2.3 %collective-permute-done.14.refs_1_ = bf16[32,4096]{1,0:T(8,128)(2,1)S(1)} collective-permute-done((bf16[32,4096]{1,0:T(8,128)(2,1)S(1)}, bf16[32,4096]{1,0:T(8,128)(2,1)S(1)}, u32[]{:S(2)}, u32[]{:S(2)}) %collective-permute-start.14) | collective-permute-done | bytes 262176 | tf_op jit(solution)/shard_map/ppermute | solution.py:207
  20.6 1.4 %collective-permute-done.1 = bf16[8,4224]{1,0:T(8,128)(2,1)S(1)} collective-permute-done((bf16[8,4224]{1,0:T(8,128)(2,1)S(1)}, bf16[8,4224]{1,0:T(8,128)(2,1)S(1)}, u32[]{:S(2)}, u32[]{:S(2)}) %collective-permute-start.1) | collective-permute-done | bytes 67616 | tf_op jit(solution)/shard_map/ppermute | solution.py:207
  22.9 6.7 %h_partial.3 = (f32[64,4096]{1,0:T(8,128)}, bf16[64,4096]{1,0:T(8,128)(2,1)}) custom-call(bf16[128,960]{1,0:T(8,128)(2,1)} %get-tuple-element.13.wt_ref, bf16[960,128]{1,0:T(8,128)(2,1)} %get-tuple-element.12.w_ref, bf16[32,4096]{1,0:T(8,128)(2,1)S(1)} %pad_maximum_fusion.1.refs_0_, bf16[32,4096]{1,0:T(8,128)(2,1)S(1)} %collective-permute-done.14.refs_1_, ...), custom_call_target="tpu_custom_call" | custom-call | flops 2013265920 | bytes 7864320 | tf_op jit(solution)/shard_map/h_partial/pallas_call | solution.py:139
  30.3 1.9 %collective-permute-done.4.refs_2_ = bf16[32,4224]{1,0:T(8,128)(2,1)S(1)} collective-permute-done((bf16[32,4224]{1,0:T(8,128)(2,1)S(1)}, bf16[32,4224]{1,0:T(8,128)(2,1)S(1)}, u32[]{:S(2)}, u32[]{:S(2)}) %collective-permute-start.4) | collective-permute-done | bytes 270368 | tf_op jit(solution)/shard_map/ppermute | solution.py:207
  32.6 6.9 %h_partial.2 = (f32[64,4096]{1,0:T(8,128)}, bf16[64,4096]{1,0:T(8,128)(2,1)}) custom-call(bf16[128,960]{1,0:T(8,128)(2,1)} %get-tuple-element.13.wt_ref, bf16[960,128]{1,0:T(8,128)(2,1)} %get-tuple-element.12.w_ref, bf16[32,4224]{1,0:T(8,128)(2,1)S(1)} %pad_maximum_fusion.refs_0_, bf16[32,4224]{1,0:T(8,128)(2,1)S(1)} %collective-permute-done.3.refs_1_, ...), custom_call_target="tpu_custom_call" | custom-call | flops 2013265920 | bytes 7864320 | tf_op jit(solution)/shard_map/h_partial/pallas_call | solution.py:139
  40.1 1.3 %collective-permute-start.18 = (bf16[32,4096]{1,0:T(8,128)(2,1)S(1)}, bf16[32,4096]{1,0:T(8,128)(2,1)S(1)}, u32[]{:S(2)}, u32[]{:S(2)}) collective-permute-start(bf16[32,4096]{1,0:T(8,128)(2,1)S(1)} %fusion.15), channel_id=1, source_target_pairs={{0,4},{2,6},{4,0},{6,2},{8,12},{10,14},{12,8},{14,10},{16,20},{18,... | collective-permute-start | bytes 786440 | tf_op jit(solution)/shard_map/ppermute | solution.py:207
  41.6 1.5 %fusion.6 = f32[64,4096]{1,0:T(8,128)S(1)} fusion(f32[64,4096]{1,0:T(8,128)} %get-tuple-element.15, bf16[64,4096]{1,0:T(8,128)(2,1)S(1)} %collective-permute-done.6), kind=kLoop, calls=%fused_computation.14 | loop fusion | flops 1835008 | bytes 2621440 | tf_op jit(solution)/shard_map/add | solution.py:247
  43.2 1.3 %collective-permute-start.7 = (bf16[32,4096]{1,0:T(8,128)(2,1)S(1)}, bf16[32,4096]{1,0:T(8,128)(2,1)S(1)}, u32[]{:S(2)}, u32[]{:S(2)}) collective-permute-start(bf16[32,4096]{1,0:T(8,128)(2,1)S(1)} %fusion.14), channel_id=1, source_target_pairs={{0,4},{2,6},{4,0},{6,2},{8,12},{10,14},{12,8},{14,10},{16,20},{18,... | collective-permute-start | bytes 786440 | tf_op jit(solution)/shard_map/ppermute | solution.py:207
  44.5 4.9 %collective-permute-done.18 = bf16[32,4096]{1,0:T(8,128)(2,1)S(1)} collective-permute-done((bf16[32,4096]{1,0:T(8,128)(2,1)S(1)}, bf16[32,4096]{1,0:T(8,128)(2,1)S(1)}, u32[]{:S(2)}, u32[]{:S(2)}) %collective-permute-start.18) | collective-permute-done | bytes 262176 | tf_op jit(solution)/shard_map/ppermute | solution.py:207
  49.6 2.1 %collective-permute-start.21 = (bf16[8,4096]{1,0:T(8,128)(2,1)S(1)}, bf16[8,4096]{1,0:T(8,128)(2,1)S(1)}, u32[]{:S(2)}, u32[]{:S(2)}) collective-permute-start(bf16[8,4096]{1,0:T(8,128)(2,1)S(1)} %get-tuple-element.29), channel_id=1, source_target_pairs={{0,24},{2,26},{4,28},{6,30},{8,0},{10,2},{12,4},{14,6},{16,8},{18,... | collective-permute-start | bytes 196616 | tf_op jit(solution)/shard_map/ppermute | solution.py:207
  52.5 1.9 %collective-permute-done.7 = bf16[32,4096]{1,0:T(8,128)(2,1)S(1)} collective-permute-done((bf16[32,4096]{1,0:T(8,128)(2,1)S(1)}, bf16[32,4096]{1,0:T(8,128)(2,1)S(1)}, u32[]{:S(2)}, u32[]{:S(2)}) %collective-permute-start.7) | collective-permute-done | bytes 262176 | tf_op jit(solution)/shard_map/ppermute | solution.py:207
  54.6 1.4 %collective-permute-start.8 = (bf16[8,4096]{1,0:T(8,128)(2,1)S(1)}, bf16[8,4096]{1,0:T(8,128)(2,1)S(1)}, u32[]{:S(2)}, u32[]{:S(2)}) collective-permute-start(bf16[8,4096]{1,0:T(8,128)(2,1)S(1)} %get-tuple-element.33), channel_id=1, source_target_pairs={{0,8},{2,10},{4,12},{6,14},{8,16},{10,18},{12,20},{14,22},{16,24},... | collective-permute-start | bytes 196616 | tf_op jit(solution)/shard_map/ppermute | solution.py:207
  56.1 1.2 %collective-permute-start.9 = (bf16[8,4096]{1,0:T(8,128)(2,1)S(1)}, bf16[8,4096]{1,0:T(8,128)(2,1)S(1)}, u32[]{:S(2)}, u32[]{:S(2)}) collective-permute-start(bf16[8,4096]{1,0:T(8,128)(2,1)S(1)} %get-tuple-element.32), channel_id=1, source_target_pairs={{0,16},{2,18},{4,20},{6,22},{8,24},{10,26},{12,28},{14,30},{16,0},... | collective-permute-start | bytes 196616 | tf_op jit(solution)/shard_map/ppermute | solution.py:207
  59.6 1.7 %collective-permute-start.29 = (bf16[8,4096]{1,0:T(8,128)(2,1)S(1)}, bf16[8,4096]{1,0:T(8,128)(2,1)S(1)}, u32[]{:S(2)}, u32[]{:S(2)}) collective-permute-start(bf16[8,4096]{1,0:T(8,128)(2,1)S(1)} %get-tuple-element.22), channel_id=1, source_target_pairs={{0,16},{2,18},{4,20},{6,22},{8,24},{10,26},{12,28},{14,30},{16,0},... | collective-permute-start | bytes 196616 | tf_op jit(solution)/shard_map/ppermute | solution.py:207
  61.4 2.3 %collective-permute-start.28 = (bf16[8,4096]{1,0:T(8,128)(2,1)S(1)}, bf16[8,4096]{1,0:T(8,128)(2,1)S(1)}, u32[]{:S(2)}, u32[]{:S(2)}) collective-permute-start(bf16[8,4096]{1,0:T(8,128)(2,1)S(1)} %get-tuple-element.22), channel_id=1, source_target_pairs={{0,24},{2,26},{4,28},{6,30},{8,0},{10,2},{12,4},{14,6},{16,8},{18,... | collective-permute-start | bytes 196616 | tf_op jit(solution)/shard_map/ppermute | solution.py:207
  65.1 3.0 %collective-permute-start.24 = (bf16[8,4096]{1,0:T(8,128)(2,1)S(1)}, bf16[8,4096]{1,0:T(8,128)(2,1)S(1)}, u32[]{:S(2)}, u32[]{:S(2)}) collective-permute-start(bf16[8,4096]{1,0:T(8,128)(2,1)S(1)} %get-tuple-element.24), channel_id=1, source_target_pairs={{0,8},{2,10},{4,12},{6,14},{8,16},{10,18},{12,20},{14,22},{16,24},... | collective-permute-start | bytes 196616 | tf_op jit(solution)/shard_map/ppermute | solution.py:207
  68.9 1.7 %collective-permute-start.22 = (bf16[8,4096]{1,0:T(8,128)(2,1)S(1)}, bf16[8,4096]{1,0:T(8,128)(2,1)S(1)}, u32[]{:S(2)}, u32[]{:S(2)}) collective-permute-start(bf16[8,4096]{1,0:T(8,128)(2,1)S(1)} %get-tuple-element.24), channel_id=1, source_target_pairs={{0,24},{2,26},{4,28},{6,30},{8,0},{10,2},{12,4},{14,6},{16,8},{18,... | collective-permute-start | bytes 196616 | tf_op jit(solution)/shard_map/ppermute | solution.py:207
  71.9 2.6 %collective-permute-done.23 = bf16[8,4096]{1,0:T(8,128)(2,1)S(1)} collective-permute-done((bf16[8,4096]{1,0:T(8,128)(2,1)S(1)}, bf16[8,4096]{1,0:T(8,128)(2,1)S(1)}, u32[]{:S(2)}, u32[]{:S(2)}) %collective-permute-start.23) | collective-permute-done | bytes 65568 | tf_op jit(solution)/shard_map/ppermute | solution.py:207
  75.7 3.6 %collective-permute-done.31.refs_1_ = bf16[32,4096]{1,0:T(8,128)(2,1)S(1)} collective-permute-done((bf16[32,4096]{1,0:T(8,128)(2,1)S(1)}, bf16[32,4096]{1,0:T(8,128)(2,1)S(1)}, u32[]{:S(2)}, u32[]{:S(2)}) %collective-permute-start.31) | collective-permute-done | bytes 262176 | tf_op jit(solution)/shard_map/ppermute | solution.py:207
  79.8 3.7 %collective-permute-done.25.refs_1_ = bf16[32,4096]{1,0:T(8,128)(2,1)S(1)} collective-permute-done((bf16[32,4096]{1,0:T(8,128)(2,1)S(1)}, bf16[32,4096]{1,0:T(8,128)(2,1)S(1)}, u32[]{:S(2)}, u32[]{:S(2)}) %collective-permute-start.25) | collective-permute-done | bytes 262176 | tf_op jit(solution)/shard_map/ppermute | solution.py:207
  83.5 7.6 %w_partial.2 = (f32[960,128]{1,0:T(8,128)}, f32[8,128]{1,0:T(8,128)}) custom-call(bf16[960,128]{1,0:T(8,128)(2,1)} %get-tuple-element.12.w_ref, bf16[32,4096]{1,0:T(8,128)(2,1)S(1)} %pad_maximum_fusion.3.refs_0_, bf16[32,4096]{1,0:T(8,128)(2,1)S(1)} %collective-permute-done.31.refs_1_, bf16[32,4096]{1,0:T(8,128)(2,1)S(1)} %collective-permute-done.32.refs_2_, ...), custom_call_target="tpu_custom_call" | custom-call | flops 2013265920 | bytes 7864320 | tf_op jit(solution)/shard_map/w_partial/pallas_call | solution.py:176
  91.1 8.3 %w_partial.3 = bf16[976,128]{1,0:T(8,128)(2,1)} custom-call(bf16[960,128]{1,0:T(8,128)(2,1)} %get-tuple-element.12.w_ref, bf16[32,4096]{1,0:T(8,128)(2,1)S(1)} %pad_maximum_fusion.2.refs_0_, bf16[32,4096]{1,0:T(8,128)(2,1)S(1)} %collective-permute-done.25.refs_1_, bf16[32,4096]{1,0:T(8,128)(2,1)S(1)} %collective-permute-done.26.refs_2_, ...), custom_call_target="tpu_custom_call" | custom-call | flops 2013265920 | bytes 7864320 | tf_op jit(solution)/shard_map/w_partial/pallas_call | solution.py:176
  99.4 1.3 %collective-permute-start.34 = (bf16[976,128]{1,0:T(8,128)(2,1)}, bf16[976,128]{1,0:T(8,128)(2,1)S(1)}, u32[]{:S(2)}, u32[]{:S(2)}) collective-permute-start(bf16[976,128]{1,0:T(8,128)(2,1)} %w_partial.3), channel_id=1, source_target_pairs={{0,1},{1,0},{2,3},{3,2},{4,5},{5,4},{6,7},{7,6},{8,9},{9,8},{10,11... | collective-permute-start | bytes 749576 | tf_op jit(solution)/shard_map/ppermute | solution.py:292
  101.5 6.6 %collective-permute-done.34 = bf16[976,128]{1,0:T(8,128)(2,1)S(1)} collective-permute-done((bf16[976,128]{1,0:T(8,128)(2,1)}, bf16[976,128]{1,0:T(8,128)(2,1)S(1)}, u32[]{:S(2)}, u32[]{:S(2)}) %collective-permute-start.34) | collective-permute-done | bytes 249888 | tf_op jit(solution)/shard_map/ppermute | solution.py:292
  108.9 2.0 %fusion.26 = f32[960,128]{1,0:T(8,128)} fusion(f32[960,128]{1,0:T(8,128)S(1)} %copy-done, bf16[976,128]{1,0:T(8,128)(2,1)S(1)} %collective-permute-done.34, bf16[976,128]{1,0:T(8,128)(2,1)} %w_partial.3, f32[128]{0:T(128)S(1)} %fusion.79), kind=kLoop, calls=%fused_computation.42 | loop fusion | flops 1597440 | bytes 1475072 | tf_op jit(solution)/shard_map/div | solution.py:299
  (81 shorter events, 16.7 us)
Async XLA Ops:
  1.6 10.6 %collective-permute-start.13 = (bf16[8,4096]{1,0:T(8,128)(2,1)S(1)}, bf16[8,4096]{1,0:T(8,128)(2,1)S(1)}, u32[]{:S(2)}, u32[]{:S(2)}) collective-permute-start(bf16[8,4096]{1,0:T(8,128)(2,1)S(1)} %get-tuple-element.26), channel_id=1, source_target_pairs={{0,8},{2,10},{4,12},{6,14},{8,16},{10,18},{12,20},{14,22},{16,24},... | collective-permute-start | bytes 196616 | tf_op jit(solution)/shard_map/ppermute | solution.py:207
  4.7 7.5 %collective-permute-start.12 = (bf16[8,4096]{1,0:T(8,128)(2,1)S(1)}, bf16[8,4096]{1,0:T(8,128)(2,1)S(1)}, u32[]{:S(2)}, u32[]{:S(2)}) collective-permute-start(bf16[8,4096]{1,0:T(8,128)(2,1)S(1)} %get-tuple-element.26), channel_id=1, source_target_pairs={{0,16},{2,18},{4,20},{6,22},{8,24},{10,26},{12,28},{14,30},{16,0},... | collective-permute-start | bytes 196616 | tf_op jit(solution)/shard_map/ppermute | solution.py:207
  7.3 4.9 %collective-permute-start.11 = (bf16[8,4096]{1,0:T(8,128)(2,1)S(1)}, bf16[8,4096]{1,0:T(8,128)(2,1)S(1)}, u32[]{:S(2)}, u32[]{:S(2)}) collective-permute-start(bf16[8,4096]{1,0:T(8,128)(2,1)S(1)} %get-tuple-element.26), channel_id=1, source_target_pairs={{0,24},{2,26},{4,28},{6,30},{8,0},{10,2},{12,4},{14,6},{16,8},{18,... | collective-permute-start | bytes 196616 | tf_op jit(solution)/shard_map/ppermute | solution.py:207
  12.3 7.6 %collective-permute-start.14 = (bf16[32,4096]{1,0:T(8,128)(2,1)S(1)}, bf16[32,4096]{1,0:T(8,128)(2,1)S(1)}, u32[]{:S(2)}, u32[]{:S(2)}) collective-permute-start(bf16[32,4096]{1,0:T(8,128)(2,1)S(1)} %pad_maximum_fusion.1.refs_0_), channel_id=1, source_target_pairs={{0,4},{2,6},{4,0},{6,2},{8,12},{10,14},{12,8},{14,10},{16,20},{18,... | collective-permute-start | bytes 786440 | tf_op jit(solution)/shard_map/ppermute | solution.py:207
  13.8 6.8 %collective-permute-start.2 = (bf16[8,4224]{1,0:T(8,128)(2,1)S(1)}, bf16[8,4224]{1,0:T(8,128)(2,1)S(1)}, u32[]{:S(2)}, u32[]{:S(2)}) collective-permute-start(bf16[8,4224]{1,0:T(8,128)(2,1)S(1)} %pad_maximum_fusion.5), channel_id=1, source_target_pairs={{0,8},{2,10},{4,12},{6,14},{8,16},{10,18},{12,20},{14,22},{16,24},... | collective-permute-start | bytes 202760 | tf_op jit(solution)/shard_map/ppermute | solution.py:207
  15.2 6.8 %collective-permute-start.1 = (bf16[8,4224]{1,0:T(8,128)(2,1)S(1)}, bf16[8,4224]{1,0:T(8,128)(2,1)S(1)}, u32[]{:S(2)}, u32[]{:S(2)}) collective-permute-start(bf16[8,4224]{1,0:T(8,128)(2,1)S(1)} %pad_maximum_fusion.5), channel_id=1, source_target_pairs={{0,16},{2,18},{4,20},{6,22},{8,24},{10,26},{12,28},{14,30},{16,0},... | collective-permute-start | bytes 202760 | tf_op jit(solution)/shard_map/ppermute | solution.py:207
  17.2 4.8 %collective-permute-start = (bf16[8,4224]{1,0:T(8,128)(2,1)S(1)}, bf16[8,4224]{1,0:T(8,128)(2,1)S(1)}, u32[]{:S(2)}, u32[]{:S(2)}) collective-permute-start(bf16[8,4224]{1,0:T(8,128)(2,1)S(1)} %pad_maximum_fusion.5), channel_id=1, source_target_pairs={{0,24},{2,26},{4,28},{6,30},{8,0},{10,2},{12,4},{14,6},{16,8},{18,... | collective-permute-start | bytes 202760 | tf_op jit(solution)/shard_map/ppermute | solution.py:207
  17.7 5.3 %collective-permute-start.15 = (bf16[32,4096]{1,0:T(8,128)(2,1)S(1)}, bf16[32,4096]{1,0:T(8,128)(2,1)S(1)}, u32[]{:S(2)}, u32[]{:S(2)}) collective-permute-start(bf16[32,4096]{1,0:T(8,128)(2,1)S(1)} %pad_maximum_fusion.1.refs_0_), channel_id=1, source_target_pairs={{0,2},{2,0},{4,6},{6,4},{8,10},{10,8},{12,14},{14,12},{16,18},{18,... | collective-permute-start | bytes 786440 | tf_op jit(solution)/shard_map/ppermute | solution.py:207
  19.9 3.0 %collective-permute-start.16 = (bf16[32,4096]{1,0:T(8,128)(2,1)S(1)}, bf16[32,4096]{1,0:T(8,128)(2,1)S(1)}, u32[]{:S(2)}, u32[]{:S(2)}) collective-permute-start(bf16[32,4096]{1,0:T(8,128)(2,1)S(1)} %collective-permute-done.14.refs_1_), channel_id=1, source_target_pairs={{0,2},{2,0},{4,6},{6,4},{8,10},{10,8},{12,14},{14,12},{16,18},{18,... | collective-permute-start | bytes 786440 | tf_op jit(solution)/shard_map/ppermute | solution.py:207
  22.0 8.2 %collective-permute-start.3 = (bf16[32,4224]{1,0:T(8,128)(2,1)S(1)}, bf16[32,4224]{1,0:T(8,128)(2,1)S(1)}, u32[]{:S(2)}, u32[]{:S(2)}) collective-permute-start(bf16[32,4224]{1,0:T(8,128)(2,1)S(1)} %pad_maximum_fusion.refs_0_), channel_id=1, source_target_pairs={{0,4},{2,6},{4,0},{6,2},{8,12},{10,14},{12,8},{14,10},{16,20},{18,... | collective-permute-start | bytes 811016 | tf_op jit(solution)/shard_map/ppermute | solution.py:207
  29.6 10.1 %collective-permute-start.17 = (bf16[64,4096]{1,0:T(8,128)(2,1)}, bf16[64,4096]{1,0:T(8,128)(2,1)S(1)}, u32[]{:S(2)}, u32[]{:S(2)}) collective-permute-start(bf16[64,4096]{1,0:T(8,128)(2,1)} %get-tuple-element.18), channel_id=1, source_target_pairs={{0,2},{2,0},{4,6},{6,4},{8,10},{10,8},{12,14},{14,12},{16,18},{18,... | collective-permute-start | bytes 1572872 | tf_op jit(solution)/shard_map/ppermute | solution.py:207
  40.1 9.2 %collective-permute-start.18 = (bf16[32,4096]{1,0:T(8,128)(2,1)S(1)}, bf16[32,4096]{1,0:T(8,128)(2,1)S(1)}, u32[]{:S(2)}, u32[]{:S(2)}) collective-permute-start(bf16[32,4096]{1,0:T(8,128)(2,1)S(1)} %fusion.15), channel_id=1, source_target_pairs={{0,4},{2,6},{4,0},{6,2},{8,12},{10,14},{12,8},{14,10},{16,20},{18,... | collective-permute-start | bytes 786440 | tf_op jit(solution)/shard_map/ppermute | solution.py:207
  43.2 11.2 %collective-permute-start.7 = (bf16[32,4096]{1,0:T(8,128)(2,1)S(1)}, bf16[32,4096]{1,0:T(8,128)(2,1)S(1)}, u32[]{:S(2)}, u32[]{:S(2)}) collective-permute-start(bf16[32,4096]{1,0:T(8,128)(2,1)S(1)} %fusion.14), channel_id=1, source_target_pairs={{0,4},{2,6},{4,0},{6,2},{8,12},{10,14},{12,8},{14,10},{16,20},{18,... | collective-permute-start | bytes 786440 | tf_op jit(solution)/shard_map/ppermute | solution.py:207
  49.6 7.7 %collective-permute-start.21 = (bf16[8,4096]{1,0:T(8,128)(2,1)S(1)}, bf16[8,4096]{1,0:T(8,128)(2,1)S(1)}, u32[]{:S(2)}, u32[]{:S(2)}) collective-permute-start(bf16[8,4096]{1,0:T(8,128)(2,1)S(1)} %get-tuple-element.29), channel_id=1, source_target_pairs={{0,24},{2,26},{4,28},{6,30},{8,0},{10,2},{12,4},{14,6},{16,8},{18,... | collective-permute-start | bytes 196616 | tf_op jit(solution)/shard_map/ppermute | solution.py:207
  51.7 6.8 %collective-permute-start.20 = (bf16[8,4096]{1,0:T(8,128)(2,1)S(1)}, bf16[8,4096]{1,0:T(8,128)(2,1)S(1)}, u32[]{:S(2)}, u32[]{:S(2)}) collective-permute-start(bf16[8,4096]{1,0:T(8,128)(2,1)S(1)} %get-tuple-element.30), channel_id=1, source_target_pairs={{0,16},{2,18},{4,20},{6,22},{8,24},{10,26},{12,28},{14,30},{16,0},... | collective-permute-start | bytes 196616 | tf_op jit(solution)/shard_map/ppermute | solution.py:207
  52.5 6.1 %collective-permute-start.19 = (bf16[8,4096]{1,0:T(8,128)(2,1)S(1)}, bf16[8,4096]{1,0:T(8,128)(2,1)S(1)}, u32[]{:S(2)}, u32[]{:S(2)}) collective-permute-start(bf16[8,4096]{1,0:T(8,128)(2,1)S(1)} %get-tuple-element.28), channel_id=1, source_target_pairs={{0,8},{2,10},{4,12},{6,14},{8,16},{10,18},{12,20},{14,22},{16,24},... | collective-permute-start | bytes 196616 | tf_op jit(solution)/shard_map/ppermute | solution.py:207
  54.6 6.8 %collective-permute-start.8 = (bf16[8,4096]{1,0:T(8,128)(2,1)S(1)}, bf16[8,4096]{1,0:T(8,128)(2,1)S(1)}, u32[]{:S(2)}, u32[]{:S(2)}) collective-permute-start(bf16[8,4096]{1,0:T(8,128)(2,1)S(1)} %get-tuple-element.33), channel_id=1, source_target_pairs={{0,8},{2,10},{4,12},{6,14},{8,16},{10,18},{12,20},{14,22},{16,24},... | collective-permute-start | bytes 196616 | tf_op jit(solution)/shard_map/ppermute | solution.py:207
  56.1 8.8 %collective-permute-start.9 = (bf16[8,4096]{1,0:T(8,128)(2,1)S(1)}, bf16[8,4096]{1,0:T(8,128)(2,1)S(1)}, u32[]{:S(2)}, u32[]{:S(2)}) collective-permute-start(bf16[8,4096]{1,0:T(8,128)(2,1)S(1)} %get-tuple-element.32), channel_id=1, source_target_pairs={{0,16},{2,18},{4,20},{6,22},{8,24},{10,26},{12,28},{14,30},{16,0},... | collective-permute-start | bytes 196616 | tf_op jit(solution)/shard_map/ppermute | solution.py:207
  57.3 7.6 %collective-permute-start.10 = (bf16[8,4096]{1,0:T(8,128)(2,1)S(1)}, bf16[8,4096]{1,0:T(8,128)(2,1)S(1)}, u32[]{:S(2)}, u32[]{:S(2)}) collective-permute-start(bf16[8,4096]{1,0:T(8,128)(2,1)S(1)} %get-tuple-element.31), channel_id=1, source_target_pairs={{0,24},{2,26},{4,28},{6,30},{8,0},{10,2},{12,4},{14,6},{16,8},{18,... | collective-permute-start | bytes 196616 | tf_op jit(solution)/shard_map/ppermute | solution.py:207
  58.7 10.1 %collective-permute-start.30 = (bf16[8,4096]{1,0:T(8,128)(2,1)S(1)}, bf16[8,4096]{1,0:T(8,128)(2,1)S(1)}, u32[]{:S(2)}, u32[]{:S(2)}) collective-permute-start(bf16[8,4096]{1,0:T(8,128)(2,1)S(1)} %get-tuple-element.22), channel_id=1, source_target_pairs={{0,8},{2,10},{4,12},{6,14},{8,16},{10,18},{12,20},{14,22},{16,24},... | collective-permute-start | bytes 196616 | tf_op jit(solution)/shard_map/ppermute | solution.py:207
  59.6 11.0 %collective-permute-start.29 = (bf16[8,4096]{1,0:T(8,128)(2,1)S(1)}, bf16[8,4096]{1,0:T(8,128)(2,1)S(1)}, u32[]{:S(2)}, u32[]{:S(2)}) collective-permute-start(bf16[8,4096]{1,0:T(8,128)(2,1)S(1)} %get-tuple-element.22), channel_id=1, source_target_pairs={{0,16},{2,18},{4,20},{6,22},{8,24},{10,26},{12,28},{14,30},{16,0},... | collective-permute-start | bytes 196616 | tf_op jit(solution)/shard_map/ppermute | solution.py:207
  61.4 9.2 %collective-permute-start.28 = (bf16[8,4096]{1,0:T(8,128)(2,1)S(1)}, bf16[8,4096]{1,0:T(8,128)(2,1)S(1)}, u32[]{:S(2)}, u32[]{:S(2)}) collective-permute-start(bf16[8,4096]{1,0:T(8,128)(2,1)S(1)} %get-tuple-element.22), channel_id=1, source_target_pairs={{0,24},{2,26},{4,28},{6,30},{8,0},{10,2},{12,4},{14,6},{16,8},{18,... | collective-permute-start | bytes 196616 | tf_op jit(solution)/shard_map/ppermute | solution.py:207
  65.1 6.8 %collective-permute-start.24 = (bf16[8,4096]{1,0:T(8,128)(2,1)S(1)}, bf16[8,4096]{1,0:T(8,128)(2,1)S(1)}, u32[]{:S(2)}, u32[]{:S(2)}) collective-permute-start(bf16[8,4096]{1,0:T(8,128)(2,1)S(1)} %get-tuple-element.24), channel_id=1, source_target_pairs={{0,8},{2,10},{4,12},{6,14},{8,16},{10,18},{12,20},{14,22},{16,24},... | collective-permute-start | bytes 196616 | tf_op jit(solution)/shard_map/ppermute | solution.py:207
  68.2 6.3 %collective-permute-start.23 = (bf16[8,4096]{1,0:T(8,128)(2,1)S(1)}, bf16[8,4096]{1,0:T(8,128)(2,1)S(1)}, u32[]{:S(2)}, u32[]{:S(2)}) collective-permute-start(bf16[8,4096]{1,0:T(8,128)(2,1)S(1)} %get-tuple-element.24), channel_id=1, source_target_pairs={{0,16},{2,18},{4,20},{6,22},{8,24},{10,26},{12,28},{14,30},{16,0},... | collective-permute-start | bytes 196616 | tf_op jit(solution)/shard_map/ppermute | solution.py:207
  68.9 5.6 %collective-permute-start.22 = (bf16[8,4096]{1,0:T(8,128)(2,1)S(1)}, bf16[8,4096]{1,0:T(8,128)(2,1)S(1)}, u32[]{:S(2)}, u32[]{:S(2)}) collective-permute-start(bf16[8,4096]{1,0:T(8,128)(2,1)S(1)} %get-tuple-element.24), channel_id=1, source_target_pairs={{0,24},{2,26},{4,28},{6,30},{8,0},{10,2},{12,4},{14,6},{16,8},{18,... | collective-permute-start | bytes 196616 | tf_op jit(solution)/shard_map/ppermute | solution.py:207
  70.6 8.7 %collective-permute-start.31 = (bf16[32,4096]{1,0:T(8,128)(2,1)S(1)}, bf16[32,4096]{1,0:T(8,128)(2,1)S(1)}, u32[]{:S(2)}, u32[]{:S(2)}) collective-permute-start(bf16[32,4096]{1,0:T(8,128)(2,1)S(1)} %pad_maximum_fusion.3.refs_0_), channel_id=1, source_target_pairs={{0,4},{2,6},{4,0},{6,2},{8,12},{10,14},{12,8},{14,10},{16,20},{18,... | collective-permute-start | bytes 786440 | tf_op jit(solution)/shard_map/ppermute | solution.py:207
  74.5 9.0 %collective-permute-start.25 = (bf16[32,4096]{1,0:T(8,128)(2,1)S(1)}, bf16[32,4096]{1,0:T(8,128)(2,1)S(1)}, u32[]{:S(2)}, u32[]{:S(2)}) collective-permute-start(bf16[32,4096]{1,0:T(8,128)(2,1)S(1)} %pad_maximum_fusion.2.refs_0_), channel_id=1, source_target_pairs={{0,4},{2,6},{4,0},{6,2},{8,12},{10,14},{12,8},{14,10},{16,20},{18,... | collective-permute-start | bytes 786440 | tf_op jit(solution)/shard_map/ppermute | solution.py:207
  75.7 7.8 %collective-permute-start.32 = (bf16[32,4096]{1,0:T(8,128)(2,1)S(1)}, bf16[32,4096]{1,0:T(8,128)(2,1)S(1)}, u32[]{:S(2)}, u32[]{:S(2)}) collective-permute-start(bf16[32,4096]{1,0:T(8,128)(2,1)S(1)} %pad_maximum_fusion.3.refs_0_), channel_id=1, source_target_pairs={{0,2},{2,0},{4,6},{6,4},{8,10},{10,8},{12,14},{14,12},{16,18},{18,... | collective-permute-start | bytes 786440 | tf_op jit(solution)/shard_map/ppermute | solution.py:207
  79.3 4.2 %collective-permute-start.33 = (bf16[32,4096]{1,0:T(8,128)(2,1)S(1)}, bf16[32,4096]{1,0:T(8,128)(2,1)S(1)}, u32[]{:S(2)}, u32[]{:S(2)}) collective-permute-start(bf16[32,4096]{1,0:T(8,128)(2,1)S(1)} %collective-permute-done.31.refs_1_), channel_id=1, source_target_pairs={{0,2},{2,0},{4,6},{6,4},{8,10},{10,8},{12,14},{14,12},{16,18},{18,... | collective-permute-start | bytes 786440 | tf_op jit(solution)/shard_map/ppermute | solution.py:207
  79.3 11.8 %collective-permute-start.26 = (bf16[32,4096]{1,0:T(8,128)(2,1)S(1)}, bf16[32,4096]{1,0:T(8,128)(2,1)S(1)}, u32[]{:S(2)}, u32[]{:S(2)}) collective-permute-start(bf16[32,4096]{1,0:T(8,128)(2,1)S(1)} %pad_maximum_fusion.2.refs_0_), channel_id=1, source_target_pairs={{0,2},{2,0},{4,6},{6,4},{8,10},{10,8},{12,14},{14,12},{16,18},{18,... | collective-permute-start | bytes 786440 | tf_op jit(solution)/shard_map/ppermute | solution.py:207
  83.5 7.6 %collective-permute-start.27 = (bf16[32,4096]{1,0:T(8,128)(2,1)S(1)}, bf16[32,4096]{1,0:T(8,128)(2,1)S(1)}, u32[]{:S(2)}, u32[]{:S(2)}) collective-permute-start(bf16[32,4096]{1,0:T(8,128)(2,1)S(1)} %collective-permute-done.25.refs_1_), channel_id=1, source_target_pairs={{0,2},{2,0},{4,6},{6,4},{8,10},{10,8},{12,14},{14,12},{16,18},{18,... | collective-permute-start | bytes 786440 | tf_op jit(solution)/shard_map/ppermute | solution.py:207
  99.4 8.7 %collective-permute-start.34 = (bf16[976,128]{1,0:T(8,128)(2,1)}, bf16[976,128]{1,0:T(8,128)(2,1)S(1)}, u32[]{:S(2)}, u32[]{:S(2)}) collective-permute-start(bf16[976,128]{1,0:T(8,128)(2,1)} %w_partial.3), channel_id=1, source_target_pairs={{0,1},{1,0},{2,3},{3,2},{4,5},{5,4},{6,7},{7,6},{8,9},{9,8},{10,11... | collective-permute-start | bytes 749576 | tf_op jit(solution)/shard_map/ppermute | solution.py:292
  (6 other events, 80.4 us)

commit v2 on v1

v2 whole, which is shorter than its diff:
```python
import functools

import jax
import jax.numpy as jnp
from jax import lax
from jax.experimental import pallas as pl
from jax.experimental.pallas import tpu as pltpu
from jax.sharding import PartitionSpec as P


F32 = jnp.float32
BF16 = jnp.bfloat16
SPACE = pltpu.VMEM
H_SHARES = (1, 1, 2, 4)
W_SHARES = (1, 1, 1, 1)
LIMIT = 40 << 20
SPLIT = (4, 4)
H_KNEE = 2.0**20
W_KNEE = 2.0**17


def encode(value, knee):
    part = jnp.minimum(value * (1.0 / knee), 1.0)
    return (value * part * part * part).astype(BF16)


def decode(code, knee):
    code = code.astype(F32)
    root = knee * lax.rsqrt(lax.rsqrt(code * (1.0 / knee)))
    return jnp.where(code < knee, root, code)


def encode_square(value, knee):
    return (value * jnp.minimum(value * (1.0 / knee), 1.0)).astype(BF16)


def decode_square(code, knee):
    code = code.astype(F32)
    square = code * knee
    return jnp.where(code < knee, square * lax.rsqrt(jnp.maximum(square, 1e-30)), code)


def parts_of(value):
    high = value.astype(BF16)
    rest = value - high.astype(F32)
    middle = rest.astype(BF16)
    low = (rest - middle.astype(F32)).astype(BF16)
    return [part.astype(F32) for part in (high, middle, low)]


def prepare_kernel(w_ref, pick_ref, w_rel_ref, wt_rel_ref, sum_ref):
    w_value = w_ref[...]
    w_copy = w_value.astype(BF16)
    pick = pick_ref[...]
    second = (((1,), (1,)), ((), ()))
    w_rel_ref[...] = lax.dot_general(w_copy, pick, second, preferred_element_type=F32).astype(BF16)
    wt_rel_ref[...] = lax.dot_general(pick, w_copy, second, preferred_element_type=F32).astype(BF16)
    rank = w_ref.shape[1]
    rows = sum_ref.shape[0]
    high, middle, low = parts_of(jnp.sum(w_value, axis=0, keepdims=True))
    for block in range(sum_ref.shape[1] // rank):
        row = lax.broadcasted_iota(jnp.int32, (rows, rank), 0) + block * rows
        value = jnp.where(row == 0, high, jnp.where(row == 1, middle, low))
        sum_ref[:, block * rank : (block + 1) * rank] = jnp.where(row < 3, value, 0.0).astype(BF16)


def prepare(w_factor, pick, sum_shape):
    cells, rank = w_factor.shape
    return pl.pallas_call(
        prepare_kernel,
        out_shape=[
            jax.ShapeDtypeStruct((cells, rank), BF16),
            jax.ShapeDtypeStruct((rank, cells), BF16),
            jax.ShapeDtypeStruct(sum_shape, BF16),
        ],
        compiler_params=pltpu.CompilerParams(vmem_limit_bytes=LIMIT),
        name="prepare",
    )(w_factor, pick)


def streamed(counts_ref, buffer_ref, sems, start, shares):
    width = buffer_ref.shape[1]
    sizes = [width * share // sum(shares) for share in shares]
    copies = []
    at = 0
    for i, size in enumerate(sizes):
        copy = pltpu.make_async_copy(
            counts_ref.at[:, pl.ds(start + at, size)],
            buffer_ref.at[:, pl.ds(at, size)],
            sems.at[i],
        )
        copy.start()
        copies.append((copy, slice(at, at + size)))
        at += size
    return copies


def quotient_of(w_ref, h_tile, block):
    modeled = jnp.dot(w_ref[...], h_tile, preferred_element_type=F32)
    return (block.astype(F32) / modeled).astype(BF16)


def h_kernel(wt_ref, w_ref, *refs, start):
    pieces, (counts_ref, keep_ref, send_ref, buffer_ref, sems) = refs[:-5], refs[-5:]
    keep = keep_ref.shape[0]
    for copy, span in streamed(counts_ref, buffer_ref, sems, start, H_SHARES):
        h_tile = jnp.concatenate([piece[:, span] for piece in pieces], axis=0)
        copy.wait()
        quotient = quotient_of(w_ref, h_tile, buffer_ref[:, span])
        term = jnp.dot(wt_ref[...], quotient, preferred_element_type=F32)
        keep_ref[:, span] = term[:keep]
        send_ref[:, span] = encode_square(term[keep:], H_KNEE)


def w_kernel(w_ref, *refs, count, start, first, last):
    pieces, counts_ref = refs[:count], refs[count]
    if last:
        running, pick_ref = refs[count + 1 : -6], refs[-6]
        out_ref, buffer_ref, sems, total_ref, sum_ref = refs[-5:]
    else:
        running = refs[count + 1 : -4]
        total_ref, sum_ref, buffer_ref, sems = refs[-4:]
    copies = streamed(counts_ref, buffer_ref, sems, start, W_SHARES)
    across = (((1,), (1,)), ((), ()))
    if first:
        total_ref[...] = jnp.zeros_like(total_ref)
        sum_ref[...] = jnp.zeros_like(sum_ref)
    else:
        total_ref[...] = running[0][...]
        sum_ref[...] = running[1][...]
    for copy, span in copies:
        h_tile = jnp.concatenate([piece[:, span] for piece in pieces], axis=0)
        ones = jnp.ones((sum_ref.shape[0], h_tile.shape[1]), BF16)
        copy.wait()
        quotient = quotient_of(w_ref, h_tile, buffer_ref[:, span])
        total_ref[...] += lax.dot_general(quotient, h_tile, across, preferred_element_type=F32)
        sum_ref[...] += lax.dot_general(ones, h_tile, across, preferred_element_type=F32)

    if last:
        cells = total_ref.shape[0]
        exact = lax.Precision.HIGHEST
        pick = pick_ref[...]
        total = jnp.dot(total_ref[...], pick, precision=exact, preferred_element_type=F32)
        sums = jnp.dot(sum_ref[...], pick, precision=exact, preferred_element_type=F32)
        high, middle, low = parts_of(sums[:1])
        out_ref[:cells, :] = encode(total, W_KNEE)
        row = lax.broadcasted_iota(jnp.int32, (16, sums.shape[1]), 0)
        tail = jnp.where(row == 0, high, jnp.where(row == 1, middle, low))
        out_ref[cells:, :] = jnp.where(row < 3, tail, 0.0).astype(BF16)


def cost(cells, rank, width):
    return pl.CostEstimate(
        flops=4 * cells * rank * width, transcendentals=0, bytes_accessed=2 * cells * width
    )


def held(pieces):
    return [pltpu.with_memory_space_constraint(piece, SPACE) for piece in pieces]


def call(kernel, held_args, counts, more_args, outs, width, scratch=()):
    cells = counts.shape[0]
    held_args = held(held_args)
    more_args = held(more_args)
    local = pl.BlockSpec(memory_space=pltpu.VMEM)
    return pl.pallas_call(
        kernel,
        in_specs=[local] * len(held_args)
        + [pl.BlockSpec(memory_space=pl.ANY)]
        + [local] * len(more_args),
        out_specs=[local] * len(outs),
        out_shape=[pltpu.VMEM(shape, kind) for shape, kind in outs],
        scratch_shapes=[pltpu.VMEM((cells, width), counts.dtype), pltpu.SemaphoreType.DMA((8,))]
        + [pltpu.VMEM(shape, kind) for shape, kind in scratch],
        cost_estimate=cost(cells, held_args[0].shape[1], width),
        compiler_params=pltpu.CompilerParams(vmem_limit_bytes=LIMIT),
    )(*held_args, counts, *more_args)


def h_partial(start, wt_rel, w_rel, pieces, counts, width):
    half = wt_rel.shape[0] // 2
    outs = [((half, width), F32), ((half, width), BF16)]
    kernel = functools.partial(h_kernel, start=start)
    return call(kernel, [wt_rel, w_rel, *pieces], counts, [], outs, width)


def w_partial(start, w_rel, pieces, counts, width, running, pick):
    cells, rank = w_rel.shape
    last = pick is not None
    sums = [((cells, rank), F32), ((8, rank), F32)]
    outs = [((cells + 16, rank), BF16)] if last else sums
    kernel = functools.partial(
        w_kernel, count=len(pieces), start=start, first=not running, last=last
    )
    more = list(running) + ([pick] if last else [])
    out = call(kernel, [w_rel, *pieces], counts, more, outs, width, sums if last else ())
    return out[0] if last else out


def per_device(counts, w_factor, h_factor, *, devices, gene_devices):
    rows, genes = h_factor.shape
    cells, rank = w_factor.shape
    chips = devices // 2
    across = 2 ** ((chips.bit_length() - 1) // 2)
    along = chips // across
    block = along * rows
    widths = [genes * share // sum(SPLIT) for share in SPLIT]
    starts = [sum(widths[:i]) for i in range(len(widths))]
    chunks = len(widths)

    index = lax.axis_index("cell")
    core = index % 2
    x_at = (index // 2) % across
    z_at = index // (2 * across)

    def send(value, route):
        return lax.ppermute(value, "cell", [(i, route(i)) for i in range(devices)])

    def swap(value):
        return send(value, lambda i: i ^ 1)

    def shift_x(value, s):
        return send(
            value, lambda i: i % 2 + 2 * ((i // 2 + s) % across) + i // (2 * across) * 2 * across
        )

    def shift_z(value, s):
        return send(value, lambda i: (i + 2 * across * s) % devices)

    place = jnp.arange(rank)
    source = (
        (z_at + place // rows % along) % along * (2 * across * rows)
        + (x_at + place // block % across) % across * (2 * rows)
        + (core + place // (block * across)) % 2 * rows
        + place % rows
    )
    pick = source[:, None] == jnp.arange(rank)[None, :]

    lanes = -(-3 // rows)
    w_rel, wt_rel, sums = prepare(w_factor, pick.astype(BF16), (rows, lanes * rank))

    def gather(own):
        column = [own]
        for s in range(1, along):
            column.append(shift_z(own, along - s))
        column = jnp.concatenate(column, 0)
        mine = [column] + [shift_x(column, across - s) for s in range(1, across)]
        return mine + [swap(piece) for piece in mine]

    def reduce(keep, other):
        total = keep + decode_square(swap(other), H_KNEE)
        sent = encode(total[block:], H_KNEE)
        column = total[:block]
        got = [shift_x(sent[(s - 1) * block : s * block], s) for s in range(1, across)]
        for piece in got:
            column = column + decode(piece, H_KNEE)
        sent = encode(column[rows:], H_KNEE)
        mine = column[:rows]
        got = []
        for s in range(1, along):
            got.append(shift_z(sent[(s - 1) * rows : s * rows], s))
        for piece in got:
            mine = mine + decode(piece, H_KNEE)
        return mine

    gathered = []
    for i in range(chunks):
        own = h_factor[:, starts[i] : starts[i] + widths[i]].astype(BF16)
        if i == chunks - 1:
            own = jnp.concatenate([own, sums], 1)
        gathered.append(gather(own))
    w_totals = jnp.concatenate([piece[:, widths[-1] :] for piece in gathered[-1]], 0).astype(F32)
    w_totals = jnp.sum(jnp.sum(w_totals, axis=0).reshape(lanes, rank), axis=0)
    own_totals = lax.dynamic_slice_in_dim(w_totals, index * rows, rows, 0)[:, None]

    updated = []
    again = []
    for i in range(chunks):
        keep, other = h_partial(starts[i], wt_rel, w_rel, gathered[i], counts, widths[i])
        numerator = reduce(keep, other)
        if updated:
            numerator, _ = lax.optimization_barrier((numerator, updated[-1]))
        new = h_factor[:, starts[i] : starts[i] + widths[i]] * numerator / own_totals
        updated.append(new)
        again.append(gather(new.astype(BF16)))
    h_updated = jnp.concatenate(updated, 1)

    pick = pick.astype(F32)
    running = ()
    for i in range(chunks):
        last = i == chunks - 1 and gene_devices == 2
        running = w_partial(
            starts[i], w_rel, again[i], counts, widths[i], running, pick if last else None
        )
    if gene_devices == 2:
        got = lax.ppermute(running, "gene", [(0, 1), (1, 0)])
        totals = sum(
            side[cells + row : cells + row + 1].astype(F32)
            for row in range(3)
            for side in (running, got)
        )
        kept = decode(running[:cells], W_KNEE)
        kept, got = lax.optimization_barrier((kept, got))
        w_updated = w_factor * (kept + decode(got[:cells], W_KNEE)) * (1.0 / totals)
    else:
        numerator, h_totals = lax.psum(running, "gene")
        ratio = jnp.dot(numerator / h_totals[:1], pick, precision=lax.Precision.HIGHEST)
        w_updated = w_factor * ratio
    return (w_updated, h_updated)


def solution(mesh):
    in_specs = (P("cell", "gene"), P("cell", None), P("cell", "gene"))
    out_specs = (P("cell", None), P("cell", "gene"))

    def body(counts, w_factor, h_factor):
        return per_device(
            counts,
            w_factor,
            h_factor,
            devices=mesh.shape["cell"],
            gene_devices=mesh.shape["gene"],
        )

    return jax.shard_map(
        body, mesh=mesh, in_specs=in_specs, out_specs=out_specs, check_vma=False
    )
```

time: 111 us -> 106 us (0.955)
  Pallas kernels: 31.6 us -> 25.2 us
  other arithmetic: 7.83 us -> 3.6 us
  starting transfers between devices: 38 us -> 40.9 us
  waiting for transfers between devices: 31.5 us -> 33.2 us
    pallas_call x4, Pallas kernels: 29.5 us -> 24.9 us  [call(): pl.pallas_call(kernel, in_specs=[local] * len(held_args) + [pl.BlockSpec(...]
    ppermute x34, starting transfers between devices: 36.7 us -> 40.1 us  [send(): return lax.ppermute(value, 'cell', [(i, route(i)) for i in range(devices)])]
    div x2 -> x0, other arithmetic: 2.81 us -> none  [per_device(): w_updated = w_factor * numerator / totals]
    pallas_call x1, Pallas kernels: 2.11 us -> 0.31 us  [prepare(): pl.pallas_call(prepare_kernel, out_shape=[jax.ShapeDtypeStruct((cells, ra...]
    ppermute x34, waiting for transfers between devices: 24.9 us -> 26.4 us  [send(): return lax.ppermute(value, 'cell', [(i, route(i)) for i in range(devices)])]
    add x2, other arithmetic: 1.78 us -> 0.55 us  [reduce(): total = keep + decode_square(swap(other), H_KNEE)]
  transfers between devices with their start and end apart: 35 -> 35, of which waited for: 14 -> 13; matrix products, arithmetic and copies ran while one was open for 5% -> 3% of each run, Pallas kernels for 21% -> 16%
where the time goes in v2:
time: 106 us
  starting transfers between devices  40.9 us (39%)
  waiting for transfers between devices  33.2 us (31%)
  Pallas kernels  25.2 us (24%)
  other arithmetic  3.6 us (3%)
  local copies, waits for them, and re-layouts  2.14 us (2%)
    ppermute x34, starting transfers between devices, send(): return lax.ppermute(value, 'cell', [(i, route(i)) for i in range(devices)])  40.1 us
    ppermute x34, waiting for transfers between devices, send(): return lax.ppermute(value, 'cell', [(i, route(i)) for i in range(devices)])  26.4 us
    pallas_call x4, Pallas kernels, call(): pl.pallas_call(kernel, in_specs=[local] * len(held_args) + [pl.BlockSpec(...  24.9 us
    ppermute x1, waiting for transfers between devices, per_device(): got = lax.ppermute(running, 'gene', [(0, 1), (1, 0)])  6.89 us
  transfers between devices with their start and end apart: 35, of which 13 were waited for; matrix products, arithmetic and copies ran while one was open for 3% of the time, Pallas kernels for 16%

profile of v2, /device:TPU:0, one launch (start us, length us, event | category | flops | bytes accessed | tf_op | source)
XLA Modules:
  0.0 105.9 jit_solution(14688362253991043801)
XLA Ops:
  1.6 3.1 %collective-permute-start.13 = (bf16[8,4096]{1,0:T(8,128)(2,1)S(1)}, bf16[8,4096]{1,0:T(8,128)(2,1)S(1)}, u32[]{:S(2)}, u32[]{:S(2)}) collective-permute-start(bf16[8,4096]{1,0:T(8,128)(2,1)S(1)} %get-tuple-element.30), channel_id=1, source_target_pairs={{0,8},{2,10},{4,12},{6,14},{8,16},{10,18},{12,20},{14,22},{16,24},... | collective-permute-start | bytes 196616 | tf_op jit(solution)/shard_map/ppermute | solution.py:218
  4.7 2.6 %collective-permute-start.12 = (bf16[8,4096]{1,0:T(8,128)(2,1)S(1)}, bf16[8,4096]{1,0:T(8,128)(2,1)S(1)}, u32[]{:S(2)}, u32[]{:S(2)}) collective-permute-start(bf16[8,4096]{1,0:T(8,128)(2,1)S(1)} %get-tuple-element.30), channel_id=1, source_target_pairs={{0,16},{2,18},{4,20},{6,22},{8,24},{10,26},{12,28},{14,30},{16,0},... | collective-permute-start | bytes 196616 | tf_op jit(solution)/shard_map/ppermute | solution.py:218
  7.3 1.3 %collective-permute-start.11 = (bf16[8,4096]{1,0:T(8,128)(2,1)S(1)}, bf16[8,4096]{1,0:T(8,128)(2,1)S(1)}, u32[]{:S(2)}, u32[]{:S(2)}) collective-permute-start(bf16[8,4096]{1,0:T(8,128)(2,1)S(1)} %get-tuple-element.30), channel_id=1, source_target_pairs={{0,24},{2,26},{4,28},{6,30},{8,0},{10,2},{12,4},{14,6},{16,8},{18,... | collective-permute-start | bytes 196616 | tf_op jit(solution)/shard_map/ppermute | solution.py:218
  11.2 2.8 %collective-permute-start = (bf16[8,4224]{1,0:T(8,128)(2,1)S(1)}, bf16[8,4224]{1,0:T(8,128)(2,1)S(1)}, u32[]{:S(2)}, u32[]{:S(2)}) collective-permute-start(bf16[8,4224]{1,0:T(8,128)(2,1)S(1)} %pad_maximum_fusion.5), channel_id=1, source_target_pairs={{0,24},{2,26},{4,28},{6,30},{8,0},{10,2},{12,4},{14,6},{16,8},{18,... | collective-permute-start | bytes 202760 | tf_op jit(solution)/shard_map/ppermute | solution.py:218
  14.1 1.6 %collective-permute-start.14 = (bf16[32,4096]{1,0:T(8,128)(2,1)S(1)}, bf16[32,4096]{1,0:T(8,128)(2,1)S(1)}, u32[]{:S(2)}, u32[]{:S(2)}) collective-permute-start(bf16[32,4096]{1,0:T(8,128)(2,1)S(1)} %pad_maximum_fusion.1.refs_0_), channel_id=1, source_target_pairs={{0,4},{2,6},{4,0},{6,2},{8,12},{10,14},{12,8},{14,10},{16,20},{18,... | collective-permute-start | bytes 786440 | tf_op jit(solution)/shard_map/ppermute | solution.py:218
  16.6 1.6 %collective-permute-done.1 = bf16[8,4224]{1,0:T(8,128)(2,1)S(1)} collective-permute-done((bf16[8,4224]{1,0:T(8,128)(2,1)S(1)}, bf16[8,4224]{1,0:T(8,128)(2,1)S(1)}, u32[]{:S(2)}, u32[]{:S(2)}) %collective-permute-start.1) | collective-permute-done | bytes 67616 | tf_op jit(solution)/shard_map/ppermute | solution.py:218
  18.2 1.6 %collective-permute-start.3 = (bf16[32,4224]{1,0:T(8,128)(2,1)S(1)}, bf16[32,4224]{1,0:T(8,128)(2,1)S(1)}, u32[]{:S(2)}, u32[]{:S(2)}) collective-permute-start(bf16[32,4224]{1,0:T(8,128)(2,1)S(1)} %pad_maximum_fusion.refs_0_), channel_id=1, source_target_pairs={{0,4},{2,6},{4,0},{6,2},{8,12},{10,14},{12,8},{14,10},{16,20},{18,... | collective-permute-start | bytes 811016 | tf_op jit(solution)/shard_map/ppermute | solution.py:218
  20.2 3.1 %collective-permute-done.14.refs_1_ = bf16[32,4096]{1,0:T(8,128)(2,1)S(1)} collective-permute-done((bf16[32,4096]{1,0:T(8,128)(2,1)S(1)}, bf16[32,4096]{1,0:T(8,128)(2,1)S(1)}, u32[]{:S(2)}, u32[]{:S(2)}) %collective-permute-start.14) | collective-permute-done | bytes 262176 | tf_op jit(solution)/shard_map/ppermute | solution.py:218
  23.3 3.3 %collective-permute-done.3.refs_1_ = bf16[32,4224]{1,0:T(8,128)(2,1)S(1)} collective-permute-done((bf16[32,4224]{1,0:T(8,128)(2,1)S(1)}, bf16[32,4224]{1,0:T(8,128)(2,1)S(1)}, u32[]{:S(2)}, u32[]{:S(2)}) %collective-permute-start.3) | collective-permute-done | bytes 270368 | tf_op jit(solution)/shard_map/ppermute | solution.py:218
  26.6 5.2 %shard_map.51 = (f32[64,4096]{1,0:T(8,128)S(1)}, bf16[64,4096]{1,0:T(8,128)(2,1)S(1)}) custom-call(bf16[128,960]{1,0:T(8,128)(2,1)S(1)} %get-tuple-element.15.wt_ref, bf16[960,128]{1,0:T(8,128)(2,1)S(1)} %get-tuple-element.14.w_ref, bf16[32,4096]{1,0:T(8,128)(2,1)S(1)} %pad_maximum_fusion.1.refs_0_, bf16[32,4096]{1,0:T(8,128)(2,1)S(1)} %collective-permute-done.14.refs_1_, ...), custom_call_target="tpu_custom_call" | custom-call | flops 15099494400 | bytes 7864320 | tf_op jit(solution)/shard_map/pallas_call | solution.py:167
  32.4 5.2 %shard_map.50 = (f32[64,4096]{1,0:T(8,128)S(1)}, bf16[64,4096]{1,0:T(8,128)(2,1)S(1)}) custom-call(bf16[128,960]{1,0:T(8,128)(2,1)S(1)} %get-tuple-element.15.wt_ref, bf16[960,128]{1,0:T(8,128)(2,1)S(1)} %get-tuple-element.14.w_ref, bf16[32,4224]{1,0:T(8,128)(2,1)S(1)} %pad_maximum_fusion.refs_0_, bf16[32,4224]{1,0:T(8,128)(2,1)S(1)} %collective-permute-done.3.refs_1_, ...), custom_call_target="tpu_custom_call" | custom-call | flops 15099494400 | bytes 7864320 | tf_op jit(solution)/shard_map/pallas_call | solution.py:167
  38.1 1.6 %collective-permute-start.18 = (bf16[32,4096]{1,0:T(8,128)(2,1)S(1)}, bf16[32,4096]{1,0:T(8,128)(2,1)S(1)}, u32[]{:S(2)}, u32[]{:S(2)}) collective-permute-start(bf16[32,4096]{1,0:T(8,128)(2,1)S(1)} %fusion.15), channel_id=1, source_target_pairs={{0,4},{2,6},{4,0},{6,2},{8,12},{10,14},{12,8},{14,10},{16,20},{18,... | collective-permute-start | bytes 786440 | tf_op jit(solution)/shard_map/ppermute | solution.py:218
  40.1 1.4 %collective-permute-start.7 = (bf16[32,4096]{1,0:T(8,128)(2,1)S(1)}, bf16[32,4096]{1,0:T(8,128)(2,1)S(1)}, u32[]{:S(2)}, u32[]{:S(2)}) collective-permute-start(bf16[32,4096]{1,0:T(8,128)(2,1)S(1)} %fusion.14), channel_id=1, source_target_pairs={{0,4},{2,6},{4,0},{6,2},{8,12},{10,14},{12,8},{14,10},{16,20},{18,... | collective-permute-start | bytes 786440 | tf_op jit(solution)/shard_map/ppermute | solution.py:218
  41.5 5.9 %collective-permute-done.18 = bf16[32,4096]{1,0:T(8,128)(2,1)S(1)} collective-permute-done((bf16[32,4096]{1,0:T(8,128)(2,1)S(1)}, bf16[32,4096]{1,0:T(8,128)(2,1)S(1)}, u32[]{:S(2)}, u32[]{:S(2)}) %collective-permute-start.18) | collective-permute-done | bytes 262176 | tf_op jit(solution)/shard_map/ppermute | solution.py:218
  47.6 2.3 %collective-permute-start.21 = (bf16[8,4096]{1,0:T(8,128)(2,1)S(1)}, bf16[8,4096]{1,0:T(8,128)(2,1)S(1)}, u32[]{:S(2)}, u32[]{:S(2)}) collective-permute-start(bf16[8,4096]{1,0:T(8,128)(2,1)S(1)} %get-tuple-element.33), channel_id=1, source_target_pairs={{0,24},{2,26},{4,28},{6,30},{8,0},{10,2},{12,4},{14,6},{16,8},{18,... | collective-permute-start | bytes 196616 | tf_op jit(solution)/shard_map/ppermute | solution.py:218
  50.3 1.2 %collective-permute-start.19 = (bf16[8,4096]{1,0:T(8,128)(2,1)S(1)}, bf16[8,4096]{1,0:T(8,128)(2,1)S(1)}, u32[]{:S(2)}, u32[]{:S(2)}) collective-permute-start(bf16[8,4096]{1,0:T(8,128)(2,1)S(1)} %get-tuple-element.32), channel_id=1, source_target_pairs={{0,8},{2,10},{4,12},{6,14},{8,16},{10,18},{12,20},{14,22},{16,24},... | collective-permute-start | bytes 196616 | tf_op jit(solution)/shard_map/ppermute | solution.py:218
  51.5 1.0 collective-permute-done.7
  52.8 1.2 %collective-permute-start.8 = (bf16[8,4096]{1,0:T(8,128)(2,1)S(1)}, bf16[8,4096]{1,0:T(8,128)(2,1)S(1)}, u32[]{:S(2)}, u32[]{:S(2)}) collective-permute-start(bf16[8,4096]{1,0:T(8,128)(2,1)S(1)} %get-tuple-element.37), channel_id=1, source_target_pairs={{0,8},{2,10},{4,12},{6,14},{8,16},{10,18},{12,20},{14,22},{16,24},... | collective-permute-start | bytes 196616 | tf_op jit(solution)/shard_map/ppermute | solution.py:218
  53.9 1.7 %collective-permute-start.9 = (bf16[8,4096]{1,0:T(8,128)(2,1)S(1)}, bf16[8,4096]{1,0:T(8,128)(2,1)S(1)}, u32[]{:S(2)}, u32[]{:S(2)}) collective-permute-start(bf16[8,4096]{1,0:T(8,128)(2,1)S(1)} %get-tuple-element.36), channel_id=1, source_target_pairs={{0,16},{2,18},{4,20},{6,22},{8,24},{10,26},{12,28},{14,30},{16,0},... | collective-permute-start | bytes 196616 | tf_op jit(solution)/shard_map/ppermute | solution.py:218
  55.7 1.8 %collective-permute-start.10 = (bf16[8,4096]{1,0:T(8,128)(2,1)S(1)}, bf16[8,4096]{1,0:T(8,128)(2,1)S(1)}, u32[]{:S(2)}, u32[]{:S(2)}) collective-permute-start(bf16[8,4096]{1,0:T(8,128)(2,1)S(1)} %get-tuple-element.35), channel_id=1, source_target_pairs={{0,24},{2,26},{4,28},{6,30},{8,0},{10,2},{12,4},{14,6},{16,8},{18,... | collective-permute-start | bytes 196616 | tf_op jit(solution)/shard_map/ppermute | solution.py:218
  57.9 1.2 %collective-permute-start.29 = (bf16[8,4096]{1,0:T(8,128)(2,1)S(1)}, bf16[8,4096]{1,0:T(8,128)(2,1)S(1)}, u32[]{:S(2)}, u32[]{:S(2)}) collective-permute-start(bf16[8,4096]{1,0:T(8,128)(2,1)S(1)} %get-tuple-element.26), channel_id=1, source_target_pairs={{0,16},{2,18},{4,20},{6,22},{8,24},{10,26},{12,28},{14,30},{16,0},... | collective-permute-start | bytes 196616 | tf_op jit(solution)/shard_map/ppermute | solution.py:218
  59.6 2.3 %collective-permute-start.28 = (bf16[8,4096]{1,0:T(8,128)(2,1)S(1)}, bf16[8,4096]{1,0:T(8,128)(2,1)S(1)}, u32[]{:S(2)}, u32[]{:S(2)}) collective-permute-start(bf16[8,4096]{1,0:T(8,128)(2,1)S(1)} %get-tuple-element.26), channel_id=1, source_target_pairs={{0,24},{2,26},{4,28},{6,30},{8,0},{10,2},{12,4},{14,6},{16,8},{18,... | collective-permute-start | bytes 196616 | tf_op jit(solution)/shard_map/ppermute | solution.py:218
  62.1 4.0 %collective-permute-start.24 = (bf16[8,4096]{1,0:T(8,128)(2,1)S(1)}, bf16[8,4096]{1,0:T(8,128)(2,1)S(1)}, u32[]{:S(2)}, u32[]{:S(2)}) collective-permute-start(bf16[8,4096]{1,0:T(8,128)(2,1)S(1)} %get-tuple-element.28), channel_id=1, source_target_pairs={{0,8},{2,10},{4,12},{6,14},{8,16},{10,18},{12,20},{14,22},{16,24},... | collective-permute-start | bytes 196616 | tf_op jit(solution)/shard_map/ppermute | solution.py:218
  66.1 2.0 %collective-permute-start.23 = (bf16[8,4096]{1,0:T(8,128)(2,1)S(1)}, bf16[8,4096]{1,0:T(8,128)(2,1)S(1)}, u32[]{:S(2)}, u32[]{:S(2)}) collective-permute-start(bf16[8,4096]{1,0:T(8,128)(2,1)S(1)} %get-tuple-element.28), channel_id=1, source_target_pairs={{0,16},{2,18},{4,20},{6,22},{8,24},{10,26},{12,28},{14,30},{16,0},... | collective-permute-start | bytes 196616 | tf_op jit(solution)/shard_map/ppermute | solution.py:218
  68.6 1.6 %collective-permute-start.31 = (bf16[32,4096]{1,0:T(8,128)(2,1)S(1)}, bf16[32,4096]{1,0:T(8,128)(2,1)S(1)}, u32[]{:S(2)}, u32[]{:S(2)}) collective-permute-start(bf16[32,4096]{1,0:T(8,128)(2,1)S(1)} %pad_maximum_fusion.3.refs_0_), channel_id=1, source_target_pairs={{0,4},{2,6},{4,0},{6,2},{8,12},{10,14},{12,8},{14,10},{16,20},{18,... | collective-permute-start | bytes 786440 | tf_op jit(solution)/shard_map/ppermute | solution.py:218
  70.6 2.1 %collective-permute-done.23 = bf16[8,4096]{1,0:T(8,128)(2,1)S(1)} collective-permute-done((bf16[8,4096]{1,0:T(8,128)(2,1)S(1)}, bf16[8,4096]{1,0:T(8,128)(2,1)S(1)}, u32[]{:S(2)}, u32[]{:S(2)}) %collective-permute-start.23) | collective-permute-done | bytes 65568 | tf_op jit(solution)/shard_map/ppermute | solution.py:218
  73.2 1.1 %collective-permute-start.25 = (bf16[32,4096]{1,0:T(8,128)(2,1)S(1)}, bf16[32,4096]{1,0:T(8,128)(2,1)S(1)}, u32[]{:S(2)}, u32[]{:S(2)}) collective-permute-start(bf16[32,4096]{1,0:T(8,128)(2,1)S(1)} %pad_maximum_fusion.2.refs_0_), channel_id=1, source_target_pairs={{0,4},{2,6},{4,0},{6,2},{8,12},{10,14},{12,8},{14,10},{16,20},{18,... | collective-permute-start | bytes 786440 | tf_op jit(solution)/shard_map/ppermute | solution.py:218
  74.3 2.9 %collective-permute-done.31.refs_1_ = bf16[32,4096]{1,0:T(8,128)(2,1)S(1)} collective-permute-done((bf16[32,4096]{1,0:T(8,128)(2,1)S(1)}, bf16[32,4096]{1,0:T(8,128)(2,1)S(1)}, u32[]{:S(2)}, u32[]{:S(2)}) %collective-permute-start.31) | collective-permute-done | bytes 262176 | tf_op jit(solution)/shard_map/ppermute | solution.py:218
  77.7 4.2 %collective-permute-done.25.refs_1_ = bf16[32,4096]{1,0:T(8,128)(2,1)S(1)} collective-permute-done((bf16[32,4096]{1,0:T(8,128)(2,1)S(1)}, bf16[32,4096]{1,0:T(8,128)(2,1)S(1)}, u32[]{:S(2)}, u32[]{:S(2)}) %collective-permute-start.25) | collective-permute-done | bytes 262176 | tf_op jit(solution)/shard_map/ppermute | solution.py:218
  81.9 6.7 %shard_map.52 = (f32[960,128]{1,0:T(8,128)S(1)}, f32[8,128]{1,0:T(8,128)S(1)}) custom-call(bf16[960,128]{1,0:T(8,128)(2,1)S(1)} %get-tuple-element.14.w_ref, bf16[32,4096]{1,0:T(8,128)(2,1)S(1)} %pad_maximum_fusion.3.refs_0_, bf16[32,4096]{1,0:T(8,128)(2,1)S(1)} %collective-permute-done.31.refs_1_, bf16[32,4096]{1,0:T(8,128)(2,1)S(1)} %collective-permute-done.32.refs_2_, ...), custom_call_target="tpu_custom_call" | custom-call | flops 2013265920 | bytes 7864320 | tf_op jit(solution)/shard_map/pallas_call | solution.py:167
  88.6 7.8 %shard_map.53 = bf16[976,128]{1,0:T(8,128)(2,1)S(1)} custom-call(bf16[960,128]{1,0:T(8,128)(2,1)S(1)} %get-tuple-element.14.w_ref, bf16[32,4096]{1,0:T(8,128)(2,1)S(1)} %pad_maximum_fusion.2.refs_0_, bf16[32,4096]{1,0:T(8,128)(2,1)S(1)} %collective-permute-done.25.refs_1_, bf16[32,4096]{1,0:T(8,128)(2,1)S(1)} %collective-permute-done.26.refs_2_, ...), custom_call_target="tpu_custom_call" | custom-call | flops 2013265920 | bytes 7864320 | tf_op jit(solution)/shard_map/pallas_call | solution.py:167
  98.1 6.9 %collective-permute-done.34 = bf16[976,128]{1,0:T(8,128)(2,1)S(1)} collective-permute-done((bf16[976,128]{1,0:T(8,128)(2,1)S(1)}, bf16[976,128]{1,0:T(8,128)(2,1)S(1)}, u32[]{:S(2)}, u32[]{:S(2)}) %collective-permute-start.34) | collective-permute-done | bytes 249888 | tf_op jit(solution)/shard_map/ppermute | solution.py:297
  (80 shorter events, 12.9 us)
Async XLA Ops:
  1.6 9.6 %collective-permute-start.13 = (bf16[8,4096]{1,0:T(8,128)(2,1)S(1)}, bf16[8,4096]{1,0:T(8,128)(2,1)S(1)}, u32[]{:S(2)}, u32[]{:S(2)}) collective-permute-start(bf16[8,4096]{1,0:T(8,128)(2,1)S(1)} %get-tuple-element.30), channel_id=1, source_target_pairs={{0,8},{2,10},{4,12},{6,14},{8,16},{10,18},{12,20},{14,22},{16,24},... | collective-permute-start | bytes 196616 | tf_op jit(solution)/shard_map/ppermute | solution.py:218
  4.7 9.3 %collective-permute-start.12 = (bf16[8,4096]{1,0:T(8,128)(2,1)S(1)}, bf16[8,4096]{1,0:T(8,128)(2,1)S(1)}, u32[]{:S(2)}, u32[]{:S(2)}) collective-permute-start(bf16[8,4096]{1,0:T(8,128)(2,1)S(1)} %get-tuple-element.30), channel_id=1, source_target_pairs={{0,16},{2,18},{4,20},{6,22},{8,24},{10,26},{12,28},{14,30},{16,0},... | collective-permute-start | bytes 196616 | tf_op jit(solution)/shard_map/ppermute | solution.py:218
  7.3 6.7 %collective-permute-start.11 = (bf16[8,4096]{1,0:T(8,128)(2,1)S(1)}, bf16[8,4096]{1,0:T(8,128)(2,1)S(1)}, u32[]{:S(2)}, u32[]{:S(2)}) collective-permute-start(bf16[8,4096]{1,0:T(8,128)(2,1)S(1)} %get-tuple-element.30), channel_id=1, source_target_pairs={{0,24},{2,26},{4,28},{6,30},{8,0},{10,2},{12,4},{14,6},{16,8},{18,... | collective-permute-start | bytes 196616 | tf_op jit(solution)/shard_map/ppermute | solution.py:218
  10.1 6.4 %collective-permute-start.2 = (bf16[8,4224]{1,0:T(8,128)(2,1)S(1)}, bf16[8,4224]{1,0:T(8,128)(2,1)S(1)}, u32[]{:S(2)}, u32[]{:S(2)}) collective-permute-start(bf16[8,4224]{1,0:T(8,128)(2,1)S(1)} %pad_maximum_fusion.5), channel_id=1, source_target_pairs={{0,8},{2,10},{4,12},{6,14},{8,16},{10,18},{12,20},{14,22},{16,24},... | collective-permute-start | bytes 202760 | tf_op jit(solution)/shard_map/ppermute | solution.py:218
  10.9 7.3 %collective-permute-start.1 = (bf16[8,4224]{1,0:T(8,128)(2,1)S(1)}, bf16[8,4224]{1,0:T(8,128)(2,1)S(1)}, u32[]{:S(2)}, u32[]{:S(2)}) collective-permute-start(bf16[8,4224]{1,0:T(8,128)(2,1)S(1)} %pad_maximum_fusion.5), channel_id=1, source_target_pairs={{0,16},{2,18},{4,20},{6,22},{8,24},{10,26},{12,28},{14,30},{16,0},... | collective-permute-start | bytes 202760 | tf_op jit(solution)/shard_map/ppermute | solution.py:218
  11.2 6.9 %collective-permute-start = (bf16[8,4224]{1,0:T(8,128)(2,1)S(1)}, bf16[8,4224]{1,0:T(8,128)(2,1)S(1)}, u32[]{:S(2)}, u32[]{:S(2)}) collective-permute-start(bf16[8,4224]{1,0:T(8,128)(2,1)S(1)} %pad_maximum_fusion.5), channel_id=1, source_target_pairs={{0,24},{2,26},{4,28},{6,30},{8,0},{10,2},{12,4},{14,6},{16,8},{18,... | collective-permute-start | bytes 202760 | tf_op jit(solution)/shard_map/ppermute | solution.py:218
  14.1 9.2 %collective-permute-start.14 = (bf16[32,4096]{1,0:T(8,128)(2,1)S(1)}, bf16[32,4096]{1,0:T(8,128)(2,1)S(1)}, u32[]{:S(2)}, u32[]{:S(2)}) collective-permute-start(bf16[32,4096]{1,0:T(8,128)(2,1)S(1)} %pad_maximum_fusion.1.refs_0_), channel_id=1, source_target_pairs={{0,4},{2,6},{4,0},{6,2},{8,12},{10,14},{12,8},{14,10},{16,20},{18,... | collective-permute-start | bytes 786440 | tf_op jit(solution)/shard_map/ppermute | solution.py:218
  18.2 8.4 %collective-permute-start.3 = (bf16[32,4224]{1,0:T(8,128)(2,1)S(1)}, bf16[32,4224]{1,0:T(8,128)(2,1)S(1)}, u32[]{:S(2)}, u32[]{:S(2)}) collective-permute-start(bf16[32,4224]{1,0:T(8,128)(2,1)S(1)} %pad_maximum_fusion.refs_0_), channel_id=1, source_target_pairs={{0,4},{2,6},{4,0},{6,2},{8,12},{10,14},{12,8},{14,10},{16,20},{18,... | collective-permute-start | bytes 811016 | tf_op jit(solution)/shard_map/ppermute | solution.py:218
  19.7 6.8 %collective-permute-start.4 = (bf16[32,4224]{1,0:T(8,128)(2,1)S(1)}, bf16[32,4224]{1,0:T(8,128)(2,1)S(1)}, u32[]{:S(2)}, u32[]{:S(2)}) collective-permute-start(bf16[32,4224]{1,0:T(8,128)(2,1)S(1)} %pad_maximum_fusion.refs_0_), channel_id=1, source_target_pairs={{0,2},{2,0},{4,6},{6,4},{8,10},{10,8},{12,14},{14,12},{16,18},{18,... | collective-permute-start | bytes 811016 | tf_op jit(solution)/shard_map/ppermute | solution.py:218
  19.7 6.8 %collective-permute-start.15 = (bf16[32,4096]{1,0:T(8,128)(2,1)S(1)}, bf16[32,4096]{1,0:T(8,128)(2,1)S(1)}, u32[]{:S(2)}, u32[]{:S(2)}) collective-permute-start(bf16[32,4096]{1,0:T(8,128)(2,1)S(1)} %pad_maximum_fusion.1.refs_0_), channel_id=1, source_target_pairs={{0,2},{2,0},{4,6},{6,4},{8,10},{10,8},{12,14},{14,12},{16,18},{18,... | collective-permute-start | bytes 786440 | tf_op jit(solution)/shard_map/ppermute | solution.py:218
  26.6 5.8 %collective-permute-start.5 = (bf16[32,4224]{1,0:T(8,128)(2,1)S(1)}, bf16[32,4224]{1,0:T(8,128)(2,1)S(1)}, u32[]{:S(2)}, u32[]{:S(2)}) collective-permute-start(bf16[32,4224]{1,0:T(8,128)(2,1)S(1)} %collective-permute-done.3.refs_1_), channel_id=1, source_target_pairs={{0,2},{2,0},{4,6},{6,4},{8,10},{10,8},{12,14},{14,12},{16,18},{18,... | collective-permute-start | bytes 811016 | tf_op jit(solution)/shard_map/ppermute | solution.py:218
  31.8 5.9 %collective-permute-start.17 = (bf16[64,4096]{1,0:T(8,128)(2,1)S(1)}, bf16[64,4096]{1,0:T(8,128)(2,1)S(1)}, u32[]{:S(2)}, u32[]{:S(2)}) collective-permute-start(bf16[64,4096]{1,0:T(8,128)(2,1)S(1)} %get-tuple-element.20), channel_id=1, source_target_pairs={{0,2},{2,0},{4,6},{6,4},{8,10},{10,8},{12,14},{14,12},{16,18},{18,... | collective-permute-start | bytes 1572872 | tf_op jit(solution)/shard_map/ppermute | solution.py:218
  38.1 9.2 %collective-permute-start.18 = (bf16[32,4096]{1,0:T(8,128)(2,1)S(1)}, bf16[32,4096]{1,0:T(8,128)(2,1)S(1)}, u32[]{:S(2)}, u32[]{:S(2)}) collective-permute-start(bf16[32,4096]{1,0:T(8,128)(2,1)S(1)} %fusion.15), channel_id=1, source_target_pairs={{0,4},{2,6},{4,0},{6,2},{8,12},{10,14},{12,8},{14,10},{16,20},{18,... | collective-permute-start | bytes 786440 | tf_op jit(solution)/shard_map/ppermute | solution.py:218
  40.1 12.4 %collective-permute-start.7 = (bf16[32,4096]{1,0:T(8,128)(2,1)S(1)}, bf16[32,4096]{1,0:T(8,128)(2,1)S(1)}, u32[]{:S(2)}, u32[]{:S(2)}) collective-permute-start(bf16[32,4096]{1,0:T(8,128)(2,1)S(1)} %fusion.14), channel_id=1, source_target_pairs={{0,4},{2,6},{4,0},{6,2},{8,12},{10,14},{12,8},{14,10},{16,20},{18,... | collective-permute-start | bytes 786440 | tf_op jit(solution)/shard_map/ppermute | solution.py:218
  47.6 8.0 %collective-permute-start.21 = (bf16[8,4096]{1,0:T(8,128)(2,1)S(1)}, bf16[8,4096]{1,0:T(8,128)(2,1)S(1)}, u32[]{:S(2)}, u32[]{:S(2)}) collective-permute-start(bf16[8,4096]{1,0:T(8,128)(2,1)S(1)} %get-tuple-element.33), channel_id=1, source_target_pairs={{0,24},{2,26},{4,28},{6,30},{8,0},{10,2},{12,4},{14,6},{16,8},{18,... | collective-permute-start | bytes 196616 | tf_op jit(solution)/shard_map/ppermute | solution.py:218
  50.0 7.6 %collective-permute-start.20 = (bf16[8,4096]{1,0:T(8,128)(2,1)S(1)}, bf16[8,4096]{1,0:T(8,128)(2,1)S(1)}, u32[]{:S(2)}, u32[]{:S(2)}) collective-permute-start(bf16[8,4096]{1,0:T(8,128)(2,1)S(1)} %get-tuple-element.34), channel_id=1, source_target_pairs={{0,16},{2,18},{4,20},{6,22},{8,24},{10,26},{12,28},{14,30},{16,0},... | collective-permute-start | bytes 196616 | tf_op jit(solution)/shard_map/ppermute | solution.py:218
  50.3 7.2 %collective-permute-start.19 = (bf16[8,4096]{1,0:T(8,128)(2,1)S(1)}, bf16[8,4096]{1,0:T(8,128)(2,1)S(1)}, u32[]{:S(2)}, u32[]{:S(2)}) collective-permute-start(bf16[8,4096]{1,0:T(8,128)(2,1)S(1)} %get-tuple-element.32), channel_id=1, source_target_pairs={{0,8},{2,10},{4,12},{6,14},{8,16},{10,18},{12,20},{14,22},{16,24},... | collective-permute-start | bytes 196616 | tf_op jit(solution)/shard_map/ppermute | solution.py:218
  52.8 6.9 %collective-permute-start.8 = (bf16[8,4096]{1,0:T(8,128)(2,1)S(1)}, bf16[8,4096]{1,0:T(8,128)(2,1)S(1)}, u32[]{:S(2)}, u32[]{:S(2)}) collective-permute-start(bf16[8,4096]{1,0:T(8,128)(2,1)S(1)} %get-tuple-element.37), channel_id=1, source_target_pairs={{0,8},{2,10},{4,12},{6,14},{8,16},{10,18},{12,20},{14,22},{16,24},... | collective-permute-start | bytes 196616 | tf_op jit(solution)/shard_map/ppermute | solution.py:218
  53.9 8.0 %collective-permute-start.9 = (bf16[8,4096]{1,0:T(8,128)(2,1)S(1)}, bf16[8,4096]{1,0:T(8,128)(2,1)S(1)}, u32[]{:S(2)}, u32[]{:S(2)}) collective-permute-start(bf16[8,4096]{1,0:T(8,128)(2,1)S(1)} %get-tuple-element.36), channel_id=1, source_target_pairs={{0,16},{2,18},{4,20},{6,22},{8,24},{10,26},{12,28},{14,30},{16,0},... | collective-permute-start | bytes 196616 | tf_op jit(solution)/shard_map/ppermute | solution.py:218
  55.7 6.3 %collective-permute-start.10 = (bf16[8,4096]{1,0:T(8,128)(2,1)S(1)}, bf16[8,4096]{1,0:T(8,128)(2,1)S(1)}, u32[]{:S(2)}, u32[]{:S(2)}) collective-permute-start(bf16[8,4096]{1,0:T(8,128)(2,1)S(1)} %get-tuple-element.35), channel_id=1, source_target_pairs={{0,24},{2,26},{4,28},{6,30},{8,0},{10,2},{12,4},{14,6},{16,8},{18,... | collective-permute-start | bytes 196616 | tf_op jit(solution)/shard_map/ppermute | solution.py:218
  57.6 10.5 %collective-permute-start.30 = (bf16[8,4096]{1,0:T(8,128)(2,1)S(1)}, bf16[8,4096]{1,0:T(8,128)(2,1)S(1)}, u32[]{:S(2)}, u32[]{:S(2)}) collective-permute-start(bf16[8,4096]{1,0:T(8,128)(2,1)S(1)} %get-tuple-element.26), channel_id=1, source_target_pairs={{0,8},{2,10},{4,12},{6,14},{8,16},{10,18},{12,20},{14,22},{16,24},... | collective-permute-start | bytes 196616 | tf_op jit(solution)/shard_map/ppermute | solution.py:218
  57.9 10.7 %collective-permute-start.29 = (bf16[8,4096]{1,0:T(8,128)(2,1)S(1)}, bf16[8,4096]{1,0:T(8,128)(2,1)S(1)}, u32[]{:S(2)}, u32[]{:S(2)}) collective-permute-start(bf16[8,4096]{1,0:T(8,128)(2,1)S(1)} %get-tuple-element.26), channel_id=1, source_target_pairs={{0,16},{2,18},{4,20},{6,22},{8,24},{10,26},{12,28},{14,30},{16,0},... | collective-permute-start | bytes 196616 | tf_op jit(solution)/shard_map/ppermute | solution.py:218
  59.6 9.0 %collective-permute-start.28 = (bf16[8,4096]{1,0:T(8,128)(2,1)S(1)}, bf16[8,4096]{1,0:T(8,128)(2,1)S(1)}, u32[]{:S(2)}, u32[]{:S(2)}) collective-permute-start(bf16[8,4096]{1,0:T(8,128)(2,1)S(1)} %get-tuple-element.26), channel_id=1, source_target_pairs={{0,24},{2,26},{4,28},{6,30},{8,0},{10,2},{12,4},{14,6},{16,8},{18,... | collective-permute-start | bytes 196616 | tf_op jit(solution)/shard_map/ppermute | solution.py:218
  62.1 8.4 %collective-permute-start.24 = (bf16[8,4096]{1,0:T(8,128)(2,1)S(1)}, bf16[8,4096]{1,0:T(8,128)(2,1)S(1)}, u32[]{:S(2)}, u32[]{:S(2)}) collective-permute-start(bf16[8,4096]{1,0:T(8,128)(2,1)S(1)} %get-tuple-element.28), channel_id=1, source_target_pairs={{0,8},{2,10},{4,12},{6,14},{8,16},{10,18},{12,20},{14,22},{16,24},... | collective-permute-start | bytes 196616 | tf_op jit(solution)/shard_map/ppermute | solution.py:218
  66.1 6.5 %collective-permute-start.23 = (bf16[8,4096]{1,0:T(8,128)(2,1)S(1)}, bf16[8,4096]{1,0:T(8,128)(2,1)S(1)}, u32[]{:S(2)}, u32[]{:S(2)}) collective-permute-start(bf16[8,4096]{1,0:T(8,128)(2,1)S(1)} %get-tuple-element.28), channel_id=1, source_target_pairs={{0,16},{2,18},{4,20},{6,22},{8,24},{10,26},{12,28},{14,30},{16,0},... | collective-permute-start | bytes 196616 | tf_op jit(solution)/shard_map/ppermute | solution.py:218
  68.1 5.1 %collective-permute-start.22 = (bf16[8,4096]{1,0:T(8,128)(2,1)S(1)}, bf16[8,4096]{1,0:T(8,128)(2,1)S(1)}, u32[]{:S(2)}, u32[]{:S(2)}) collective-permute-start(bf16[8,4096]{1,0:T(8,128)(2,1)S(1)} %get-tuple-element.28), channel_id=1, source_target_pairs={{0,24},{2,26},{4,28},{6,30},{8,0},{10,2},{12,4},{14,6},{16,8},{18,... | collective-permute-start | bytes 196616 | tf_op jit(solution)/shard_map/ppermute | solution.py:218
  68.6 8.6 %collective-permute-start.31 = (bf16[32,4096]{1,0:T(8,128)(2,1)S(1)}, bf16[32,4096]{1,0:T(8,128)(2,1)S(1)}, u32[]{:S(2)}, u32[]{:S(2)}) collective-permute-start(bf16[32,4096]{1,0:T(8,128)(2,1)S(1)} %pad_maximum_fusion.3.refs_0_), channel_id=1, source_target_pairs={{0,4},{2,6},{4,0},{6,2},{8,12},{10,14},{12,8},{14,10},{16,20},{18,... | collective-permute-start | bytes 786440 | tf_op jit(solution)/shard_map/ppermute | solution.py:218
  73.2 8.7 %collective-permute-start.25 = (bf16[32,4096]{1,0:T(8,128)(2,1)S(1)}, bf16[32,4096]{1,0:T(8,128)(2,1)S(1)}, u32[]{:S(2)}, u32[]{:S(2)}) collective-permute-start(bf16[32,4096]{1,0:T(8,128)(2,1)S(1)} %pad_maximum_fusion.2.refs_0_), channel_id=1, source_target_pairs={{0,4},{2,6},{4,0},{6,2},{8,12},{10,14},{12,8},{14,10},{16,20},{18,... | collective-permute-start | bytes 786440 | tf_op jit(solution)/shard_map/ppermute | solution.py:218
  74.3 7.5 %collective-permute-start.32 = (bf16[32,4096]{1,0:T(8,128)(2,1)S(1)}, bf16[32,4096]{1,0:T(8,128)(2,1)S(1)}, u32[]{:S(2)}, u32[]{:S(2)}) collective-permute-start(bf16[32,4096]{1,0:T(8,128)(2,1)S(1)} %pad_maximum_fusion.3.refs_0_), channel_id=1, source_target_pairs={{0,2},{2,0},{4,6},{6,4},{8,10},{10,8},{12,14},{14,12},{16,18},{18,... | collective-permute-start | bytes 786440 | tf_op jit(solution)/shard_map/ppermute | solution.py:218
  77.2 11.4 %collective-permute-start.26 = (bf16[32,4096]{1,0:T(8,128)(2,1)S(1)}, bf16[32,4096]{1,0:T(8,128)(2,1)S(1)}, u32[]{:S(2)}, u32[]{:S(2)}) collective-permute-start(bf16[32,4096]{1,0:T(8,128)(2,1)S(1)} %pad_maximum_fusion.2.refs_0_), channel_id=1, source_target_pairs={{0,2},{2,0},{4,6},{6,4},{8,10},{10,8},{12,14},{14,12},{16,18},{18,... | collective-permute-start | bytes 786440 | tf_op jit(solution)/shard_map/ppermute | solution.py:218
  81.9 6.8 %collective-permute-start.27 = (bf16[32,4096]{1,0:T(8,128)(2,1)S(1)}, bf16[32,4096]{1,0:T(8,128)(2,1)S(1)}, u32[]{:S(2)}, u32[]{:S(2)}) collective-permute-start(bf16[32,4096]{1,0:T(8,128)(2,1)S(1)} %collective-permute-done.25.refs_1_), channel_id=1, source_target_pairs={{0,2},{2,0},{4,6},{6,4},{8,10},{10,8},{12,14},{14,12},{16,18},{18,... | collective-permute-start | bytes 786440 | tf_op jit(solution)/shard_map/ppermute | solution.py:218
  96.4 8.5 %collective-permute-start.34 = (bf16[976,128]{1,0:T(8,128)(2,1)S(1)}, bf16[976,128]{1,0:T(8,128)(2,1)S(1)}, u32[]{:S(2)}, u32[]{:S(2)}) collective-permute-start(bf16[976,128]{1,0:T(8,128)(2,1)S(1)} %shard_map.53), channel_id=1, source_target_pairs={{0,1},{1,0},{2,3},{3,2},{4,5},{5,4},{6,7},{7,6},{8,9},{9,8},{10,11... | collective-permute-start | bytes 749576 | tf_op jit(solution)/shard_map/ppermute | solution.py:297
  (6 other events, 68.6 us)

commit v3 on v2

--- a/solution.py
+++ b/solution.py
@@ -115,36 +115,34 @@
 def w_kernel(w_ref, *refs, count, start, first, last):
     pieces, counts_ref = refs[:count], refs[count]
     if last:
-        running, pick_ref = refs[count + 1 : -6], refs[-6]
-        out_ref, buffer_ref, sems, total_ref, sum_ref = refs[-5:]
+        running, pick_ref = refs[count + 1 : -5], refs[-5]
+        out_ref, buffer_ref, sems, total_ref = refs[-4:]
     else:
-        running = refs[count + 1 : -4]
-        total_ref, sum_ref, buffer_ref, sems = refs[-4:]
+        running = refs[count + 1 : -3]
+        total_ref, buffer_ref, sems = refs[-3:]
     copies = streamed(counts_ref, buffer_ref, sems, start, W_SHARES)
+    cells = w_ref.shape[0]
     across = (((1,), (1,)), ((), ()))
     if first:
         total_ref[...] = jnp.zeros_like(total_ref)
-        sum_ref[...] = jnp.zeros_like(sum_ref)
     else:
         total_ref[...] = running[0][...]
-        sum_ref[...] = running[1][...]
     for copy, span in copies:
         h_tile = jnp.concatenate([piece[:, span] for piece in pieces], axis=0)
-        ones = jnp.ones((sum_ref.shape[0], h_tile.shape[1]), BF16)
+        ones = jnp.ones((16, h_tile.shape[1]), BF16)
         copy.wait()
         quotient = quotient_of(w_ref, h_tile, buffer_ref[:, span])
+        quotient = jnp.concatenate([quotient, ones], axis=0)
         total_ref[...] += lax.dot_general(quotient, h_tile, across, preferred_element_type=F32)
-        sum_ref[...] += lax.dot_general(ones, h_tile, across, preferred_element_type=F32)
 
     if last:
-        cells = total_ref.shape[0]
         exact = lax.Precision.HIGHEST
-        pick = pick_ref[...]
-        total = jnp.dot(total_ref[...], pick, precision=exact, preferred_element_type=F32)
-        sums = jnp.dot(sum_ref[...], pick, precision=exact, preferred_element_type=F32)
-        high, middle, low = parts_of(sums[:1])
-        out_ref[:cells, :] = encode(total, W_KNEE)
-        row = lax.broadcasted_iota(jnp.int32, (16, sums.shape[1]), 0)
+        total = jnp.dot(
+            total_ref[...], pick_ref[...], precision=exact, preferred_element_type=F32
+        )
+        high, middle, low = parts_of(total[cells : cells + 1])
+        out_ref[:cells, :] = encode(total[:cells], W_KNEE)
+        row = lax.broadcasted_iota(jnp.int32, (16, total.shape[1]), 0)
         tail = jnp.where(row == 0, high, jnp.where(row == 1, middle, low))
         out_ref[cells:, :] = jnp.where(row < 3, tail, 0.0).astype(BF16)
 
@@ -188,14 +186,14 @@
 def w_partial(start, w_rel, pieces, counts, width, running, pick):
     cells, rank = w_rel.shape
     last = pick is not None
-    sums = [((cells, rank), F32), ((8, rank), F32)]
-    outs = [((cells + 16, rank), BF16)] if last else sums
+    total = [((cells + 16, rank), F32)]
+    outs = [((cells + 16, rank), BF16)] if last else total
     kernel = functools.partial(
         w_kernel, count=len(pieces), start=start, first=not running, last=last
     )
     more = list(running) + ([pick] if last else [])
-    out = call(kernel, [w_rel, *pieces], counts, more, outs, width, sums if last else ())
-    return out[0] if last else out
+    scratch = total if last else ()
+    return call(kernel, [w_rel, *pieces], counts, more, outs, width, scratch)
 
 
 def per_device(counts, w_factor, h_factor, *, devices, gene_devices):
@@ -246,7 +244,8 @@
             column.append(shift_z(own, along - s))
         column = jnp.concatenate(column, 0)
         mine = [column] + [shift_x(column, across - s) for s in range(1, across)]
-        return mine + [swap(piece) for piece in mine]
+        swapped = [swap(column)]
+        return mine + swapped + [swap(piece) for piece in mine[1:]]
 
     def reduce(keep, other):
         total = keep + decode_square(swap(other), H_KNEE)
@@ -266,7 +265,10 @@
 
     gathered = []
     for i in range(chunks):
-        own = h_factor[:, starts[i] : starts[i] + widths[i]].astype(BF16)
+        source = h_factor
+        if i == chunks - 1:
+            source, sums = lax.optimization_barrier((source, sums))
+        own = source[:, starts[i] : starts[i] + widths[i]].astype(BF16)
         if i == chunks - 1:
             own = jnp.concatenate([own, sums], 1)
         gathered.append(gather(own))
@@ -293,6 +295,7 @@
         running = w_partial(
             starts[i], w_rel, again[i], counts, widths[i], running, pick if last else None
         )
+    running = running[0]
     if gene_devices == 2:
         got = lax.ppermute(running, "gene", [(0, 1), (1, 0)])
         totals = sum(
@@ -304,8 +307,10 @@
         kept, got = lax.optimization_barrier((kept, got))
         w_updated = w_factor * (kept + decode(got[:cells], W_KNEE)) * (1.0 / totals)
     else:
-        numerator, h_totals = lax.psum(running, "gene")
-        ratio = jnp.dot(numerator / h_totals[:1], pick, precision=lax.Precision.HIGHEST)
+        total = lax.psum(running, "gene")
+        ratio = jnp.dot(
+            total[:cells] / total[cells : cells + 1], pick, precision=lax.Precision.HIGHEST
+        )
         w_updated = w_factor * ratio
     return (w_updated, h_updated)
 

time: 106 us -> 106 us (level)
  waiting for transfers between devices: 33.2 us -> 31 us
  starting transfers between devices: 40.9 us -> 42.2 us
    ppermute x34, waiting for transfers between devices: 26.4 us -> 24.9 us  [send(): return lax.ppermute(value, 'cell', [(i, route(i)) for i in range(devices)])]
  transfers between devices with their start and end apart: 35 -> 35, of which waited for: 13 -> 11; matrix products, arithmetic and copies ran while one was open for 3% -> 3% of each run, Pallas kernels for 16% -> 16%
where the time goes in v3:
time: 106 us; the launch traced here: 105 us
  starting transfers between devices  42.2 us (40%)
  waiting for transfers between devices  31 us (29%)
  Pallas kernels  24.7 us (23%)
  other arithmetic  3.6 us (3%)
  local copies, waits for them, and re-layouts  2.98 us (3%)
    ppermute x34, starting transfers between devices, send(): return lax.ppermute(value, 'cell', [(i, route(i)) for i in range(devices)])  40.6 us
    ppermute x34, waiting for transfers between devices, send(): return lax.ppermute(value, 'cell', [(i, route(i)) for i in range(devices)])  24.9 us
    pallas_call x4, Pallas kernels, call(): pl.pallas_call(kernel, in_specs=[local] * len(held_args) + [pl.BlockSpec(...  24.4 us
    ppermute x1, waiting for transfers between devices, per_device(): got = lax.ppermute(running, 'gene', [(0, 1), (1, 0)])  6.08 us
  transfers between devices with their start and end apart: 35, of which 11 were waited for; matrix products, arithmetic and copies ran while one was open for 3% of the time, Pallas kernels for 16%

profile of v3, /device:TPU:0, one launch (start us, length us, event | category | flops | bytes accessed | tf_op | source)
XLA Modules:
  0.0 105.3 jit_solution(10352253540549014642)
XLA Ops:
  1.5 3.1 %collective-permute-start.13 = (bf16[8,4096]{1,0:T(8,128)(2,1)S(1)}, bf16[8,4096]{1,0:T(8,128)(2,1)S(1)}, u32[]{:S(2)}, u32[]{:S(2)}) collective-permute-start(bf16[8,4096]{1,0:T(8,128)(2,1)S(1)} %slice.199), channel_id=1, source_target_pairs={{0,8},{2,10},{4,12},{6,14},{8,16},{10,18},{12,20},{14,22},{16,24},... | collective-permute-start | bytes 196616 | tf_op jit(solution)/shard_map/ppermute | solution.py:216
  4.6 2.6 %collective-permute-start.12 = (bf16[8,4096]{1,0:T(8,128)(2,1)S(1)}, bf16[8,4096]{1,0:T(8,128)(2,1)S(1)}, u32[]{:S(2)}, u32[]{:S(2)}) collective-permute-start(bf16[8,4096]{1,0:T(8,128)(2,1)S(1)} %slice.199), channel_id=1, source_target_pairs={{0,16},{2,18},{4,20},{6,22},{8,24},{10,26},{12,28},{14,30},{16,0},... | collective-permute-start | bytes 196616 | tf_op jit(solution)/shard_map/ppermute | solution.py:216
  7.2 1.3 %collective-permute-start.11 = (bf16[8,4096]{1,0:T(8,128)(2,1)S(1)}, bf16[8,4096]{1,0:T(8,128)(2,1)S(1)}, u32[]{:S(2)}, u32[]{:S(2)}) collective-permute-start(bf16[8,4096]{1,0:T(8,128)(2,1)S(1)} %slice.199), channel_id=1, source_target_pairs={{0,24},{2,26},{4,28},{6,30},{8,0},{10,2},{12,4},{14,6},{16,8},{18,... | collective-permute-start | bytes 196616 | tf_op jit(solution)/shard_map/ppermute | solution.py:216
  12.0 2.8 %collective-permute-start = (bf16[8,4224]{1,0:T(8,128)(2,1)S(1)}, bf16[8,4224]{1,0:T(8,128)(2,1)S(1)}, u32[]{:S(2)}, u32[]{:S(2)}) collective-permute-start(bf16[8,4224]{1,0:T(8,128)(2,1)S(1)} %pad_maximum_fusion.5), channel_id=1, source_target_pairs={{0,24},{2,26},{4,28},{6,30},{8,0},{10,2},{12,4},{14,6},{16,8},{18,... | collective-permute-start | bytes 202760 | tf_op jit(solution)/shard_map/ppermute | solution.py:216
  14.8 1.6 %collective-permute-start.14 = (bf16[32,4096]{1,0:T(8,128)(2,1)S(1)}, bf16[32,4096]{1,0:T(8,128)(2,1)S(1)}, u32[]{:S(2)}, u32[]{:S(2)}) collective-permute-start(bf16[32,4096]{1,0:T(8,128)(2,1)S(1)} %pad_maximum_fusion.1.refs_0_), channel_id=1, source_target_pairs={{0,4},{2,6},{4,0},{6,2},{8,12},{10,14},{12,8},{14,10},{16,20},{18,... | collective-permute-start | bytes 786440 | tf_op jit(solution)/shard_map/ppermute | solution.py:216
  17.3 1.6 %collective-permute-done.1 = bf16[8,4224]{1,0:T(8,128)(2,1)S(1)} collective-permute-done((bf16[8,4224]{1,0:T(8,128)(2,1)S(1)}, bf16[8,4224]{1,0:T(8,128)(2,1)S(1)}, u32[]{:S(2)}, u32[]{:S(2)}) %collective-permute-start.1) | collective-permute-done | bytes 67616 | tf_op jit(solution)/shard_map/ppermute | solution.py:216
  19.0 1.6 %collective-permute-start.3 = (bf16[32,4224]{1,0:T(8,128)(2,1)S(1)}, bf16[32,4224]{1,0:T(8,128)(2,1)S(1)}, u32[]{:S(2)}, u32[]{:S(2)}) collective-permute-start(bf16[32,4224]{1,0:T(8,128)(2,1)S(1)} %pad_maximum_fusion.refs_0_), channel_id=1, source_target_pairs={{0,4},{2,6},{4,0},{6,2},{8,12},{10,14},{12,8},{14,10},{16,20},{18,... | collective-permute-start | bytes 811016 | tf_op jit(solution)/shard_map/ppermute | solution.py:216
  21.0 3.1 %collective-permute-done.14.refs_1_ = bf16[32,4096]{1,0:T(8,128)(2,1)S(1)} collective-permute-done((bf16[32,4096]{1,0:T(8,128)(2,1)S(1)}, bf16[32,4096]{1,0:T(8,128)(2,1)S(1)}, u32[]{:S(2)}, u32[]{:S(2)}) %collective-permute-start.14) | collective-permute-done | bytes 262176 | tf_op jit(solution)/shard_map/ppermute | solution.py:216
  24.1 3.3 %collective-permute-done.3.refs_1_ = bf16[32,4224]{1,0:T(8,128)(2,1)S(1)} collective-permute-done((bf16[32,4224]{1,0:T(8,128)(2,1)S(1)}, bf16[32,4224]{1,0:T(8,128)(2,1)S(1)}, u32[]{:S(2)}, u32[]{:S(2)}) %collective-permute-start.3) | collective-permute-done | bytes 270368 | tf_op jit(solution)/shard_map/ppermute | solution.py:216
  27.4 5.2 %shard_map.51 = (f32[64,4096]{1,0:T(8,128)S(1)}, bf16[64,4096]{1,0:T(8,128)(2,1)S(1)}) custom-call(bf16[128,960]{1,0:T(8,128)(2,1)S(1)} %get-tuple-element.15.wt_ref, bf16[960,128]{1,0:T(8,128)(2,1)S(1)} %get-tuple-element.14.w_ref, bf16[32,4096]{1,0:T(8,128)(2,1)S(1)} %pad_maximum_fusion.1.refs_0_, bf16[32,4096]{1,0:T(8,128)(2,1)S(1)} %collective-permute-done.14.refs_1_, ...), custom_call_target="tpu_custom_call" | custom-call | flops 15099494400 | bytes 7864320 | tf_op jit(solution)/shard_map/pallas_call | solution.py:165
  33.1 5.2 %shard_map.50 = (f32[64,4096]{1,0:T(8,128)S(1)}, bf16[64,4096]{1,0:T(8,128)(2,1)S(1)}) custom-call(bf16[128,960]{1,0:T(8,128)(2,1)S(1)} %get-tuple-element.15.wt_ref, bf16[960,128]{1,0:T(8,128)(2,1)S(1)} %get-tuple-element.14.w_ref, bf16[32,4224]{1,0:T(8,128)(2,1)S(1)} %pad_maximum_fusion.refs_0_, bf16[32,4224]{1,0:T(8,128)(2,1)S(1)} %collective-permute-done.3.refs_1_, ...), custom_call_target="tpu_custom_call" | custom-call | flops 15099494400 | bytes 7864320 | tf_op jit(solution)/shard_map/pallas_call | solution.py:165
  38.9 1.5 %collective-permute-start.18 = (bf16[32,4096]{1,0:T(8,128)(2,1)S(1)}, bf16[32,4096]{1,0:T(8,128)(2,1)S(1)}, u32[]{:S(2)}, u32[]{:S(2)}) collective-permute-start(bf16[32,4096]{1,0:T(8,128)(2,1)S(1)} %fusion.15), channel_id=1, source_target_pairs={{0,4},{2,6},{4,0},{6,2},{8,12},{10,14},{12,8},{14,10},{16,20},{18,... | collective-permute-start | bytes 786440 | tf_op jit(solution)/shard_map/ppermute | solution.py:216
  40.9 1.4 %collective-permute-start.7 = (bf16[32,4096]{1,0:T(8,128)(2,1)S(1)}, bf16[32,4096]{1,0:T(8,128)(2,1)S(1)}, u32[]{:S(2)}, u32[]{:S(2)}) collective-permute-start(bf16[32,4096]{1,0:T(8,128)(2,1)S(1)} %fusion.14), channel_id=1, source_target_pairs={{0,4},{2,6},{4,0},{6,2},{8,12},{10,14},{12,8},{14,10},{16,20},{18,... | collective-permute-start | bytes 786440 | tf_op jit(solution)/shard_map/ppermute | solution.py:216
  42.2 5.9 %collective-permute-done.18 = bf16[32,4096]{1,0:T(8,128)(2,1)S(1)} collective-permute-done((bf16[32,4096]{1,0:T(8,128)(2,1)S(1)}, bf16[32,4096]{1,0:T(8,128)(2,1)S(1)}, u32[]{:S(2)}, u32[]{:S(2)}) %collective-permute-start.18) | collective-permute-done | bytes 262176 | tf_op jit(solution)/shard_map/ppermute | solution.py:216
  49.4 1.1 %collective-permute-start.20 = (bf16[8,4096]{1,0:T(8,128)(2,1)S(1)}, bf16[8,4096]{1,0:T(8,128)(2,1)S(1)}, u32[]{:S(2)}, u32[]{:S(2)}) collective-permute-start(bf16[8,4096]{1,0:T(8,128)(2,1)S(1)} %get-tuple-element.32), channel_id=1, source_target_pairs={{0,16},{2,18},{4,20},{6,22},{8,24},{10,26},{12,28},{14,30},{16,0},... | collective-permute-start | bytes 196616 | tf_op jit(solution)/shard_map/ppermute | solution.py:216
  50.6 1.7 %collective-permute-start.19 = (bf16[8,4096]{1,0:T(8,128)(2,1)S(1)}, bf16[8,4096]{1,0:T(8,128)(2,1)S(1)}, u32[]{:S(2)}, u32[]{:S(2)}) collective-permute-start(bf16[8,4096]{1,0:T(8,128)(2,1)S(1)} %get-tuple-element.30), channel_id=1, source_target_pairs={{0,8},{2,10},{4,12},{6,14},{8,16},{10,18},{12,20},{14,22},{16,24},... | collective-permute-start | bytes 196616 | tf_op jit(solution)/shard_map/ppermute | solution.py:216
  52.2 1.0 collective-permute-done.7
  54.3 1.2 %collective-permute-start.9 = (bf16[8,4096]{1,0:T(8,128)(2,1)S(1)}, bf16[8,4096]{1,0:T(8,128)(2,1)S(1)}, u32[]{:S(2)}, u32[]{:S(2)}) collective-permute-start(bf16[8,4096]{1,0:T(8,128)(2,1)S(1)} %get-tuple-element.34), channel_id=1, source_target_pairs={{0,16},{2,18},{4,20},{6,22},{8,24},{10,26},{12,28},{14,30},{16,0},... | collective-permute-start | bytes 196616 | tf_op jit(solution)/shard_map/ppermute | solution.py:216
  55.4 2.8 %collective-permute-start.10 = (bf16[8,4096]{1,0:T(8,128)(2,1)S(1)}, bf16[8,4096]{1,0:T(8,128)(2,1)S(1)}, u32[]{:S(2)}, u32[]{:S(2)}) collective-permute-start(bf16[8,4096]{1,0:T(8,128)(2,1)S(1)} %get-tuple-element.33), channel_id=1, source_target_pairs={{0,24},{2,26},{4,28},{6,30},{8,0},{10,2},{12,4},{14,6},{16,8},{18,... | collective-permute-start | bytes 196616 | tf_op jit(solution)/shard_map/ppermute | solution.py:216
  58.5 1.2 %collective-permute-start.29 = (bf16[8,4096]{1,0:T(8,128)(2,1)S(1)}, bf16[8,4096]{1,0:T(8,128)(2,1)S(1)}, u32[]{:S(2)}, u32[]{:S(2)}) collective-permute-start(bf16[8,4096]{1,0:T(8,128)(2,1)S(1)} %get-tuple-element.26), channel_id=1, source_target_pairs={{0,16},{2,18},{4,20},{6,22},{8,24},{10,26},{12,28},{14,30},{16,0},... | collective-permute-start | bytes 196616 | tf_op jit(solution)/shard_map/ppermute | solution.py:216
  60.4 2.2 %collective-permute-start.28 = (bf16[8,4096]{1,0:T(8,128)(2,1)S(1)}, bf16[8,4096]{1,0:T(8,128)(2,1)S(1)}, u32[]{:S(2)}, u32[]{:S(2)}) collective-permute-start(bf16[8,4096]{1,0:T(8,128)(2,1)S(1)} %get-tuple-element.26), channel_id=1, source_target_pairs={{0,24},{2,26},{4,28},{6,30},{8,0},{10,2},{12,4},{14,6},{16,8},{18,... | collective-permute-start | bytes 196616 | tf_op jit(solution)/shard_map/ppermute | solution.py:216
  62.8 4.4 %collective-permute-start.24 = (bf16[8,4096]{1,0:T(8,128)(2,1)S(1)}, bf16[8,4096]{1,0:T(8,128)(2,1)S(1)}, u32[]{:S(2)}, u32[]{:S(2)}) collective-permute-start(bf16[8,4096]{1,0:T(8,128)(2,1)S(1)} %get-tuple-element.28), channel_id=1, source_target_pairs={{0,8},{2,10},{4,12},{6,14},{8,16},{10,18},{12,20},{14,22},{16,24},... | collective-permute-start | bytes 196616 | tf_op jit(solution)/shard_map/ppermute | solution.py:216
  67.9 1.8 %collective-permute-start.22 = (bf16[8,4096]{1,0:T(8,128)(2,1)S(1)}, bf16[8,4096]{1,0:T(8,128)(2,1)S(1)}, u32[]{:S(2)}, u32[]{:S(2)}) collective-permute-start(bf16[8,4096]{1,0:T(8,128)(2,1)S(1)} %get-tuple-element.28), channel_id=1, source_target_pairs={{0,24},{2,26},{4,28},{6,30},{8,0},{10,2},{12,4},{14,6},{16,8},{18,... | collective-permute-start | bytes 196616 | tf_op jit(solution)/shard_map/ppermute | solution.py:216
  69.7 1.6 %collective-permute-start.31 = (bf16[32,4096]{1,0:T(8,128)(2,1)S(1)}, bf16[32,4096]{1,0:T(8,128)(2,1)S(1)}, u32[]{:S(2)}, u32[]{:S(2)}) collective-permute-start(bf16[32,4096]{1,0:T(8,128)(2,1)S(1)} %pad_maximum_fusion.3.refs_0_), channel_id=1, source_target_pairs={{0,4},{2,6},{4,0},{6,2},{8,12},{10,14},{12,8},{14,10},{16,20},{18,... | collective-permute-start | bytes 786440 | tf_op jit(solution)/shard_map/ppermute | solution.py:216
  71.2 2.0 %collective-permute-done.23 = bf16[8,4096]{1,0:T(8,128)(2,1)S(1)} collective-permute-done((bf16[8,4096]{1,0:T(8,128)(2,1)S(1)}, bf16[8,4096]{1,0:T(8,128)(2,1)S(1)}, u32[]{:S(2)}, u32[]{:S(2)}) %collective-permute-start.23) | collective-permute-done | bytes 65568 | tf_op jit(solution)/shard_map/ppermute | solution.py:216
  73.3 1.6 %collective-permute-start.25 = (bf16[32,4096]{1,0:T(8,128)(2,1)S(1)}, bf16[32,4096]{1,0:T(8,128)(2,1)S(1)}, u32[]{:S(2)}, u32[]{:S(2)}) collective-permute-start(bf16[32,4096]{1,0:T(8,128)(2,1)S(1)} %pad_maximum_fusion.2.refs_0_), channel_id=1, source_target_pairs={{0,4},{2,6},{4,0},{6,2},{8,12},{10,14},{12,8},{14,10},{16,20},{18,... | collective-permute-start | bytes 786440 | tf_op jit(solution)/shard_map/ppermute | solution.py:216
  74.9 3.7 %collective-permute-done.31.refs_1_ = bf16[32,4096]{1,0:T(8,128)(2,1)S(1)} collective-permute-done((bf16[32,4096]{1,0:T(8,128)(2,1)S(1)}, bf16[32,4096]{1,0:T(8,128)(2,1)S(1)}, u32[]{:S(2)}, u32[]{:S(2)}) %collective-permute-start.31) | collective-permute-done | bytes 262176 | tf_op jit(solution)/shard_map/ppermute | solution.py:216
  79.1 2.7 %collective-permute-done.25.refs_1_ = bf16[32,4096]{1,0:T(8,128)(2,1)S(1)} collective-permute-done((bf16[32,4096]{1,0:T(8,128)(2,1)S(1)}, bf16[32,4096]{1,0:T(8,128)(2,1)S(1)}, u32[]{:S(2)}, u32[]{:S(2)}) %collective-permute-start.25) | collective-permute-done | bytes 262176 | tf_op jit(solution)/shard_map/ppermute | solution.py:216
  81.7 6.5 %shard_map.52.refs_5_ = f32[976,128]{1,0:T(8,128)S(1)} custom-call(bf16[960,128]{1,0:T(8,128)(2,1)S(1)} %get-tuple-element.14.w_ref, bf16[32,4096]{1,0:T(8,128)(2,1)S(1)} %pad_maximum_fusion.3.refs_0_, bf16[32,4096]{1,0:T(8,128)(2,1)S(1)} %collective-permute-done.31.refs_1_, bf16[32,4096]{1,0:T(8,128)(2,1)S(1)} %collective-permute-done.32.refs_2_, ...), custom_call_target="tpu_custom_call" | custom-call | flops 2013265920 | bytes 7864320 | tf_op jit(solution)/shard_map/pallas_call | solution.py:165
  88.3 7.5 %shard_map.53 = bf16[976,128]{1,0:T(8,128)(2,1)S(1)} custom-call(bf16[960,128]{1,0:T(8,128)(2,1)S(1)} %get-tuple-element.14.w_ref, bf16[32,4096]{1,0:T(8,128)(2,1)S(1)} %pad_maximum_fusion.2.refs_0_, bf16[32,4096]{1,0:T(8,128)(2,1)S(1)} %collective-permute-done.25.refs_1_, bf16[32,4096]{1,0:T(8,128)(2,1)S(1)} %collective-permute-done.26.refs_2_, ...), custom_call_target="tpu_custom_call" | custom-call | flops 2013265920 | bytes 7864320 | tf_op jit(solution)/shard_map/pallas_call | solution.py:165
  95.8 1.6 %collective-permute-start.34 = (bf16[976,128]{1,0:T(8,128)(2,1)S(1)}, bf16[976,128]{1,0:T(8,128)(2,1)S(1)}, u32[]{:S(2)}, u32[]{:S(2)}) collective-permute-start(bf16[976,128]{1,0:T(8,128)(2,1)S(1)} %shard_map.53), channel_id=1, source_target_pairs={{0,1},{1,0},{2,3},{3,2},{4,5},{5,4},{6,7},{7,6},{8,9},{9,8},{10,11... | collective-permute-start | bytes 749576 | tf_op jit(solution)/shard_map/ppermute | solution.py:300
  98.2 6.1 %collective-permute-done.34 = bf16[976,128]{1,0:T(8,128)(2,1)S(1)} collective-permute-done((bf16[976,128]{1,0:T(8,128)(2,1)S(1)}, bf16[976,128]{1,0:T(8,128)(2,1)S(1)}, u32[]{:S(2)}, u32[]{:S(2)}) %collective-permute-start.34) | collective-permute-done | bytes 249888 | tf_op jit(solution)/shard_map/ppermute | solution.py:300
  (81 shorter events, 13.7 us)
Async XLA Ops:
  1.5 10.4 %collective-permute-start.13 = (bf16[8,4096]{1,0:T(8,128)(2,1)S(1)}, bf16[8,4096]{1,0:T(8,128)(2,1)S(1)}, u32[]{:S(2)}, u32[]{:S(2)}) collective-permute-start(bf16[8,4096]{1,0:T(8,128)(2,1)S(1)} %slice.199), channel_id=1, source_target_pairs={{0,8},{2,10},{4,12},{6,14},{8,16},{10,18},{12,20},{14,22},{16,24},... | collective-permute-start | bytes 196616 | tf_op jit(solution)/shard_map/ppermute | solution.py:216
  4.6 10.2 %collective-permute-start.12 = (bf16[8,4096]{1,0:T(8,128)(2,1)S(1)}, bf16[8,4096]{1,0:T(8,128)(2,1)S(1)}, u32[]{:S(2)}, u32[]{:S(2)}) collective-permute-start(bf16[8,4096]{1,0:T(8,128)(2,1)S(1)} %slice.199), channel_id=1, source_target_pairs={{0,16},{2,18},{4,20},{6,22},{8,24},{10,26},{12,28},{14,30},{16,0},... | collective-permute-start | bytes 196616 | tf_op jit(solution)/shard_map/ppermute | solution.py:216
  7.2 7.6 %collective-permute-start.11 = (bf16[8,4096]{1,0:T(8,128)(2,1)S(1)}, bf16[8,4096]{1,0:T(8,128)(2,1)S(1)}, u32[]{:S(2)}, u32[]{:S(2)}) collective-permute-start(bf16[8,4096]{1,0:T(8,128)(2,1)S(1)} %slice.199), channel_id=1, source_target_pairs={{0,24},{2,26},{4,28},{6,30},{8,0},{10,2},{12,4},{14,6},{16,8},{18,... | collective-permute-start | bytes 196616 | tf_op jit(solution)/shard_map/ppermute | solution.py:216
  10.9 6.4 %collective-permute-start.2 = (bf16[8,4224]{1,0:T(8,128)(2,1)S(1)}, bf16[8,4224]{1,0:T(8,128)(2,1)S(1)}, u32[]{:S(2)}, u32[]{:S(2)}) collective-permute-start(bf16[8,4224]{1,0:T(8,128)(2,1)S(1)} %pad_maximum_fusion.5), channel_id=1, source_target_pairs={{0,8},{2,10},{4,12},{6,14},{8,16},{10,18},{12,20},{14,22},{16,24},... | collective-permute-start | bytes 202760 | tf_op jit(solution)/shard_map/ppermute | solution.py:216
  11.6 7.3 %collective-permute-start.1 = (bf16[8,4224]{1,0:T(8,128)(2,1)S(1)}, bf16[8,4224]{1,0:T(8,128)(2,1)S(1)}, u32[]{:S(2)}, u32[]{:S(2)}) collective-permute-start(bf16[8,4224]{1,0:T(8,128)(2,1)S(1)} %pad_maximum_fusion.5), channel_id=1, source_target_pairs={{0,16},{2,18},{4,20},{6,22},{8,24},{10,26},{12,28},{14,30},{16,0},... | collective-permute-start | bytes 202760 | tf_op jit(solution)/shard_map/ppermute | solution.py:216
  12.0 6.9 %collective-permute-start = (bf16[8,4224]{1,0:T(8,128)(2,1)S(1)}, bf16[8,4224]{1,0:T(8,128)(2,1)S(1)}, u32[]{:S(2)}, u32[]{:S(2)}) collective-permute-start(bf16[8,4224]{1,0:T(8,128)(2,1)S(1)} %pad_maximum_fusion.5), channel_id=1, source_target_pairs={{0,24},{2,26},{4,28},{6,30},{8,0},{10,2},{12,4},{14,6},{16,8},{18,... | collective-permute-start | bytes 202760 | tf_op jit(solution)/shard_map/ppermute | solution.py:216
  14.8 9.2 %collective-permute-start.14 = (bf16[32,4096]{1,0:T(8,128)(2,1)S(1)}, bf16[32,4096]{1,0:T(8,128)(2,1)S(1)}, u32[]{:S(2)}, u32[]{:S(2)}) collective-permute-start(bf16[32,4096]{1,0:T(8,128)(2,1)S(1)} %pad_maximum_fusion.1.refs_0_), channel_id=1, source_target_pairs={{0,4},{2,6},{4,0},{6,2},{8,12},{10,14},{12,8},{14,10},{16,20},{18,... | collective-permute-start | bytes 786440 | tf_op jit(solution)/shard_map/ppermute | solution.py:216
  19.0 8.4 %collective-permute-start.3 = (bf16[32,4224]{1,0:T(8,128)(2,1)S(1)}, bf16[32,4224]{1,0:T(8,128)(2,1)S(1)}, u32[]{:S(2)}, u32[]{:S(2)}) collective-permute-start(bf16[32,4224]{1,0:T(8,128)(2,1)S(1)} %pad_maximum_fusion.refs_0_), channel_id=1, source_target_pairs={{0,4},{2,6},{4,0},{6,2},{8,12},{10,14},{12,8},{14,10},{16,20},{18,... | collective-permute-start | bytes 811016 | tf_op jit(solution)/shard_map/ppermute | solution.py:216
  20.5 6.8 %collective-permute-start.4 = (bf16[32,4224]{1,0:T(8,128)(2,1)S(1)}, bf16[32,4224]{1,0:T(8,128)(2,1)S(1)}, u32[]{:S(2)}, u32[]{:S(2)}) collective-permute-start(bf16[32,4224]{1,0:T(8,128)(2,1)S(1)} %pad_maximum_fusion.refs_0_), channel_id=1, source_target_pairs={{0,2},{2,0},{4,6},{6,4},{8,10},{10,8},{12,14},{14,12},{16,18},{18,... | collective-permute-start | bytes 811016 | tf_op jit(solution)/shard_map/ppermute | solution.py:216
  20.5 6.8 %collective-permute-start.15 = (bf16[32,4096]{1,0:T(8,128)(2,1)S(1)}, bf16[32,4096]{1,0:T(8,128)(2,1)S(1)}, u32[]{:S(2)}, u32[]{:S(2)}) collective-permute-start(bf16[32,4096]{1,0:T(8,128)(2,1)S(1)} %pad_maximum_fusion.1.refs_0_), channel_id=1, source_target_pairs={{0,2},{2,0},{4,6},{6,4},{8,10},{10,8},{12,14},{14,12},{16,18},{18,... | collective-permute-start | bytes 786440 | tf_op jit(solution)/shard_map/ppermute | solution.py:216
  27.3 5.8 %collective-permute-start.5 = (bf16[32,4224]{1,0:T(8,128)(2,1)S(1)}, bf16[32,4224]{1,0:T(8,128)(2,1)S(1)}, u32[]{:S(2)}, u32[]{:S(2)}) collective-permute-start(bf16[32,4224]{1,0:T(8,128)(2,1)S(1)} %collective-permute-done.3.refs_1_), channel_id=1, source_target_pairs={{0,2},{2,0},{4,6},{6,4},{8,10},{10,8},{12,14},{14,12},{16,18},{18,... | collective-permute-start | bytes 811016 | tf_op jit(solution)/shard_map/ppermute | solution.py:216
  32.6 5.9 %collective-permute-start.17 = (bf16[64,4096]{1,0:T(8,128)(2,1)S(1)}, bf16[64,4096]{1,0:T(8,128)(2,1)S(1)}, u32[]{:S(2)}, u32[]{:S(2)}) collective-permute-start(bf16[64,4096]{1,0:T(8,128)(2,1)S(1)} %get-tuple-element.22), channel_id=1, source_target_pairs={{0,2},{2,0},{4,6},{6,4},{8,10},{10,8},{12,14},{14,12},{16,18},{18,... | collective-permute-start | bytes 1572872 | tf_op jit(solution)/shard_map/ppermute | solution.py:216
  38.9 9.2 %collective-permute-start.18 = (bf16[32,4096]{1,0:T(8,128)(2,1)S(1)}, bf16[32,4096]{1,0:T(8,128)(2,1)S(1)}, u32[]{:S(2)}, u32[]{:S(2)}) collective-permute-start(bf16[32,4096]{1,0:T(8,128)(2,1)S(1)} %fusion.15), channel_id=1, source_target_pairs={{0,4},{2,6},{4,0},{6,2},{8,12},{10,14},{12,8},{14,10},{16,20},{18,... | collective-permute-start | bytes 786440 | tf_op jit(solution)/shard_map/ppermute | solution.py:216
  40.9 12.4 %collective-permute-start.7 = (bf16[32,4096]{1,0:T(8,128)(2,1)S(1)}, bf16[32,4096]{1,0:T(8,128)(2,1)S(1)}, u32[]{:S(2)}, u32[]{:S(2)}) collective-permute-start(bf16[32,4096]{1,0:T(8,128)(2,1)S(1)} %fusion.14), channel_id=1, source_target_pairs={{0,4},{2,6},{4,0},{6,2},{8,12},{10,14},{12,8},{14,10},{16,20},{18,... | collective-permute-start | bytes 786440 | tf_op jit(solution)/shard_map/ppermute | solution.py:216
  48.4 7.0 %collective-permute-start.21 = (bf16[8,4096]{1,0:T(8,128)(2,1)S(1)}, bf16[8,4096]{1,0:T(8,128)(2,1)S(1)}, u32[]{:S(2)}, u32[]{:S(2)}) collective-permute-start(bf16[8,4096]{1,0:T(8,128)(2,1)S(1)} %get-tuple-element.31), channel_id=1, source_target_pairs={{0,24},{2,26},{4,28},{6,30},{8,0},{10,2},{12,4},{14,6},{16,8},{18,... | collective-permute-start | bytes 196616 | tf_op jit(solution)/shard_map/ppermute | solution.py:216
  49.4 8.8 %collective-permute-start.20 = (bf16[8,4096]{1,0:T(8,128)(2,1)S(1)}, bf16[8,4096]{1,0:T(8,128)(2,1)S(1)}, u32[]{:S(2)}, u32[]{:S(2)}) collective-permute-start(bf16[8,4096]{1,0:T(8,128)(2,1)S(1)} %get-tuple-element.32), channel_id=1, source_target_pairs={{0,16},{2,18},{4,20},{6,22},{8,24},{10,26},{12,28},{14,30},{16,0},... | collective-permute-start | bytes 196616 | tf_op jit(solution)/shard_map/ppermute | solution.py:216
  50.6 7.7 %collective-permute-start.19 = (bf16[8,4096]{1,0:T(8,128)(2,1)S(1)}, bf16[8,4096]{1,0:T(8,128)(2,1)S(1)}, u32[]{:S(2)}, u32[]{:S(2)}) collective-permute-start(bf16[8,4096]{1,0:T(8,128)(2,1)S(1)} %get-tuple-element.30), channel_id=1, source_target_pairs={{0,8},{2,10},{4,12},{6,14},{8,16},{10,18},{12,20},{14,22},{16,24},... | collective-permute-start | bytes 196616 | tf_op jit(solution)/shard_map/ppermute | solution.py:216
  53.6 6.8 %collective-permute-start.8 = (bf16[8,4096]{1,0:T(8,128)(2,1)S(1)}, bf16[8,4096]{1,0:T(8,128)(2,1)S(1)}, u32[]{:S(2)}, u32[]{:S(2)}) collective-permute-start(bf16[8,4096]{1,0:T(8,128)(2,1)S(1)} %get-tuple-element.35), channel_id=1, source_target_pairs={{0,8},{2,10},{4,12},{6,14},{8,16},{10,18},{12,20},{14,22},{16,24},... | collective-permute-start | bytes 196616 | tf_op jit(solution)/shard_map/ppermute | solution.py:216
  54.3 8.3 %collective-permute-start.9 = (bf16[8,4096]{1,0:T(8,128)(2,1)S(1)}, bf16[8,4096]{1,0:T(8,128)(2,1)S(1)}, u32[]{:S(2)}, u32[]{:S(2)}) collective-permute-start(bf16[8,4096]{1,0:T(8,128)(2,1)S(1)} %get-tuple-element.34), channel_id=1, source_target_pairs={{0,16},{2,18},{4,20},{6,22},{8,24},{10,26},{12,28},{14,30},{16,0},... | collective-permute-start | bytes 196616 | tf_op jit(solution)/shard_map/ppermute | solution.py:216
  55.4 7.2 %collective-permute-start.10 = (bf16[8,4096]{1,0:T(8,128)(2,1)S(1)}, bf16[8,4096]{1,0:T(8,128)(2,1)S(1)}, u32[]{:S(2)}, u32[]{:S(2)}) collective-permute-start(bf16[8,4096]{1,0:T(8,128)(2,1)S(1)} %get-tuple-element.33), channel_id=1, source_target_pairs={{0,24},{2,26},{4,28},{6,30},{8,0},{10,2},{12,4},{14,6},{16,8},{18,... | collective-permute-start | bytes 196616 | tf_op jit(solution)/shard_map/ppermute | solution.py:216
  58.4 9.5 %collective-permute-start.30 = (bf16[8,4096]{1,0:T(8,128)(2,1)S(1)}, bf16[8,4096]{1,0:T(8,128)(2,1)S(1)}, u32[]{:S(2)}, u32[]{:S(2)}) collective-permute-start(bf16[8,4096]{1,0:T(8,128)(2,1)S(1)} %get-tuple-element.26), channel_id=1, source_target_pairs={{0,8},{2,10},{4,12},{6,14},{8,16},{10,18},{12,20},{14,22},{16,24},... | collective-permute-start | bytes 196616 | tf_op jit(solution)/shard_map/ppermute | solution.py:216
  58.5 11.1 %collective-permute-start.29 = (bf16[8,4096]{1,0:T(8,128)(2,1)S(1)}, bf16[8,4096]{1,0:T(8,128)(2,1)S(1)}, u32[]{:S(2)}, u32[]{:S(2)}) collective-permute-start(bf16[8,4096]{1,0:T(8,128)(2,1)S(1)} %get-tuple-element.26), channel_id=1, source_target_pairs={{0,16},{2,18},{4,20},{6,22},{8,24},{10,26},{12,28},{14,30},{16,0},... | collective-permute-start | bytes 196616 | tf_op jit(solution)/shard_map/ppermute | solution.py:216
  60.4 9.3 %collective-permute-start.28 = (bf16[8,4096]{1,0:T(8,128)(2,1)S(1)}, bf16[8,4096]{1,0:T(8,128)(2,1)S(1)}, u32[]{:S(2)}, u32[]{:S(2)}) collective-permute-start(bf16[8,4096]{1,0:T(8,128)(2,1)S(1)} %get-tuple-element.26), channel_id=1, source_target_pairs={{0,24},{2,26},{4,28},{6,30},{8,0},{10,2},{12,4},{14,6},{16,8},{18,... | collective-permute-start | bytes 196616 | tf_op jit(solution)/shard_map/ppermute | solution.py:216
  62.8 8.4 %collective-permute-start.24 = (bf16[8,4096]{1,0:T(8,128)(2,1)S(1)}, bf16[8,4096]{1,0:T(8,128)(2,1)S(1)}, u32[]{:S(2)}, u32[]{:S(2)}) collective-permute-start(bf16[8,4096]{1,0:T(8,128)(2,1)S(1)} %get-tuple-element.28), channel_id=1, source_target_pairs={{0,8},{2,10},{4,12},{6,14},{8,16},{10,18},{12,20},{14,22},{16,24},... | collective-permute-start | bytes 196616 | tf_op jit(solution)/shard_map/ppermute | solution.py:216
  67.2 6.0 %collective-permute-start.23 = (bf16[8,4096]{1,0:T(8,128)(2,1)S(1)}, bf16[8,4096]{1,0:T(8,128)(2,1)S(1)}, u32[]{:S(2)}, u32[]{:S(2)}) collective-permute-start(bf16[8,4096]{1,0:T(8,128)(2,1)S(1)} %get-tuple-element.28), channel_id=1, source_target_pairs={{0,16},{2,18},{4,20},{6,22},{8,24},{10,26},{12,28},{14,30},{16,0},... | collective-permute-start | bytes 196616 | tf_op jit(solution)/shard_map/ppermute | solution.py:216
  67.9 5.4 %collective-permute-start.22 = (bf16[8,4096]{1,0:T(8,128)(2,1)S(1)}, bf16[8,4096]{1,0:T(8,128)(2,1)S(1)}, u32[]{:S(2)}, u32[]{:S(2)}) collective-permute-start(bf16[8,4096]{1,0:T(8,128)(2,1)S(1)} %get-tuple-element.28), channel_id=1, source_target_pairs={{0,24},{2,26},{4,28},{6,30},{8,0},{10,2},{12,4},{14,6},{16,8},{18,... | collective-permute-start | bytes 196616 | tf_op jit(solution)/shard_map/ppermute | solution.py:216
  69.7 8.9 %collective-permute-start.31 = (bf16[32,4096]{1,0:T(8,128)(2,1)S(1)}, bf16[32,4096]{1,0:T(8,128)(2,1)S(1)}, u32[]{:S(2)}, u32[]{:S(2)}) collective-permute-start(bf16[32,4096]{1,0:T(8,128)(2,1)S(1)} %pad_maximum_fusion.3.refs_0_), channel_id=1, source_target_pairs={{0,4},{2,6},{4,0},{6,2},{8,12},{10,14},{12,8},{14,10},{16,20},{18,... | collective-permute-start | bytes 786440 | tf_op jit(solution)/shard_map/ppermute | solution.py:216
  73.3 8.4 %collective-permute-start.25 = (bf16[32,4096]{1,0:T(8,128)(2,1)S(1)}, bf16[32,4096]{1,0:T(8,128)(2,1)S(1)}, u32[]{:S(2)}, u32[]{:S(2)}) collective-permute-start(bf16[32,4096]{1,0:T(8,128)(2,1)S(1)} %pad_maximum_fusion.2.refs_0_), channel_id=1, source_target_pairs={{0,4},{2,6},{4,0},{6,2},{8,12},{10,14},{12,8},{14,10},{16,20},{18,... | collective-permute-start | bytes 786440 | tf_op jit(solution)/shard_map/ppermute | solution.py:216
  74.8 6.9 %collective-permute-start.32 = (bf16[32,4096]{1,0:T(8,128)(2,1)S(1)}, bf16[32,4096]{1,0:T(8,128)(2,1)S(1)}, u32[]{:S(2)}, u32[]{:S(2)}) collective-permute-start(bf16[32,4096]{1,0:T(8,128)(2,1)S(1)} %pad_maximum_fusion.3.refs_0_), channel_id=1, source_target_pairs={{0,2},{2,0},{4,6},{6,4},{8,10},{10,8},{12,14},{14,12},{16,18},{18,... | collective-permute-start | bytes 786440 | tf_op jit(solution)/shard_map/ppermute | solution.py:216
  78.6 9.7 %collective-permute-start.26 = (bf16[32,4096]{1,0:T(8,128)(2,1)S(1)}, bf16[32,4096]{1,0:T(8,128)(2,1)S(1)}, u32[]{:S(2)}, u32[]{:S(2)}) collective-permute-start(bf16[32,4096]{1,0:T(8,128)(2,1)S(1)} %pad_maximum_fusion.2.refs_0_), channel_id=1, source_target_pairs={{0,2},{2,0},{4,6},{6,4},{8,10},{10,8},{12,14},{14,12},{16,18},{18,... | collective-permute-start | bytes 786440 | tf_op jit(solution)/shard_map/ppermute | solution.py:216
  81.7 6.6 %collective-permute-start.27 = (bf16[32,4096]{1,0:T(8,128)(2,1)S(1)}, bf16[32,4096]{1,0:T(8,128)(2,1)S(1)}, u32[]{:S(2)}, u32[]{:S(2)}) collective-permute-start(bf16[32,4096]{1,0:T(8,128)(2,1)S(1)} %collective-permute-done.25.refs_1_), channel_id=1, source_target_pairs={{0,2},{2,0},{4,6},{6,4},{8,10},{10,8},{12,14},{14,12},{16,18},{18,... | collective-permute-start | bytes 786440 | tf_op jit(solution)/shard_map/ppermute | solution.py:216
  95.8 8.5 %collective-permute-start.34 = (bf16[976,128]{1,0:T(8,128)(2,1)S(1)}, bf16[976,128]{1,0:T(8,128)(2,1)S(1)}, u32[]{:S(2)}, u32[]{:S(2)}) collective-permute-start(bf16[976,128]{1,0:T(8,128)(2,1)S(1)} %shard_map.53), channel_id=1, source_target_pairs={{0,1},{1,0},{2,3},{3,2},{4,5},{5,4},{6,7},{7,6},{8,9},{9,8},{10,11... | collective-permute-start | bytes 749576 | tf_op jit(solution)/shard_map/ppermute | solution.py:300
  (6 other events, 66.4 us)

commit v4 on v3

--- a/solution.py
+++ b/solution.py
@@ -265,10 +265,7 @@
 
     gathered = []
     for i in range(chunks):
-        source = h_factor
-        if i == chunks - 1:
-            source, sums = lax.optimization_barrier((source, sums))
-        own = source[:, starts[i] : starts[i] + widths[i]].astype(BF16)
+        own = h_factor[:, starts[i] : starts[i] + widths[i]].astype(BF16)
         if i == chunks - 1:
             own = jnp.concatenate([own, sums], 1)
         gathered.append(gather(own))

time: 106 us -> 106 us (level)
  waiting for transfers between devices: 31 us -> 33.2 us
  starting transfers between devices: 42.2 us -> 40.9 us
    ppermute x34, waiting for transfers between devices: 24.9 us -> 26.4 us  [send(): return lax.ppermute(value, 'cell', [(i, route(i)) for i in range(devices)])]
  transfers between devices with their start and end apart: 35 -> 35, of which waited for: 11 -> 13; matrix products, arithmetic and copies ran while one was open for 3% -> 3% of each run, Pallas kernels for 16% -> 16%
where the time goes in v4:
time: 106 us; the launch traced here: 105 us
  starting transfers between devices  40.9 us (39%)
  waiting for transfers between devices  33.2 us (31%)
  Pallas kernels  24.7 us (23%)
  other arithmetic  3.61 us (3%)
  local copies, waits for them, and re-layouts  2.14 us (2%)
    ppermute x34, starting transfers between devices, send(): return lax.ppermute(value, 'cell', [(i, route(i)) for i in range(devices)])  40.1 us
    ppermute x34, waiting for transfers between devices, send(): return lax.ppermute(value, 'cell', [(i, route(i)) for i in range(devices)])  26.4 us
    pallas_call x4, Pallas kernels, call(): pl.pallas_call(kernel, in_specs=[local] * len(held_args) + [pl.BlockSpec(...  24.4 us
    ppermute x1, waiting for transfers between devices, per_device(): got = lax.ppermute(running, 'gene', [(0, 1), (1, 0)])  6.9 us
  transfers between devices with their start and end apart: 35, of which 13 were waited for; matrix products, arithmetic and copies ran while one was open for 3% of the time, Pallas kernels for 16%

profile of v4, /device:TPU:0, one launch (start us, length us, event | category | flops | bytes accessed | tf_op | source)
XLA Modules:
  0.0 105.4 jit_solution(5031503848764708933)
XLA Ops:
  1.6 3.1 %collective-permute-start.13 = (bf16[8,4096]{1,0:T(8,128)(2,1)S(1)}, bf16[8,4096]{1,0:T(8,128)(2,1)S(1)}, u32[]{:S(2)}, u32[]{:S(2)}) collective-permute-start(bf16[8,4096]{1,0:T(8,128)(2,1)S(1)} %get-tuple-element.26), channel_id=1, source_target_pairs={{0,8},{2,10},{4,12},{6,14},{8,16},{10,18},{12,20},{14,22},{16,24},... | collective-permute-start | bytes 196616 | tf_op jit(solution)/shard_map/ppermute | solution.py:216
  4.7 2.6 %collective-permute-start.12 = (bf16[8,4096]{1,0:T(8,128)(2,1)S(1)}, bf16[8,4096]{1,0:T(8,128)(2,1)S(1)}, u32[]{:S(2)}, u32[]{:S(2)}) collective-permute-start(bf16[8,4096]{1,0:T(8,128)(2,1)S(1)} %get-tuple-element.26), channel_id=1, source_target_pairs={{0,16},{2,18},{4,20},{6,22},{8,24},{10,26},{12,28},{14,30},{16,0},... | collective-permute-start | bytes 196616 | tf_op jit(solution)/shard_map/ppermute | solution.py:216
  7.3 1.3 %collective-permute-start.11 = (bf16[8,4096]{1,0:T(8,128)(2,1)S(1)}, bf16[8,4096]{1,0:T(8,128)(2,1)S(1)}, u32[]{:S(2)}, u32[]{:S(2)}) collective-permute-start(bf16[8,4096]{1,0:T(8,128)(2,1)S(1)} %get-tuple-element.26), channel_id=1, source_target_pairs={{0,24},{2,26},{4,28},{6,30},{8,0},{10,2},{12,4},{14,6},{16,8},{18,... | collective-permute-start | bytes 196616 | tf_op jit(solution)/shard_map/ppermute | solution.py:216
  11.2 2.8 %collective-permute-start = (bf16[8,4224]{1,0:T(8,128)(2,1)S(1)}, bf16[8,4224]{1,0:T(8,128)(2,1)S(1)}, u32[]{:S(2)}, u32[]{:S(2)}) collective-permute-start(bf16[8,4224]{1,0:T(8,128)(2,1)S(1)} %pad_maximum_fusion.5), channel_id=1, source_target_pairs={{0,24},{2,26},{4,28},{6,30},{8,0},{10,2},{12,4},{14,6},{16,8},{18,... | collective-permute-start | bytes 202760 | tf_op jit(solution)/shard_map/ppermute | solution.py:216
  14.1 1.6 %collective-permute-start.14 = (bf16[32,4096]{1,0:T(8,128)(2,1)S(1)}, bf16[32,4096]{1,0:T(8,128)(2,1)S(1)}, u32[]{:S(2)}, u32[]{:S(2)}) collective-permute-start(bf16[32,4096]{1,0:T(8,128)(2,1)S(1)} %pad_maximum_fusion.1.refs_0_), channel_id=1, source_target_pairs={{0,4},{2,6},{4,0},{6,2},{8,12},{10,14},{12,8},{14,10},{16,20},{18,... | collective-permute-start | bytes 786440 | tf_op jit(solution)/shard_map/ppermute | solution.py:216
  16.6 1.6 %collective-permute-done.1 = bf16[8,4224]{1,0:T(8,128)(2,1)S(1)} collective-permute-done((bf16[8,4224]{1,0:T(8,128)(2,1)S(1)}, bf16[8,4224]{1,0:T(8,128)(2,1)S(1)}, u32[]{:S(2)}, u32[]{:S(2)}) %collective-permute-start.1) | collective-permute-done | bytes 67616 | tf_op jit(solution)/shard_map/ppermute | solution.py:216
  18.2 1.6 %collective-permute-start.3 = (bf16[32,4224]{1,0:T(8,128)(2,1)S(1)}, bf16[32,4224]{1,0:T(8,128)(2,1)S(1)}, u32[]{:S(2)}, u32[]{:S(2)}) collective-permute-start(bf16[32,4224]{1,0:T(8,128)(2,1)S(1)} %pad_maximum_fusion.refs_0_), channel_id=1, source_target_pairs={{0,4},{2,6},{4,0},{6,2},{8,12},{10,14},{12,8},{14,10},{16,20},{18,... | collective-permute-start | bytes 811016 | tf_op jit(solution)/shard_map/ppermute | solution.py:216
  20.2 3.1 %collective-permute-done.14.refs_1_ = bf16[32,4096]{1,0:T(8,128)(2,1)S(1)} collective-permute-done((bf16[32,4096]{1,0:T(8,128)(2,1)S(1)}, bf16[32,4096]{1,0:T(8,128)(2,1)S(1)}, u32[]{:S(2)}, u32[]{:S(2)}) %collective-permute-start.14) | collective-permute-done | bytes 262176 | tf_op jit(solution)/shard_map/ppermute | solution.py:216
  23.3 3.3 %collective-permute-done.3.refs_1_ = bf16[32,4224]{1,0:T(8,128)(2,1)S(1)} collective-permute-done((bf16[32,4224]{1,0:T(8,128)(2,1)S(1)}, bf16[32,4224]{1,0:T(8,128)(2,1)S(1)}, u32[]{:S(2)}, u32[]{:S(2)}) %collective-permute-start.3) | collective-permute-done | bytes 270368 | tf_op jit(solution)/shard_map/ppermute | solution.py:216
  26.6 5.2 %shard_map.51 = (f32[64,4096]{1,0:T(8,128)S(1)}, bf16[64,4096]{1,0:T(8,128)(2,1)S(1)}) custom-call(bf16[128,960]{1,0:T(8,128)(2,1)S(1)} %get-tuple-element.13.wt_ref, bf16[960,128]{1,0:T(8,128)(2,1)S(1)} %get-tuple-element.12.w_ref, bf16[32,4096]{1,0:T(8,128)(2,1)S(1)} %pad_maximum_fusion.1.refs_0_, bf16[32,4096]{1,0:T(8,128)(2,1)S(1)} %collective-permute-done.14.refs_1_, ...), custom_call_target="tpu_custom_call" | custom-call | flops 15099494400 | bytes 7864320 | tf_op jit(solution)/shard_map/pallas_call | solution.py:165
  32.4 5.2 %shard_map.50 = (f32[64,4096]{1,0:T(8,128)S(1)}, bf16[64,4096]{1,0:T(8,128)(2,1)S(1)}) custom-call(bf16[128,960]{1,0:T(8,128)(2,1)S(1)} %get-tuple-element.13.wt_ref, bf16[960,128]{1,0:T(8,128)(2,1)S(1)} %get-tuple-element.12.w_ref, bf16[32,4224]{1,0:T(8,128)(2,1)S(1)} %pad_maximum_fusion.refs_0_, bf16[32,4224]{1,0:T(8,128)(2,1)S(1)} %collective-permute-done.3.refs_1_, ...), custom_call_target="tpu_custom_call" | custom-call | flops 15099494400 | bytes 7864320 | tf_op jit(solution)/shard_map/pallas_call | solution.py:165
  38.1 1.6 %collective-permute-start.18 = (bf16[32,4096]{1,0:T(8,128)(2,1)S(1)}, bf16[32,4096]{1,0:T(8,128)(2,1)S(1)}, u32[]{:S(2)}, u32[]{:S(2)}) collective-permute-start(bf16[32,4096]{1,0:T(8,128)(2,1)S(1)} %fusion.15), channel_id=1, source_target_pairs={{0,4},{2,6},{4,0},{6,2},{8,12},{10,14},{12,8},{14,10},{16,20},{18,... | collective-permute-start | bytes 786440 | tf_op jit(solution)/shard_map/ppermute | solution.py:216
  40.1 1.4 %collective-permute-start.7 = (bf16[32,4096]{1,0:T(8,128)(2,1)S(1)}, bf16[32,4096]{1,0:T(8,128)(2,1)S(1)}, u32[]{:S(2)}, u32[]{:S(2)}) collective-permute-start(bf16[32,4096]{1,0:T(8,128)(2,1)S(1)} %fusion.14), channel_id=1, source_target_pairs={{0,4},{2,6},{4,0},{6,2},{8,12},{10,14},{12,8},{14,10},{16,20},{18,... | collective-permute-start | bytes 786440 | tf_op jit(solution)/shard_map/ppermute | solution.py:216
  41.5 5.9 %collective-permute-done.18 = bf16[32,4096]{1,0:T(8,128)(2,1)S(1)} collective-permute-done((bf16[32,4096]{1,0:T(8,128)(2,1)S(1)}, bf16[32,4096]{1,0:T(8,128)(2,1)S(1)}, u32[]{:S(2)}, u32[]{:S(2)}) %collective-permute-start.18) | collective-permute-done | bytes 262176 | tf_op jit(solution)/shard_map/ppermute | solution.py:216
  47.6 2.3 %collective-permute-start.21 = (bf16[8,4096]{1,0:T(8,128)(2,1)S(1)}, bf16[8,4096]{1,0:T(8,128)(2,1)S(1)}, u32[]{:S(2)}, u32[]{:S(2)}) collective-permute-start(bf16[8,4096]{1,0:T(8,128)(2,1)S(1)} %get-tuple-element.29), channel_id=1, source_target_pairs={{0,24},{2,26},{4,28},{6,30},{8,0},{10,2},{12,4},{14,6},{16,8},{18,... | collective-permute-start | bytes 196616 | tf_op jit(solution)/shard_map/ppermute | solution.py:216
  50.3 1.2 %collective-permute-start.19 = (bf16[8,4096]{1,0:T(8,128)(2,1)S(1)}, bf16[8,4096]{1,0:T(8,128)(2,1)S(1)}, u32[]{:S(2)}, u32[]{:S(2)}) collective-permute-start(bf16[8,4096]{1,0:T(8,128)(2,1)S(1)} %get-tuple-element.28), channel_id=1, source_target_pairs={{0,8},{2,10},{4,12},{6,14},{8,16},{10,18},{12,20},{14,22},{16,24},... | collective-permute-start | bytes 196616 | tf_op jit(solution)/shard_map/ppermute | solution.py:216
  51.5 1.0 collective-permute-done.7
  52.8 1.2 %collective-permute-start.8 = (bf16[8,4096]{1,0:T(8,128)(2,1)S(1)}, bf16[8,4096]{1,0:T(8,128)(2,1)S(1)}, u32[]{:S(2)}, u32[]{:S(2)}) collective-permute-start(bf16[8,4096]{1,0:T(8,128)(2,1)S(1)} %get-tuple-element.33), channel_id=1, source_target_pairs={{0,8},{2,10},{4,12},{6,14},{8,16},{10,18},{12,20},{14,22},{16,24},... | collective-permute-start | bytes 196616 | tf_op jit(solution)/shard_map/ppermute | solution.py:216
  53.9 1.7 %collective-permute-start.9 = (bf16[8,4096]{1,0:T(8,128)(2,1)S(1)}, bf16[8,4096]{1,0:T(8,128)(2,1)S(1)}, u32[]{:S(2)}, u32[]{:S(2)}) collective-permute-start(bf16[8,4096]{1,0:T(8,128)(2,1)S(1)} %get-tuple-element.32), channel_id=1, source_target_pairs={{0,16},{2,18},{4,20},{6,22},{8,24},{10,26},{12,28},{14,30},{16,0},... | collective-permute-start | bytes 196616 | tf_op jit(solution)/shard_map/ppermute | solution.py:216
  55.7 1.8 %collective-permute-start.10 = (bf16[8,4096]{1,0:T(8,128)(2,1)S(1)}, bf16[8,4096]{1,0:T(8,128)(2,1)S(1)}, u32[]{:S(2)}, u32[]{:S(2)}) collective-permute-start(bf16[8,4096]{1,0:T(8,128)(2,1)S(1)} %get-tuple-element.31), channel_id=1, source_target_pairs={{0,24},{2,26},{4,28},{6,30},{8,0},{10,2},{12,4},{14,6},{16,8},{18,... | collective-permute-start | bytes 196616 | tf_op jit(solution)/shard_map/ppermute | solution.py:216
  57.9 1.2 %collective-permute-start.29 = (bf16[8,4096]{1,0:T(8,128)(2,1)S(1)}, bf16[8,4096]{1,0:T(8,128)(2,1)S(1)}, u32[]{:S(2)}, u32[]{:S(2)}) collective-permute-start(bf16[8,4096]{1,0:T(8,128)(2,1)S(1)} %get-tuple-element.22), channel_id=1, source_target_pairs={{0,16},{2,18},{4,20},{6,22},{8,24},{10,26},{12,28},{14,30},{16,0},... | collective-permute-start | bytes 196616 | tf_op jit(solution)/shard_map/ppermute | solution.py:216
  59.6 2.3 %collective-permute-start.28 = (bf16[8,4096]{1,0:T(8,128)(2,1)S(1)}, bf16[8,4096]{1,0:T(8,128)(2,1)S(1)}, u32[]{:S(2)}, u32[]{:S(2)}) collective-permute-start(bf16[8,4096]{1,0:T(8,128)(2,1)S(1)} %get-tuple-element.22), channel_id=1, source_target_pairs={{0,24},{2,26},{4,28},{6,30},{8,0},{10,2},{12,4},{14,6},{16,8},{18,... | collective-permute-start | bytes 196616 | tf_op jit(solution)/shard_map/ppermute | solution.py:216
  62.1 4.0 %collective-permute-start.24 = (bf16[8,4096]{1,0:T(8,128)(2,1)S(1)}, bf16[8,4096]{1,0:T(8,128)(2,1)S(1)}, u32[]{:S(2)}, u32[]{:S(2)}) collective-permute-start(bf16[8,4096]{1,0:T(8,128)(2,1)S(1)} %get-tuple-element.24), channel_id=1, source_target_pairs={{0,8},{2,10},{4,12},{6,14},{8,16},{10,18},{12,20},{14,22},{16,24},... | collective-permute-start | bytes 196616 | tf_op jit(solution)/shard_map/ppermute | solution.py:216
  66.1 2.0 %collective-permute-start.23 = (bf16[8,4096]{1,0:T(8,128)(2,1)S(1)}, bf16[8,4096]{1,0:T(8,128)(2,1)S(1)}, u32[]{:S(2)}, u32[]{:S(2)}) collective-permute-start(bf16[8,4096]{1,0:T(8,128)(2,1)S(1)} %get-tuple-element.24), channel_id=1, source_target_pairs={{0,16},{2,18},{4,20},{6,22},{8,24},{10,26},{12,28},{14,30},{16,0},... | collective-permute-start | bytes 196616 | tf_op jit(solution)/shard_map/ppermute | solution.py:216
  68.6 1.6 %collective-permute-start.31 = (bf16[32,4096]{1,0:T(8,128)(2,1)S(1)}, bf16[32,4096]{1,0:T(8,128)(2,1)S(1)}, u32[]{:S(2)}, u32[]{:S(2)}) collective-permute-start(bf16[32,4096]{1,0:T(8,128)(2,1)S(1)} %pad_maximum_fusion.3.refs_0_), channel_id=1, source_target_pairs={{0,4},{2,6},{4,0},{6,2},{8,12},{10,14},{12,8},{14,10},{16,20},{18,... | collective-permute-start | bytes 786440 | tf_op jit(solution)/shard_map/ppermute | solution.py:216
  70.6 2.1 %collective-permute-done.23 = bf16[8,4096]{1,0:T(8,128)(2,1)S(1)} collective-permute-done((bf16[8,4096]{1,0:T(8,128)(2,1)S(1)}, bf16[8,4096]{1,0:T(8,128)(2,1)S(1)}, u32[]{:S(2)}, u32[]{:S(2)}) %collective-permute-start.23) | collective-permute-done | bytes 65568 | tf_op jit(solution)/shard_map/ppermute | solution.py:216
  73.2 1.1 %collective-permute-start.25 = (bf16[32,4096]{1,0:T(8,128)(2,1)S(1)}, bf16[32,4096]{1,0:T(8,128)(2,1)S(1)}, u32[]{:S(2)}, u32[]{:S(2)}) collective-permute-start(bf16[32,4096]{1,0:T(8,128)(2,1)S(1)} %pad_maximum_fusion.2.refs_0_), channel_id=1, source_target_pairs={{0,4},{2,6},{4,0},{6,2},{8,12},{10,14},{12,8},{14,10},{16,20},{18,... | collective-permute-start | bytes 786440 | tf_op jit(solution)/shard_map/ppermute | solution.py:216
  74.3 2.9 %collective-permute-done.31.refs_1_ = bf16[32,4096]{1,0:T(8,128)(2,1)S(1)} collective-permute-done((bf16[32,4096]{1,0:T(8,128)(2,1)S(1)}, bf16[32,4096]{1,0:T(8,128)(2,1)S(1)}, u32[]{:S(2)}, u32[]{:S(2)}) %collective-permute-start.31) | collective-permute-done | bytes 262176 | tf_op jit(solution)/shard_map/ppermute | solution.py:216
  77.7 4.2 %collective-permute-done.25.refs_1_ = bf16[32,4096]{1,0:T(8,128)(2,1)S(1)} collective-permute-done((bf16[32,4096]{1,0:T(8,128)(2,1)S(1)}, bf16[32,4096]{1,0:T(8,128)(2,1)S(1)}, u32[]{:S(2)}, u32[]{:S(2)}) %collective-permute-start.25) | collective-permute-done | bytes 262176 | tf_op jit(solution)/shard_map/ppermute | solution.py:216
  81.9 6.5 %shard_map.52.refs_5_ = f32[976,128]{1,0:T(8,128)S(1)} custom-call(bf16[960,128]{1,0:T(8,128)(2,1)S(1)} %get-tuple-element.12.w_ref, bf16[32,4096]{1,0:T(8,128)(2,1)S(1)} %pad_maximum_fusion.3.refs_0_, bf16[32,4096]{1,0:T(8,128)(2,1)S(1)} %collective-permute-done.31.refs_1_, bf16[32,4096]{1,0:T(8,128)(2,1)S(1)} %collective-permute-done.32.refs_2_, ...), custom_call_target="tpu_custom_call" | custom-call | flops 2013265920 | bytes 7864320 | tf_op jit(solution)/shard_map/pallas_call | solution.py:165
  88.4 7.5 %shard_map.53 = bf16[976,128]{1,0:T(8,128)(2,1)S(1)} custom-call(bf16[960,128]{1,0:T(8,128)(2,1)S(1)} %get-tuple-element.12.w_ref, bf16[32,4096]{1,0:T(8,128)(2,1)S(1)} %pad_maximum_fusion.2.refs_0_, bf16[32,4096]{1,0:T(8,128)(2,1)S(1)} %collective-permute-done.25.refs_1_, bf16[32,4096]{1,0:T(8,128)(2,1)S(1)} %collective-permute-done.26.refs_2_, ...), custom_call_target="tpu_custom_call" | custom-call | flops 2013265920 | bytes 7864320 | tf_op jit(solution)/shard_map/pallas_call | solution.py:165
  97.5 6.9 %collective-permute-done.34 = bf16[976,128]{1,0:T(8,128)(2,1)S(1)} collective-permute-done((bf16[976,128]{1,0:T(8,128)(2,1)S(1)}, bf16[976,128]{1,0:T(8,128)(2,1)S(1)}, u32[]{:S(2)}, u32[]{:S(2)}) %collective-permute-start.34) | collective-permute-done | bytes 249888 | tf_op jit(solution)/shard_map/ppermute | solution.py:297
  (80 shorter events, 13.0 us)
Async XLA Ops:
  1.6 9.6 %collective-permute-start.13 = (bf16[8,4096]{1,0:T(8,128)(2,1)S(1)}, bf16[8,4096]{1,0:T(8,128)(2,1)S(1)}, u32[]{:S(2)}, u32[]{:S(2)}) collective-permute-start(bf16[8,4096]{1,0:T(8,128)(2,1)S(1)} %get-tuple-element.26), channel_id=1, source_target_pairs={{0,8},{2,10},{4,12},{6,14},{8,16},{10,18},{12,20},{14,22},{16,24},... | collective-permute-start | bytes 196616 | tf_op jit(solution)/shard_map/ppermute | solution.py:216
  4.7 9.3 %collective-permute-start.12 = (bf16[8,4096]{1,0:T(8,128)(2,1)S(1)}, bf16[8,4096]{1,0:T(8,128)(2,1)S(1)}, u32[]{:S(2)}, u32[]{:S(2)}) collective-permute-start(bf16[8,4096]{1,0:T(8,128)(2,1)S(1)} %get-tuple-element.26), channel_id=1, source_target_pairs={{0,16},{2,18},{4,20},{6,22},{8,24},{10,26},{12,28},{14,30},{16,0},... | collective-permute-start | bytes 196616 | tf_op jit(solution)/shard_map/ppermute | solution.py:216
  7.3 6.7 %collective-permute-start.11 = (bf16[8,4096]{1,0:T(8,128)(2,1)S(1)}, bf16[8,4096]{1,0:T(8,128)(2,1)S(1)}, u32[]{:S(2)}, u32[]{:S(2)}) collective-permute-start(bf16[8,4096]{1,0:T(8,128)(2,1)S(1)} %get-tuple-element.26), channel_id=1, source_target_pairs={{0,24},{2,26},{4,28},{6,30},{8,0},{10,2},{12,4},{14,6},{16,8},{18,... | collective-permute-start | bytes 196616 | tf_op jit(solution)/shard_map/ppermute | solution.py:216
  10.1 6.4 %collective-permute-start.2 = (bf16[8,4224]{1,0:T(8,128)(2,1)S(1)}, bf16[8,4224]{1,0:T(8,128)(2,1)S(1)}, u32[]{:S(2)}, u32[]{:S(2)}) collective-permute-start(bf16[8,4224]{1,0:T(8,128)(2,1)S(1)} %pad_maximum_fusion.5), channel_id=1, source_target_pairs={{0,8},{2,10},{4,12},{6,14},{8,16},{10,18},{12,20},{14,22},{16,24},... | collective-permute-start | bytes 202760 | tf_op jit(solution)/shard_map/ppermute | solution.py:216
  10.9 7.3 %collective-permute-start.1 = (bf16[8,4224]{1,0:T(8,128)(2,1)S(1)}, bf16[8,4224]{1,0:T(8,128)(2,1)S(1)}, u32[]{:S(2)}, u32[]{:S(2)}) collective-permute-start(bf16[8,4224]{1,0:T(8,128)(2,1)S(1)} %pad_maximum_fusion.5), channel_id=1, source_target_pairs={{0,16},{2,18},{4,20},{6,22},{8,24},{10,26},{12,28},{14,30},{16,0},... | collective-permute-start | bytes 202760 | tf_op jit(solution)/shard_map/ppermute | solution.py:216
  11.2 6.9 %collective-permute-start = (bf16[8,4224]{1,0:T(8,128)(2,1)S(1)}, bf16[8,4224]{1,0:T(8,128)(2,1)S(1)}, u32[]{:S(2)}, u32[]{:S(2)}) collective-permute-start(bf16[8,4224]{1,0:T(8,128)(2,1)S(1)} %pad_maximum_fusion.5), channel_id=1, source_target_pairs={{0,24},{2,26},{4,28},{6,30},{8,0},{10,2},{12,4},{14,6},{16,8},{18,... | collective-permute-start | bytes 202760 | tf_op jit(solution)/shard_map/ppermute | solution.py:216
  14.1 9.2 %collective-permute-start.14 = (bf16[32,4096]{1,0:T(8,128)(2,1)S(1)}, bf16[32,4096]{1,0:T(8,128)(2,1)S(1)}, u32[]{:S(2)}, u32[]{:S(2)}) collective-permute-start(bf16[32,4096]{1,0:T(8,128)(2,1)S(1)} %pad_maximum_fusion.1.refs_0_), channel_id=1, source_target_pairs={{0,4},{2,6},{4,0},{6,2},{8,12},{10,14},{12,8},{14,10},{16,20},{18,... | collective-permute-start | bytes 786440 | tf_op jit(solution)/shard_map/ppermute | solution.py:216
  18.2 8.4 %collective-permute-start.3 = (bf16[32,4224]{1,0:T(8,128)(2,1)S(1)}, bf16[32,4224]{1,0:T(8,128)(2,1)S(1)}, u32[]{:S(2)}, u32[]{:S(2)}) collective-permute-start(bf16[32,4224]{1,0:T(8,128)(2,1)S(1)} %pad_maximum_fusion.refs_0_), channel_id=1, source_target_pairs={{0,4},{2,6},{4,0},{6,2},{8,12},{10,14},{12,8},{14,10},{16,20},{18,... | collective-permute-start | bytes 811016 | tf_op jit(solution)/shard_map/ppermute | solution.py:216
  19.7 6.8 %collective-permute-start.4 = (bf16[32,4224]{1,0:T(8,128)(2,1)S(1)}, bf16[32,4224]{1,0:T(8,128)(2,1)S(1)}, u32[]{:S(2)}, u32[]{:S(2)}) collective-permute-start(bf16[32,4224]{1,0:T(8,128)(2,1)S(1)} %pad_maximum_fusion.refs_0_), channel_id=1, source_target_pairs={{0,2},{2,0},{4,6},{6,4},{8,10},{10,8},{12,14},{14,12},{16,18},{18,... | collective-permute-start | bytes 811016 | tf_op jit(solution)/shard_map/ppermute | solution.py:216
  19.7 6.8 %collective-permute-start.15 = (bf16[32,4096]{1,0:T(8,128)(2,1)S(1)}, bf16[32,4096]{1,0:T(8,128)(2,1)S(1)}, u32[]{:S(2)}, u32[]{:S(2)}) collective-permute-start(bf16[32,4096]{1,0:T(8,128)(2,1)S(1)} %pad_maximum_fusion.1.refs_0_), channel_id=1, source_target_pairs={{0,2},{2,0},{4,6},{6,4},{8,10},{10,8},{12,14},{14,12},{16,18},{18,... | collective-permute-start | bytes 786440 | tf_op jit(solution)/shard_map/ppermute | solution.py:216
  26.6 5.8 %collective-permute-start.5 = (bf16[32,4224]{1,0:T(8,128)(2,1)S(1)}, bf16[32,4224]{1,0:T(8,128)(2,1)S(1)}, u32[]{:S(2)}, u32[]{:S(2)}) collective-permute-start(bf16[32,4224]{1,0:T(8,128)(2,1)S(1)} %collective-permute-done.3.refs_1_), channel_id=1, source_target_pairs={{0,2},{2,0},{4,6},{6,4},{8,10},{10,8},{12,14},{14,12},{16,18},{18,... | collective-permute-start | bytes 811016 | tf_op jit(solution)/shard_map/ppermute | solution.py:216
  31.8 5.9 %collective-permute-start.17 = (bf16[64,4096]{1,0:T(8,128)(2,1)S(1)}, bf16[64,4096]{1,0:T(8,128)(2,1)S(1)}, u32[]{:S(2)}, u32[]{:S(2)}) collective-permute-start(bf16[64,4096]{1,0:T(8,128)(2,1)S(1)} %get-tuple-element.18), channel_id=1, source_target_pairs={{0,2},{2,0},{4,6},{6,4},{8,10},{10,8},{12,14},{14,12},{16,18},{18,... | collective-permute-start | bytes 1572872 | tf_op jit(solution)/shard_map/ppermute | solution.py:216
  38.1 9.2 %collective-permute-start.18 = (bf16[32,4096]{1,0:T(8,128)(2,1)S(1)}, bf16[32,4096]{1,0:T(8,128)(2,1)S(1)}, u32[]{:S(2)}, u32[]{:S(2)}) collective-permute-start(bf16[32,4096]{1,0:T(8,128)(2,1)S(1)} %fusion.15), channel_id=1, source_target_pairs={{0,4},{2,6},{4,0},{6,2},{8,12},{10,14},{12,8},{14,10},{16,20},{18,... | collective-permute-start | bytes 786440 | tf_op jit(solution)/shard_map/ppermute | solution.py:216
  40.1 12.4 %collective-permute-start.7 = (bf16[32,4096]{1,0:T(8,128)(2,1)S(1)}, bf16[32,4096]{1,0:T(8,128)(2,1)S(1)}, u32[]{:S(2)}, u32[]{:S(2)}) collective-permute-start(bf16[32,4096]{1,0:T(8,128)(2,1)S(1)} %fusion.14), channel_id=1, source_target_pairs={{0,4},{2,6},{4,0},{6,2},{8,12},{10,14},{12,8},{14,10},{16,20},{18,... | collective-permute-start | bytes 786440 | tf_op jit(solution)/shard_map/ppermute | solution.py:216
  47.6 8.0 %collective-permute-start.21 = (bf16[8,4096]{1,0:T(8,128)(2,1)S(1)}, bf16[8,4096]{1,0:T(8,128)(2,1)S(1)}, u32[]{:S(2)}, u32[]{:S(2)}) collective-permute-start(bf16[8,4096]{1,0:T(8,128)(2,1)S(1)} %get-tuple-element.29), channel_id=1, source_target_pairs={{0,24},{2,26},{4,28},{6,30},{8,0},{10,2},{12,4},{14,6},{16,8},{18,... | collective-permute-start | bytes 196616 | tf_op jit(solution)/shard_map/ppermute | solution.py:216
  50.0 7.6 %collective-permute-start.20 = (bf16[8,4096]{1,0:T(8,128)(2,1)S(1)}, bf16[8,4096]{1,0:T(8,128)(2,1)S(1)}, u32[]{:S(2)}, u32[]{:S(2)}) collective-permute-start(bf16[8,4096]{1,0:T(8,128)(2,1)S(1)} %get-tuple-element.30), channel_id=1, source_target_pairs={{0,16},{2,18},{4,20},{6,22},{8,24},{10,26},{12,28},{14,30},{16,0},... | collective-permute-start | bytes 196616 | tf_op jit(solution)/shard_map/ppermute | solution.py:216
  50.3 7.2 %collective-permute-start.19 = (bf16[8,4096]{1,0:T(8,128)(2,1)S(1)}, bf16[8,4096]{1,0:T(8,128)(2,1)S(1)}, u32[]{:S(2)}, u32[]{:S(2)}) collective-permute-start(bf16[8,4096]{1,0:T(8,128)(2,1)S(1)} %get-tuple-element.28), channel_id=1, source_target_pairs={{0,8},{2,10},{4,12},{6,14},{8,16},{10,18},{12,20},{14,22},{16,24},... | collective-permute-start | bytes 196616 | tf_op jit(solution)/shard_map/ppermute | solution.py:216
  52.8 6.9 %collective-permute-start.8 = (bf16[8,4096]{1,0:T(8,128)(2,1)S(1)}, bf16[8,4096]{1,0:T(8,128)(2,1)S(1)}, u32[]{:S(2)}, u32[]{:S(2)}) collective-permute-start(bf16[8,4096]{1,0:T(8,128)(2,1)S(1)} %get-tuple-element.33), channel_id=1, source_target_pairs={{0,8},{2,10},{4,12},{6,14},{8,16},{10,18},{12,20},{14,22},{16,24},... | collective-permute-start | bytes 196616 | tf_op jit(solution)/shard_map/ppermute | solution.py:216
  53.9 8.0 %collective-permute-start.9 = (bf16[8,4096]{1,0:T(8,128)(2,1)S(1)}, bf16[8,4096]{1,0:T(8,128)(2,1)S(1)}, u32[]{:S(2)}, u32[]{:S(2)}) collective-permute-start(bf16[8,4096]{1,0:T(8,128)(2,1)S(1)} %get-tuple-element.32), channel_id=1, source_target_pairs={{0,16},{2,18},{4,20},{6,22},{8,24},{10,26},{12,28},{14,30},{16,0},... | collective-permute-start | bytes 196616 | tf_op jit(solution)/shard_map/ppermute | solution.py:216
  55.7 6.3 %collective-permute-start.10 = (bf16[8,4096]{1,0:T(8,128)(2,1)S(1)}, bf16[8,4096]{1,0:T(8,128)(2,1)S(1)}, u32[]{:S(2)}, u32[]{:S(2)}) collective-permute-start(bf16[8,4096]{1,0:T(8,128)(2,1)S(1)} %get-tuple-element.31), channel_id=1, source_target_pairs={{0,24},{2,26},{4,28},{6,30},{8,0},{10,2},{12,4},{14,6},{16,8},{18,... | collective-permute-start | bytes 196616 | tf_op jit(solution)/shard_map/ppermute | solution.py:216
  57.6 10.5 %collective-permute-start.30 = (bf16[8,4096]{1,0:T(8,128)(2,1)S(1)}, bf16[8,4096]{1,0:T(8,128)(2,1)S(1)}, u32[]{:S(2)}, u32[]{:S(2)}) collective-permute-start(bf16[8,4096]{1,0:T(8,128)(2,1)S(1)} %get-tuple-element.22), channel_id=1, source_target_pairs={{0,8},{2,10},{4,12},{6,14},{8,16},{10,18},{12,20},{14,22},{16,24},... | collective-permute-start | bytes 196616 | tf_op jit(solution)/shard_map/ppermute | solution.py:216
  57.9 10.7 %collective-permute-start.29 = (bf16[8,4096]{1,0:T(8,128)(2,1)S(1)}, bf16[8,4096]{1,0:T(8,128)(2,1)S(1)}, u32[]{:S(2)}, u32[]{:S(2)}) collective-permute-start(bf16[8,4096]{1,0:T(8,128)(2,1)S(1)} %get-tuple-element.22), channel_id=1, source_target_pairs={{0,16},{2,18},{4,20},{6,22},{8,24},{10,26},{12,28},{14,30},{16,0},... | collective-permute-start | bytes 196616 | tf_op jit(solution)/shard_map/ppermute | solution.py:216
  59.6 9.0 %collective-permute-start.28 = (bf16[8,4096]{1,0:T(8,128)(2,1)S(1)}, bf16[8,4096]{1,0:T(8,128)(2,1)S(1)}, u32[]{:S(2)}, u32[]{:S(2)}) collective-permute-start(bf16[8,4096]{1,0:T(8,128)(2,1)S(1)} %get-tuple-element.22), channel_id=1, source_target_pairs={{0,24},{2,26},{4,28},{6,30},{8,0},{10,2},{12,4},{14,6},{16,8},{18,... | collective-permute-start | bytes 196616 | tf_op jit(solution)/shard_map/ppermute | solution.py:216
  62.1 8.4 %collective-permute-start.24 = (bf16[8,4096]{1,0:T(8,128)(2,1)S(1)}, bf16[8,4096]{1,0:T(8,128)(2,1)S(1)}, u32[]{:S(2)}, u32[]{:S(2)}) collective-permute-start(bf16[8,4096]{1,0:T(8,128)(2,1)S(1)} %get-tuple-element.24), channel_id=1, source_target_pairs={{0,8},{2,10},{4,12},{6,14},{8,16},{10,18},{12,20},{14,22},{16,24},... | collective-permute-start | bytes 196616 | tf_op jit(solution)/shard_map/ppermute | solution.py:216
  66.1 6.5 %collective-permute-start.23 = (bf16[8,4096]{1,0:T(8,128)(2,1)S(1)}, bf16[8,4096]{1,0:T(8,128)(2,1)S(1)}, u32[]{:S(2)}, u32[]{:S(2)}) collective-permute-start(bf16[8,4096]{1,0:T(8,128)(2,1)S(1)} %get-tuple-element.24), channel_id=1, source_target_pairs={{0,16},{2,18},{4,20},{6,22},{8,24},{10,26},{12,28},{14,30},{16,0},... | collective-permute-start | bytes 196616 | tf_op jit(solution)/shard_map/ppermute | solution.py:216
  68.1 5.1 %collective-permute-start.22 = (bf16[8,4096]{1,0:T(8,128)(2,1)S(1)}, bf16[8,4096]{1,0:T(8,128)(2,1)S(1)}, u32[]{:S(2)}, u32[]{:S(2)}) collective-permute-start(bf16[8,4096]{1,0:T(8,128)(2,1)S(1)} %get-tuple-element.24), channel_id=1, source_target_pairs={{0,24},{2,26},{4,28},{6,30},{8,0},{10,2},{12,4},{14,6},{16,8},{18,... | collective-permute-start | bytes 196616 | tf_op jit(solution)/shard_map/ppermute | solution.py:216
  68.6 8.6 %collective-permute-start.31 = (bf16[32,4096]{1,0:T(8,128)(2,1)S(1)}, bf16[32,4096]{1,0:T(8,128)(2,1)S(1)}, u32[]{:S(2)}, u32[]{:S(2)}) collective-permute-start(bf16[32,4096]{1,0:T(8,128)(2,1)S(1)} %pad_maximum_fusion.3.refs_0_), channel_id=1, source_target_pairs={{0,4},{2,6},{4,0},{6,2},{8,12},{10,14},{12,8},{14,10},{16,20},{18,... | collective-permute-start | bytes 786440 | tf_op jit(solution)/shard_map/ppermute | solution.py:216
  73.2 8.7 %collective-permute-start.25 = (bf16[32,4096]{1,0:T(8,128)(2,1)S(1)}, bf16[32,4096]{1,0:T(8,128)(2,1)S(1)}, u32[]{:S(2)}, u32[]{:S(2)}) collective-permute-start(bf16[32,4096]{1,0:T(8,128)(2,1)S(1)} %pad_maximum_fusion.2.refs_0_), channel_id=1, source_target_pairs={{0,4},{2,6},{4,0},{6,2},{8,12},{10,14},{12,8},{14,10},{16,20},{18,... | collective-permute-start | bytes 786440 | tf_op jit(solution)/shard_map/ppermute | solution.py:216
  74.3 7.5 %collective-permute-start.32 = (bf16[32,4096]{1,0:T(8,128)(2,1)S(1)}, bf16[32,4096]{1,0:T(8,128)(2,1)S(1)}, u32[]{:S(2)}, u32[]{:S(2)}) collective-permute-start(bf16[32,4096]{1,0:T(8,128)(2,1)S(1)} %pad_maximum_fusion.3.refs_0_), channel_id=1, source_target_pairs={{0,2},{2,0},{4,6},{6,4},{8,10},{10,8},{12,14},{14,12},{16,18},{18,... | collective-permute-start | bytes 786440 | tf_op jit(solution)/shard_map/ppermute | solution.py:216
  77.2 11.2 %collective-permute-start.26 = (bf16[32,4096]{1,0:T(8,128)(2,1)S(1)}, bf16[32,4096]{1,0:T(8,128)(2,1)S(1)}, u32[]{:S(2)}, u32[]{:S(2)}) collective-permute-start(bf16[32,4096]{1,0:T(8,128)(2,1)S(1)} %pad_maximum_fusion.2.refs_0_), channel_id=1, source_target_pairs={{0,2},{2,0},{4,6},{6,4},{8,10},{10,8},{12,14},{14,12},{16,18},{18,... | collective-permute-start | bytes 786440 | tf_op jit(solution)/shard_map/ppermute | solution.py:216
  81.9 6.6 %collective-permute-start.27 = (bf16[32,4096]{1,0:T(8,128)(2,1)S(1)}, bf16[32,4096]{1,0:T(8,128)(2,1)S(1)}, u32[]{:S(2)}, u32[]{:S(2)}) collective-permute-start(bf16[32,4096]{1,0:T(8,128)(2,1)S(1)} %collective-permute-done.25.refs_1_), channel_id=1, source_target_pairs={{0,2},{2,0},{4,6},{6,4},{8,10},{10,8},{12,14},{14,12},{16,18},{18,... | collective-permute-start | bytes 786440 | tf_op jit(solution)/shard_map/ppermute | solution.py:216
  95.9 8.5 %collective-permute-start.34 = (bf16[976,128]{1,0:T(8,128)(2,1)S(1)}, bf16[976,128]{1,0:T(8,128)(2,1)S(1)}, u32[]{:S(2)}, u32[]{:S(2)}) collective-permute-start(bf16[976,128]{1,0:T(8,128)(2,1)S(1)} %shard_map.53), channel_id=1, source_target_pairs={{0,1},{1,0},{2,3},{3,2},{4,5},{5,4},{6,7},{7,6},{8,9},{9,8},{10,11... | collective-permute-start | bytes 749576 | tf_op jit(solution)/shard_map/ppermute | solution.py:297
  (6 other events, 68.1 us)
